TPU v7x, 256 devices: a whole 4x4x8 slice. The times are simulated.
256 devices in a mesh: chan: 16 (over x_lo, y, core), pulse: 16 (over x_hi, z).
Axes of the slice: x: 4 (x_hi: 2, x_lo: 2; x = x_hi * 2 + x_lo), y: 4, z: 8, core: 2. Of those that a mesh axis runs over, the one named last changes fastest.
Arguments:
- echoes: float32 [16, 2, 4096, 4096], P('chan', None, 'pulse'), may hold values from -6 to 6
- chirp_phase: float32 [4096], replicated, may hold values from -3.140625 to 3.140625
- rcmc_kernel: float32 [32, 128, 128], P('pulse'), may hold values from -0.5 to 0.5
- rcmc_offset: int32 [32], P('pulse'), may hold values from 1 to 64, as said below
- az_phase: float32 [4096, 32], P(None, 'pulse'), may hold values from -3.140625 to 3.140625
- weight_table: float32 [2, 64], replicated, may hold values from -1.5 to 1.5
- weight_index: int32 [16, 32], P('chan'), may hold values from 0 to 63
Outputs:
- image: float32 [2, 4096, 4096], P(None, 'chan', 'pulse')
Inputs may be any that keep to these rules, and one draw needn't show every extreme that they name: `rcmc_offset`: every offset is at least 1, and in every draw some block's offset equals 64.
All inputs are finite; a program needn't handle non-finite values.
Results may differ from a plain program's by a relative error of at most 0.0001.
Values sent between devices are 32-bit elements; how exact they have to be, the bound alone decides.
No kernel may reach another device: no remote copies, remote signals or barrier semaphores. Data moves between devices by JAX's collectives and lax.ppermute only.
A program may use at most 128 MiB of HBM per device.

v0:
```python
import math

import jax
import jax.numpy as jnp
from jax import lax
from jax.sharding import PartitionSpec as P

BLOCK = 128
DBLOCK = 128
HALF = 64


def shifted(block, axis, distance):
    devices = range(lax.axis_size(axis))
    route = [(i - distance, i) for i in devices if i - distance in devices]
    return lax.ppermute(block, axis, route)


def factor_pair(length):
    return (128, length // 128)


def unit_table(count_a, count_b, modulus, sign_value):
    row_index = lax.broadcasted_iota(jnp.int32, (count_a, count_b), 0)
    col_index = lax.broadcasted_iota(jnp.int32, (count_a, count_b), 1)
    angles = (
        sign_value * 2.0 * math.pi / modulus * (row_index * col_index % modulus).astype(jnp.float32)
    )
    return (jnp.cos(angles), jnp.sin(angles))


def realify(coef_re, coef_im):
    return jnp.stack([jnp.stack([coef_re, coef_im]), jnp.stack([-coef_im, coef_re])])


def transform(stacked, sign_value, along_rows, prefactor=None):
    exact = lax.Precision.HIGHEST
    length = stacked.shape[1] if along_rows else stacked.shape[2]
    inner_len, outer_len = factor_pair(length)
    outer_re, outer_im = unit_table(outer_len, outer_len, outer_len, sign_value)
    inner_re, inner_im = unit_table(inner_len, inner_len, inner_len, sign_value)
    twist_re, twist_im = unit_table(outer_len, inner_len, length, sign_value)
    first_re = (
        outer_re[:, :, None] * twist_re[None, :, :] - outer_im[:, :, None] * twist_im[None, :, :]
    )
    first_im = (
        outer_re[:, :, None] * twist_im[None, :, :] + outer_im[:, :, None] * twist_re[None, :, :]
    )
    if prefactor is not None:
        pre_re = jnp.cos(prefactor).reshape(outer_len, inner_len)[:, None, :]
        pre_im = jnp.sin(prefactor).reshape(outer_len, inner_len)[:, None, :]
        first_re, first_im = (
            first_re * pre_re - first_im * pre_im,
            first_re * pre_im + first_im * pre_re,
        )
    first_table = realify(first_re, first_im)
    norm_scale = 1.0 / math.sqrt(length)
    second_table = realify(inner_re * norm_scale, inner_im * norm_scale)
    if along_rows:
        col_count = stacked.shape[2]
        data = stacked.reshape(2, outer_len, inner_len, col_count)
        middle = jnp.einsum("sabc,stakb->tkbc", data, first_table, precision=exact)
        result = jnp.einsum("tkbc,tubj->ujkc", middle, second_table, precision=exact)
        return result.reshape(2, length, col_count)
    row_count = stacked.shape[1]
    data = stacked.reshape(2, row_count, outer_len, inner_len)
    middle = jnp.einsum("srab,stakb->trkb", data, first_table, precision=exact)
    result = jnp.einsum("trkb,tubj->urjk", middle, second_table, precision=exact)
    return result.reshape(2, row_count, length)


def azimuth(exchanged):
    return transform(exchanged[:, :, 0, :], -1.0, True)[:, :, None, :]


def body(echoes, chirp_phase, rcmc_kernel, rcmc_offset, az_phase, weight_table, weight_index):
    own_data = echoes[0]
    pulses_dev = own_data.shape[1]
    gate_count = own_data.shape[2]
    pulse_devs = lax.axis_size("pulse")
    gates_dev = gate_count // pulse_devs
    spectrum = transform(own_data, -1.0, False)
    compressed = transform(spectrum, 1.0, False, chirp_phase)
    pieces = compressed.reshape(2, pulses_dev, pulse_devs, gates_dev)
    doppler = azimuth(lax.all_to_all(pieces, "pulse", split_axis=2, concat_axis=1, tiled=True))[
        :, :, 0, :
    ]
    beyond = shifted(doppler[:, :, :HALF], "pulse", -1)
    extended = jnp.concatenate([doppler, beyond], axis=2)
    pulses = extended.shape[1]
    rows_ext = extended.shape[2]
    blocks_dev = gates_dev // BLOCK
    row_ids = lax.broadcasted_iota(jnp.int32, (rows_ext, blocks_dev, BLOCK), 0)
    blk_ids = lax.broadcasted_iota(jnp.int32, (rows_ext, blocks_dev, BLOCK), 1)
    lane_ids = lax.broadcasted_iota(jnp.int32, (rows_ext, blocks_dev, BLOCK), 2)
    targets = blk_ids * BLOCK + rcmc_offset[None, :, None] + lane_ids
    selector = (row_ids == targets).astype(jnp.float32)
    banded = jnp.einsum("rbj,bjm->rbm", selector, rcmc_kernel, precision=lax.Precision.HIGHEST)
    banded = banded.reshape(rows_ext, gates_dev)
    migrated = jnp.einsum("cpr,rg->cpg", extended, banded, precision=lax.Precision.HIGHEST)
    table_count = weight_table.shape[1]
    entry_ids = lax.broadcasted_iota(jnp.int32, (weight_index.shape[1], table_count), 1)
    one_hot = (weight_index[0][:, None] == entry_ids).astype(jnp.float32)
    chosen = jnp.dot(one_hot, weight_table.T, precision=lax.Precision.HIGHEST)
    per_pulse = jnp.repeat(chosen, DBLOCK, axis=0)
    phase_re = jnp.cos(az_phase)
    phase_im = jnp.sin(az_phase)
    gain_re = (phase_re * per_pulse[:, 0:1] - phase_im * per_pulse[:, 1:2])[:, :, None]
    gain_im = (phase_re * per_pulse[:, 1:2] + phase_im * per_pulse[:, 0:1])[:, :, None]
    mig_re = migrated[0].reshape(pulses, blocks_dev, BLOCK)
    mig_im = migrated[1].reshape(pulses, blocks_dev, BLOCK)
    filt_re = (mig_re * gain_re - mig_im * gain_im).reshape(pulses, gates_dev)
    filt_im = (mig_re * gain_im + mig_im * gain_re).reshape(pulses, gates_dev)
    filtered = jnp.stack([filt_re, filt_im])
    focused = transform(filtered, 1.0, True)
    return lax.psum_scatter(focused, "chan", scatter_dimension=1, tiled=True)


def solution(mesh):
    return jax.shard_map(
        body,
        mesh=mesh,
        in_specs=(
            P("chan", None, "pulse", None),
            P(),
            P("pulse", None, None),
            P("pulse"),
            P(None, "pulse"),
            P(),
            P("chan", None),
        ),
        out_specs=P(None, "chan", "pulse"),
        check_vma=False,
    )
```

profile of v0, /device:TPU:4, one launch (start us, length us, event | category | flops | bytes accessed | tf_op | source)
XLA Modules:
  0.0 619.5 jit_solution(3688297036515816386)
XLA Ops:
  12.5 7.6 %copy.86 = f32[2,2,32,32,128]{2,3,0,1,4:T(8,128)} copy(f32[2,2,32,32,128]{4,3,2,1,0:T(8,128)S(1)} %pad_maximum_fusion.2) | data formatting | bytes 4194304 | tf_op jit(solution)/shard_map/stack | solution.py:33
  21.0 7.6 %copy.93 = f32[2,2,32,32,128]{2,3,0,1,4:T(8,128)} copy(f32[2,2,32,32,128]{4,3,2,1,0:T(8,128)S(1)} %pad_maximum_fusion.1) | data formatting | bytes 4194304 | tf_op jit(solution)/shard_map/stack | solution.py:33
  28.6 5.2 copy.135
  33.8 4.2 bitcast_bitcast_fusion
  38.0 11.0 %copy.108 = f32[2,256,32,128,1]{1,2,0,4,3:T(8,128)} copy(f32[2,256,32,128,1]{3,2,1,0,4:T(8,128)} %bitcast_bitcast_fusion) | data formatting | bytes 16777216 | tf_op jit(solution)/shard_map/reshape;squeeze | solution.py:66
  49.0 17.4 %convolution_bitcast_fusion = f32[2,256,32,128]{1,2,0,3:T(8,128)} fusion(f32[2,2,32,32,128]{2,3,0,1,4:T(8,128)} %copy.93, f32[2,256,32,128,1]{1,2,0,4,3:T(8,128)} %copy.108), kind=kOutput, calls=%fused_computation.31 | convolution fusion | flops 1610612736 | bytes 18874368 | tf_op jit(solution)/shard_map/srab,stakb->trkb/dot_general | solution.py:67
  66.4 10.1 %copy.84 = f32[2,256,32,128]{3,1,0,2:T(8,128)} copy(f32[2,256,32,128]{1,2,0,3:T(8,128)} %convolution_bitcast_fusion) | data formatting | bytes 16777216 | tf_op jit(solution)/shard_map/srab,stakb->trkb/transpose | solution.py:67
  76.6 10.6 %fusion.23 = f32[2,256,128,32]{1,2,3,0:T(8,128)S(1)} fusion(f32[2,256,32,128]{3,1,0,2:T(8,128)} %copy.84, f32[1,2,128,128]{2,3,0,1:T(8,128)S(1)} %get-tuple-element.21, f32[1,2,128,128]{2,3,0,1:T(8,128)S(1)} %get-tuple-element.20), kind=kOutput, calls=%fused_computation.25 | convolution fusion | flops 6442516480 | bytes 17039360 | tf_op jit(solution)/shard_map/trkb,tubj->urjk/dot_general | solution.py:68
  87.2 8.1 %copy.85 = f32[2,256,128,32]{1,3,2,0:T(8,128)} copy(f32[2,256,128,32]{1,2,3,0:T(8,128)S(1)} %fusion.23) | data formatting | bytes 16777216 | tf_op jit(solution)/shard_map/trkb,tubj->urjk/transpose | solution.py:68
  95.3 21.9 %fusion.26 = f32[2,256,32,128]{1,2,0,3:T(8,128)} fusion(f32[2,2,32,32,128]{2,3,0,1,4:T(8,128)} %copy.86, f32[2,256,32,128,1]{1,3,2,0,4:T(8,128)} %bitcast.143), kind=kOutput, calls=%fused_computation.26 | convolution fusion | flops 1610612736 | bytes 18874368 | tf_op jit(solution)/shard_map/srab,stakb->trkb/dot_general | solution.py:67
  117.2 10.1 %copy.89 = f32[2,256,32,128]{3,1,0,2:T(8,128)} copy(f32[2,256,32,128]{1,2,0,3:T(8,128)} %fusion.26) | data formatting | bytes 16777216 | tf_op jit(solution)/shard_map/srab,stakb->trkb/transpose | solution.py:67
  127.3 10.5 %fusion.29 = f32[2,256,128,32]{1,2,3,0:T(8,128)S(1)} fusion(f32[2,256,32,128]{3,1,0,2:T(8,128)} %copy.89, f32[1,2,128,128]{2,3,1,0:T(8,128)S(1)} %get-tuple-element.19, f32[1,2,128,128]{2,3,1,0:T(8,128)S(1)} %get-tuple-element.18), kind=kOutput, calls=%fused_computation.27 | convolution fusion | flops 6442516480 | bytes 17039360 | tf_op jit(solution)/shard_map/trkb,tubj->urjk/dot_general | solution.py:68
  137.8 4.9 copy.90
  146.5 11.6 %all-to-all-start = ((f32[2,256,16,256]{1,3,0,2:T(8,128)}), f32[2,256,16,256]{1,3,0,2:T(8,128)}, u32[]{:S(2)}, u32[]{:S(2)}) async-start(f32[2,256,16,256]{1,3,0,2:T(8,128)} %copy.91), calls=%async_computation | async-start | bytes 16777216 | tf_op jit(solution)/shard_map/all_to_all | solution.py:85
  158.5 185.2 %all-to-all-done = f32[2,256,16,256]{1,3,0,2:T(8,128)} async-done(((f32[2,256,16,256]{1,3,0,2:T(8,128)}), f32[2,256,16,256]{1,3,0,2:T(8,128)}, u32[]{:S(2)}, u32[]{:S(2)}) %all-to-all-start) | async-done | bytes 8388640 | tf_op jit(solution)/shard_map/all_to_all | solution.py:85
  343.7 8.8 %copy.92 = f32[2,256,16,256]{3,1,2,0:T(8,128)} copy(f32[2,256,16,256]{1,3,0,2:T(8,128)} %all-to-all-done) | data formatting | bytes 16777216 | tf_op jit(solution)/shard_map/all_to_all | solution.py:85
  352.5 21.7 %fusion.32 = f32[2,32,128,256]{3,1,0,2:T(8,128)} fusion(f32[2,2,32,32,128]{2,3,0,1,4:T(8,128)} %copy.93, f32[2,32,128,256,1]{3,2,1,0,4:T(8,128)} %bitcast.144), kind=kOutput, calls=%fused_computation.28 | convolution fusion | flops 1610612736 | bytes 18874368 | tf_op jit(solution)/shard_map/sabc,stakb->tkbc/dot_general | solution.py:62
  374.3 15.0 %fusion.35 = f32[2,128,32,256]{3,1,2,0:T(8,128)S(1)} fusion(f32[2,32,128,256]{3,1,0,2:T(8,128)} %fusion.32, f32[1,2,128,128]{2,3,0,1:T(8,128)S(1)} %get-tuple-element.21, f32[1,2,128,128]{2,3,0,1:T(8,128)S(1)} %get-tuple-element.20), kind=kOutput, calls=%fused_computation.29 | convolution fusion | flops 6442516480 | bytes 17039360 | tf_op jit(solution)/shard_map/tkbc,tubj->ujkc/dot_general | solution.py:63
  389.3 8.1 %copy.96 = f32[2,128,32,256]{3,2,1,0:T(8,128)} copy(f32[2,128,32,256]{3,1,2,0:T(8,128)S(1)} %fusion.35) | data formatting | bytes 16777216 | tf_op jit(solution)/shard_map/tkbc,tubj->ujkc/dot_general | solution.py:63
  397.4 8.9 %copy.98 = f32[2,4096,256]{1,2,0:T(8,128)} copy(f32[2,4096,256]{2,1,0:T(8,128)} %bitcast.147) | data formatting | bytes 16777216 | tf_op jit(solution)/shard_map/squeeze;broadcast_in_dim;reshape | solution.py:85
  409.4 4.5 collective-permute-start
  418.1 10.6 %mul.887 = f32[4096,2,128]{2,1,0:T(2,128)} broadcast(f32[4096,2]{1,0:T(8,128)S(1)} %copy.100), dimensions={0,1} | broadcast | bytes 4227072 | tf_op jit(solution)/shard_map/mul | solution.py:112
  428.6 6.4 %mul.888 = f32[1,4096,256]{2,1,0:T(8,128)} reshape(f32[4096,2,128]{2,1,0:T(2,128)} %mul.887) | data formatting | bytes 8388608 | tf_op jit(solution)/shard_map/mul | solution.py:112
  436.4 10.2 %mul.892 = f32[4096,2,128]{2,1,0:T(2,128)} broadcast(f32[4096,2]{1,0:T(8,128)S(1)} %copy.101), dimensions={0,1} | broadcast | bytes 4227072 | tf_op jit(solution)/shard_map/mul | solution.py:112
  446.6 6.5 %mul.893 = f32[1,4096,256]{2,1,0:T(8,128)} reshape(f32[4096,2,128]{2,1,0:T(2,128)} %mul.892) | data formatting | bytes 8388608 | tf_op jit(solution)/shard_map/mul | solution.py:112
  454.6 7.6 %copy.119 = f32[2,2,32,32,128]{2,3,0,1,4:T(8,128)} copy(f32[2,2,32,32,128]{4,3,2,1,0:T(8,128)S(1)} %pad_maximum_fusion) | data formatting | bytes 4194304 | tf_op jit(solution)/shard_map/stack | solution.py:33
  462.2 23.3 %fusion = f32[2,4096,256]{2,1,0:T(8,128)S(1)} fusion(f32[320,256,1]{1,0,2:T(8,128)} %reshape.278, f32[2,4096,64]{1,2,0:T(8,128)} %collective-permute-done, f32[2,4096,256]{1,2,0:T(8,128)} %copy.98), kind=kOutput, calls=%fused_computation | convolution fusion | flops 8055685120 | bytes 19202048 | tf_op jit(solution)/shard_map/cpr,rg->cpg/dot_general | solution.py:100
  489.3 4.4 copy.103
  493.7 16.5 %fusion.20 = f32[2,32,128,256]{3,1,0,2:T(8,128)} fusion(f32[2,2,32,32,128]{2,3,0,1,4:T(8,128)} %copy.119, f32[1,32,128,256]{3,1,2,0:T(8,128)} %copy.103, f32[1,32,128,256]{3,1,2,0:T(8,128)S(1)} %copy.102), kind=kOutput, calls=%fused_computation.24 | convolution fusion | flops 1612709888 | bytes 18874368 | tf_op jit(solution)/shard_map/sabc,stakb->tkbc/dot_general | solution.py:62
  510.2 15.0 %fusion.38 = f32[2,128,32,256]{3,1,2,0:T(8,128)S(1)} fusion(f32[2,32,128,256]{3,1,0,2:T(8,128)} %fusion.20, f32[1,2,128,128]{2,3,1,0:T(8,128)S(1)} %get-tuple-element.19, f32[1,2,128,128]{2,3,1,0:T(8,128)S(1)} %get-tuple-element.18), kind=kOutput, calls=%fused_computation.30 | convolution fusion | flops 6442516480 | bytes 17039360 | tf_op jit(solution)/shard_map/tkbc,tubj->ujkc/dot_general | solution.py:63
  525.3 8.1 %copy.107 = f32[2,128,32,256]{3,2,1,0:T(8,128)} copy(f32[2,128,32,256]{3,1,2,0:T(8,128)S(1)} %fusion.38) | data formatting | bytes 16777216 | tf_op jit(solution)/shard_map/tkbc,tubj->ujkc/dot_general | solution.py:63
  533.4 79.0 %reduce-scatter.2.cloned.1.call-done = f32[2,256,256]{2,1,0:T(8,128)} async-done(((f32[2,4096,256]{2,1,0:T(8,128)}), f32[2,256,256]{2,1,0:T(8,128)}) %reduce-scatter.2.cloned.1.call-update) | async-done | bytes 524304 | tf_op jit(solution)/shard_map/reduce_scatter | solution.py:116
  (59 shorter events, 24.8 us)
Async XLA Ops:
  6.5 407.4 %copy-start = (f32[2,128,128]{2,1,0:T(8,128)S(1)}, f32[2,128,128]{2,1,0:T(8,128)}, u32[]{:S(2)}) copy-start(f32[2,128,128]{2,1,0:T(8,128)} %param.9) | copy-start | bytes 393220
  117.2 10.1 %copy-start.3 = (f32[1,128,128]{1,2,0:T(8,128)S(1)}, f32[1,128,128]{1,2,0:T(8,128)}, u32[]{:S(2)}) copy-start(f32[1,128,128]{1,2,0:T(8,128)} %get-tuple-element.42) | copy-start | bytes 196612
  117.2 10.1 %copy-start.4 = (f32[1,128,128]{1,2,0:T(8,128)S(1)}, f32[1,128,128]{1,2,0:T(8,128)}, u32[]{:S(2)}) copy-start(f32[1,128,128]{1,2,0:T(8,128)} %get-tuple-element.43) | copy-start | bytes 196612
  117.2 10.1 %copy-start.5 = (f32[1,128,128]{1,2,0:T(8,128)S(1)}, f32[1,128,128]{1,2,0:T(8,128)}, u32[]{:S(2)}) copy-start(f32[1,128,128]{1,2,0:T(8,128)} %fusion.51) | copy-start | bytes 196612
  146.5 11.6 %copy-start.7 = (f32[2,64]{1,0:T(2,128)S(1)}, f32[2,64]{1,0:T(2,128)}, u32[]{:S(2)}) copy-start(f32[2,64]{1,0:T(2,128)} %param.12) | copy-start | bytes 1540
  146.5 11.6 %copy-start.8 = (s32[1,32]{1,0:T(1,128)S(1)}, s32[1,32]{1,0:T(1,128)}, u32[]{:S(2)}) copy-start(s32[1,32]{1,0:T(1,128)} %param.13) | copy-start | bytes 388
  146.5 12.0 %copy-start.9 = (s32[2]{0:T(128)S(1)}, s32[2]{0:T(128)}, u32[]{:S(2)}) copy-start(s32[2]{0:T(128)} %param.10) | copy-start | bytes 28
  146.5 197.2 %all-to-all-start = ((f32[2,256,16,256]{1,3,0,2:T(8,128)}), f32[2,256,16,256]{1,3,0,2:T(8,128)}, u32[]{:S(2)}, u32[]{:S(2)}) async-start(f32[2,256,16,256]{1,3,0,2:T(8,128)} %copy.91), calls=%async_computation | async-start | bytes 16777216 | tf_op jit(solution)/shard_map/all_to_all | solution.py:85
  158.0 454.4 %reduce-scatter.2.cloned.1.call-start = ((), (), s32[]{:S(2)}) async-start(), calls=%async_computation.2 | async-start | bytes 8912896 | tf_op jit(solution)/shard_map/reduce_scatter | solution.py:116
  397.4 18.2 %copy-start.6 = (f32[4096,2]{0,1:T(2,128)S(1)}, f32[4096,2]{0,1:T(2,128)}, u32[]{:S(2)}) copy-start(f32[4096,2]{0,1:T(2,128)} %param.11) | copy-start | bytes 98308
  409.4 52.8 %collective-permute-start = (f32[2,4096,64]{1,2,0:T(8,128)}, f32[2,4096,64]{1,2,0:T(8,128)}, u32[]{:S(2)}, u32[]{:S(2)}) collective-permute-start(f32[2,4096,64]{1,2,0:T(8,128)} %slice.22), channel_id=1, source_target_pairs={{1,0},{2,1},{3,2},{4,3},{5,4},{6,5},{7,6},{8,7},{9,8},{10,9},{11,1... | collective-permute-start | bytes 6291464 | tf_op jit(solution)/shard_map/ppermute | solution.py:16
  462.2 23.3 %copy-start.1 = (f32[1,4096,256]{2,1,0:T(8,128)S(1)}, f32[1,4096,256]{2,1,0:T(8,128)}, u32[]{:S(2)}) copy-start(f32[1,4096,256]{2,1,0:T(8,128)} %mul.888) | copy-start | bytes 12582916
  462.2 23.3 %copy-start.2 = (f32[1,4096,256]{2,1,0:T(8,128)S(1)}, f32[1,4096,256]{2,1,0:T(8,128)}, u32[]{:S(2)}) copy-start(f32[1,4096,256]{2,1,0:T(8,128)} %mul.893) | copy-start | bytes 12582916
Sparse Core Ops, SparseCore 0:
  533.5 78.8 reduce-scatter.1
where the time goes:
time: 628 us; the launch traced here: 619 us
  waiting for transfers between devices  264 us (42%)
  local copies, waits for them, and re-layouts  163 us (26%)
  matrix products  153 us (24%)
  starting transfers between devices  16.1 us (3%)
  between operations  13.9 us (2%)
  other arithmetic  9.43 us (2%)
    all_to_all x1, waiting for transfers between devices, body(): lax.all_to_all(pieces, 'pulse', split_axis=2, concat_axis=1, tiled=True)  185 us
    reduce_scatter x1, waiting for transfers between devices, body(): return lax.psum_scatter(focused, 'chan', scatter_dimension=1, tiled=True)  79 us
    dot_general x2, matrix products, transform(): middle = jnp.einsum('srab,stakb->trkb', data, first_table, precision=exact)  39.3 us
    dot_general x2, matrix products, transform(): middle = jnp.einsum('sabc,stakb->tkbc', data, first_table, precision=exact)  38.3 us
    mul x4, local copies, waits for them, and re-layouts, body(): filt_re = (mig_re * gain_re - mig_im * gain_im).reshape(pulses, gates_dev)  33.7 us
    dot_general x2, matrix products, transform(): jnp.einsum('tkbc,tubj->ujkc', middle, second_table, precision=exact)  30.1 us
    dot_general x1, matrix products, body(): jnp.einsum('cpr,rg->cpg', extended, banded, precision=lax.Precision.HIGHEST)  23.3 us
    another operation x3, local copies, waits for them, and re-layouts, realify(): jnp.stack([jnp.stack([coef_re, coef_im]), jnp.stack([-coef_im, coef_re])])  22.9 us
  transfers between devices with their start and end apart: 3, of which 2 were waited for; matrix products, arithmetic and copies ran while one was open for 8% of the time, Pallas kernels for 0%

commit v1 on v0

v1 whole, which is shorter than its diff:
```python
import functools
import math

import jax
import jax.numpy as jnp
import numpy as np
from jax import lax
from jax.experimental import pallas as pl
from jax.experimental.pallas import tpu as pltpu
from jax.sharding import PartitionSpec as P

BLOCK = 128
DBLOCK = 128
SLABS = 32
INNER = 128
ROWS = 32


def split(values):
    high = values.astype(jnp.bfloat16)
    low = (values - high.astype(jnp.float32)).astype(jnp.bfloat16)
    return high, low


def dot(left, right):
    return jnp.dot(left, right, preferred_element_type=jnp.float32)


def dot3(left, right):
    return dot(left[0], right[0]) + dot(left[0], right[1]) + dot(left[1], right[0])


def inner_tables():
    index = np.arange(INNER)
    angles = 2.0 * math.pi / INNER * (index[:, None] * index[None, :] % INNER)
    table = np.block([[np.cos(angles), -np.sin(angles)], [np.sin(angles), np.cos(angles)]])
    bf16 = jnp.bfloat16.dtype
    high = table.astype(np.float32).astype(bf16)
    low = (table - high.astype(np.float64)).astype(np.float32).astype(bf16)
    return np.stack([high, low]), np.stack([high.T, low.T])


def twiddles():
    length = SLABS * INNER
    angles = 2.0 * math.pi / length * (np.arange(SLABS)[:, None] * np.arange(INNER)[None, :])
    return np.stack([np.cos(angles), -np.sin(angles)]).astype(np.float32)


def rotate(value, turn, length, sign):
    re, im = value
    if turn == 0:
        return value
    if 4 * turn == length:
        return (-im, re) if sign > 0 else (im, -re)
    half = math.sqrt(0.5)
    if 8 * turn == length:
        return ((re - im) * half, (re + im) * half) if sign > 0 else ((re + im) * half, (im - re) * half)
    if 8 * turn == 3 * length:
        return ((-re - im) * half, (re - im) * half) if sign > 0 else ((im - re) * half, (-re - im) * half)
    cosine = math.cos(2.0 * math.pi * turn / length)
    sine = sign * math.sin(2.0 * math.pi * turn / length)
    return re * cosine - im * sine, re * sine + im * cosine


def butterflies(values, sign):
    length = len(values)
    if length == 1:
        return values
    even = butterflies(values[0::2], sign)
    odd = butterflies(values[1::2], sign)
    lower, upper = [], []
    for turn in range(length // 2):
        er, ei = even[turn]
        tr, ti = rotate(odd[turn], turn, length, sign)
        lower.append((er + tr, ei + ti))
        upper.append((er - tr, ei - ti))
    return lower + upper


def times(re, im, cr, ci):
    return re * cr - im * ci, re * ci + im * cr


def range_kernel(offset_ref, x_ref, fwd_ref, inv_ref, tw_ref, chirp_ref, *refs):
    z0_ref, z1_ref, mid_ref, y_ref = refs[-4:]

    def first(tile, carry):
        rows = pl.ds(pl.multiple_of(tile * 8, 8), 8)
        values = [
            (x_ref[0, 0, rows, a * INNER : (a + 1) * INNER], x_ref[0, 1, rows, a * INNER : (a + 1) * INNER])
            for a in range(SLABS)
        ]
        for k, (re, im) in enumerate(butterflies(values, -1)):
            re, im = times(re, im, tw_ref[0, k : k + 1, :], tw_ref[1, k : k + 1, :])
            mid_ref[k, rows, :INNER] = re
            mid_ref[k, rows, INNER:] = im
        return carry

    lax.fori_loop(0, ROWS // 8, first, 0)

    group = 256 // ROWS
    chains = 2

    def middle(step, carry):
        spans = [pl.ds(pl.multiple_of((step * chains + c) * group, group), group) for c in range(chains)]
        spectra = [dot3(split(mid_ref[ks].reshape(256, 2 * INNER)), (fwd_ref[0], fwd_ref[1])) for ks in spans]
        for ks, spec in zip(spans, spectra):
            spec = spec.reshape(group, ROWS, 2 * INNER)
            cr = chirp_ref[0, ks, :].reshape(group, 1, INNER)
            ci = chirp_ref[1, ks, :].reshape(group, 1, INNER)
            re, im = times(spec[:, :, :INNER], spec[:, :, INNER:], cr, ci)
            filtered = jnp.concatenate([re, im], axis=2).reshape(256, 2 * INNER)
            back = dot3(split(filtered), (inv_ref[0], inv_ref[1])).reshape(group, ROWS, 2 * INNER)
            tr = tw_ref[0, ks, :].reshape(group, 1, INNER)
            ti = tw_ref[1, ks, :].reshape(group, 1, INNER)
            re, im = times(back[:, :, :INNER], back[:, :, INNER:], tr, -ti)
            mid_ref[ks, :, :INNER] = re
            mid_ref[ks, :, INNER:] = im
        return carry

    lax.fori_loop(0, SLABS // (group * chains), middle, 0)

    def last(tile, carry):
        rows = pl.ds(pl.multiple_of(tile * 8, 8), 8)
        lower = pl.ds(pl.multiple_of(ROWS + tile * 8, 8), 8)
        values = [(mid_ref[k, rows, :INNER], mid_ref[k, rows, INNER:]) for k in range(SLABS)]
        for a, (re, im) in enumerate(butterflies(values, 1)):
            y_ref[a, rows, :] = re
            y_ref[a, lower, :] = im
        return carry

    lax.fori_loop(0, ROWS // 8, last, 0)
    y_ref[SLABS] = jnp.zeros((2 * ROWS, INNER), jnp.float32)
    lanes = lax.broadcasted_iota(jnp.int32, (2 * ROWS, INNER), 1)

    def window(step, carry):
        for part in range(4):
            dest = step * 4 + part
            for block, z_ref in ((0, z0_ref), (1, z1_ref)):
                slab = 2 * dest + block
                back = INNER - offset_ref[slab]
                here = pltpu.roll(y_ref[slab], back, 1)
                after = pltpu.roll(y_ref[slab + 1], back, 1)
                shifted = jnp.where(lanes < back, here, after).reshape(2, ROWS, INNER)
                if block:
                    z_ref[dest, 0] = shifted
                else:
                    z_ref[dest] = shifted
        return carry

    lax.fori_loop(0, SLABS // 8, window, 0)


def range_compress(half, offsets, echoes, fwd, inv, chirp, other=None):
    pulses, gates = echoes.shape[2] // 2, echoes.shape[3]
    dests = gates // (2 * BLOCK)
    steps = pulses // ROWS
    outs = [
        jax.ShapeDtypeStruct((dests, 2, pulses, BLOCK), jnp.float32),
        jax.ShapeDtypeStruct((dests, 2, 2, pulses, BLOCK), jnp.float32),
    ]
    whole3 = pl.BlockSpec((2, 2 * INNER, 2 * INNER), lambda i, *_: (0, 0, 0))
    table = pl.BlockSpec((2, SLABS, INNER), lambda i, *_: (0, 0, 0))
    in_specs = [pl.BlockSpec((1, 2, ROWS, gates), lambda i, *_: (0, 0, half * steps + i, 0)), whole3, whole3, table, table]
    args = [offsets, echoes, fwd, inv, jnp.asarray(twiddles()), chirp]
    aliases = {}
    if other is not None:
        in_specs.append(pl.BlockSpec(memory_space=pl.ANY))
        aliases = {len(args): 1}
        args.append(other)
    return pl.pallas_call(
        range_kernel,
        grid_spec=pltpu.PrefetchScalarGridSpec(
            num_scalar_prefetch=1,
            grid=(steps,),
            in_specs=in_specs,
            out_specs=[
                pl.BlockSpec((dests, 2, ROWS, BLOCK), lambda i, *_: (0, 0, i, 0)),
                pl.BlockSpec((dests, 1, 2, ROWS, BLOCK), lambda i, *_: (0, half, 0, i, 0)),
            ],
            scratch_shapes=[
                pltpu.VMEM((SLABS, ROWS, 2 * INNER), jnp.float32),
                pltpu.VMEM((SLABS + 1, 2 * ROWS, INNER), jnp.float32),
            ],
        ),
        out_shape=outs,
        input_output_aliases=aliases,
        name="range_compress",
    )(*args)


def azimuth_kernel(count, *refs):
    x_refs = refs[:count]
    fwd_ref, inv_ref, tw_ref, gain_ref, o_ref, mid_ref, wide_ref = refs[count:]

    def slab(a, part, rows):
        if count == 2:
            return x_refs[a % 2][a // 2, part, rows, :]
        return x_refs[0][a // 2, a % 2, part, rows, :]

    def first(tile, carry):
        start = pl.multiple_of(tile * 8, 8)
        rows = pl.ds(start, 8)
        lower = pl.ds(pl.multiple_of(INNER + tile * 8, 8), 8)
        values = [(slab(a, 0, rows), slab(a, 1, rows)) for a in range(SLABS)]
        tr, ti = tw_ref[0, rows, :], tw_ref[1, rows, :]
        gr, gi = gain_ref[0, rows, :], gain_ref[1, rows, :]
        for k, (re, im) in enumerate(butterflies(values, -1)):
            re, im = times(re, im, tr[:, k : k + 1], ti[:, k : k + 1])
            lane = slice((k % 2) * INNER, (k % 2 + 1) * INNER)
            mid_ref[k // 2, rows, lane] = re
            mid_ref[k // 2, lower, lane] = im
            wide_ref[k // 2, rows, lane] = jnp.broadcast_to(gr[:, k : k + 1], (8, INNER))
            wide_ref[k // 2, lower, lane] = jnp.broadcast_to(gi[:, k : k + 1], (8, INNER))
        return carry

    lax.fori_loop(0, INNER // 8, first, 0)

    def middle(step, carry):
        pairs = [2 * step, 2 * step + 1]
        spectra = [dot3((inv_ref[0], inv_ref[1]), split(mid_ref[pair])) for pair in pairs]
        for pair, spec in zip(pairs, spectra):
            re, im = times(spec[:INNER], spec[INNER:], wide_ref[pair, :INNER, :], wide_ref[pair, INNER:, :])
            mid_ref[pair] = dot3((fwd_ref[0], fwd_ref[1]), split(jnp.concatenate([re, im], axis=0)))
        return carry

    lax.fori_loop(0, SLABS // 4, middle, 0)

    def last(tile, carry):
        rows = pl.ds(pl.multiple_of(tile * 8, 8), 8)
        lower = pl.ds(pl.multiple_of(INNER + tile * 8, 8), 8)
        halves = (rows, lower)
        tr, ti = tw_ref[0, rows, :], tw_ref[1, rows, :]
        values = []
        for k in range(SLABS):
            lane = slice((k % 2) * INNER, (k % 2 + 1) * INNER)
            re, im = mid_ref[k // 2, rows, lane], mid_ref[k // 2, lower, lane]
            values.append(times(re, im, tr[:, k : k + 1], -ti[:, k : k + 1]))
        for a, (re, im) in enumerate(butterflies(values, 1)):
            o_ref[a // 2, 0, halves[a % 2], :] = re
            o_ref[a // 2, 1, halves[a % 2], :] = im
        return carry

    lax.fori_loop(0, INNER // 8, last, 0)


def azimuth_filter(received, fwd, inv, gain):
    vmem = pl.BlockSpec(memory_space=pltpu.VMEM)
    count = len(received)
    devices = received[0].shape[0]
    return pl.pallas_call(
        functools.partial(azimuth_kernel, count),
        in_specs=[vmem] * (count + 4),
        out_specs=vmem,
        out_shape=jax.ShapeDtypeStruct((devices, 2, 2 * INNER, BLOCK), jnp.float32),
        scratch_shapes=[
            pltpu.VMEM((SLABS // 2, 2 * INNER, 2 * INNER), jnp.float32),
            pltpu.VMEM((SLABS // 2, 2 * INNER, 2 * INNER), jnp.float32),
        ],
        name="azimuth_filter",
    )(*received, fwd, inv, jnp.asarray(twiddles().transpose(0, 2, 1)), gain)


def migrate_kernel(s_ref, kernel_ref, *refs):
    rows = jnp.sum(s_ref[...], axis=0).reshape(-1, BLOCK)
    moved = jnp.dot(rows, kernel_ref[0], precision=lax.Precision.HIGHEST, preferred_element_type=jnp.float32)
    refs[-1][...] = moved.reshape(2, -1, BLOCK)


def migrate(block, parts, kernel, other=None):
    devices, _, pulses, _ = parts.shape
    args = [parts, kernel]
    in_specs = [
        pl.BlockSpec((devices, 2, pulses, BLOCK), lambda i: (0, 0, 0, 0)),
        pl.BlockSpec((1, BLOCK, BLOCK), lambda i: (block, 0, 0)),
    ]
    aliases = {}
    if other is not None:
        in_specs.append(pl.BlockSpec(memory_space=pl.ANY))
        aliases = {2: 0}
        args.append(other)
    return pl.pallas_call(
        migrate_kernel,
        grid=(1,),
        in_specs=in_specs,
        out_specs=pl.BlockSpec((2, pulses, BLOCK), lambda i: (0, 0, block)),
        out_shape=jax.ShapeDtypeStruct((2, pulses, 2 * BLOCK), jnp.float32),
        input_output_aliases=aliases,
        name="migrate",
    )(*args)


def turn(blocks, axis):
    return lax.all_to_all(blocks, axis, split_axis=0, concat_axis=0, tiled=True)


def body(echoes, chirp_phase, rcmc_kernel, rcmc_offset, az_phase, weight_table, weight_index):
    exact = lax.Precision.HIGHEST
    gates = echoes.shape[3]
    pulses = az_phase.shape[0]
    fwd_np, inv_np = inner_tables()
    fwd, inv = jnp.asarray(fwd_np), jnp.asarray(inv_np)
    devices = lax.axis_size("pulse")
    offsets = turn(jnp.broadcast_to(rcmc_offset, (devices, rcmc_offset.shape[0])), "pulse").reshape(-1)
    by_slab = chirp_phase.reshape(INNER, SLABS).T
    chirp = jnp.stack([jnp.cos(by_slab), jnp.sin(by_slab)]) * (1.0 / gates)
    early, partial = range_compress(0, offsets, echoes, fwd, inv, chirp)
    late, full = range_compress(1, offsets, echoes, fwd, inv, chirp, partial)

    table_count = weight_table.shape[1]
    entry_ids = lax.broadcasted_iota(jnp.int32, (weight_index.shape[1], table_count), 1)
    one_hot = (weight_index[0][:, None] == entry_ids).astype(jnp.float32)
    chosen = jnp.dot(weight_table, one_hot.T, precision=exact) * (1.0 / pulses)
    weights = jnp.repeat(chosen, DBLOCK, axis=1)
    phases = az_phase.T
    gain = jnp.stack(times(jnp.cos(phases), jnp.sin(phases), weights[0:1], weights[1:2]))
    gain = gain.reshape(2, 2, INNER, SLABS)

    early = turn(early, "pulse")
    late = turn(late, "pulse")
    full = turn(full, "pulse")
    first = azimuth_filter([early, late], fwd, inv, gain[:, 0])
    first = lax.psum_scatter(first, "chan", scatter_dimension=0, tiled=True)
    image = migrate(0, first, rcmc_kernel)
    second = azimuth_filter([full], fwd, inv, gain[:, 1])
    second = turn(second, "chan")
    return migrate(1, second, rcmc_kernel, image)


def solution(mesh):
    return jax.shard_map(
        body,
        mesh=mesh,
        in_specs=(
            P("chan", None, "pulse", None),
            P(),
            P("pulse", None, None),
            P("pulse"),
            P(None, "pulse"),
            P(),
            P("chan", None),
        ),
        out_specs=P(None, "chan", "pulse"),
        check_vma=False,
    )
```

time: 628 us -> 351 us (0.56)
  the two profiles are of different devices: /device:TPU:4 before, /device:TPU:27 now
where the time goes in v1:
time: 351 us; the launch traced here: 350 us
  waiting for transfers between devices  176 us (50%)
  Pallas kernels  73.5 us (21%)
  blocking collectives  54.2 us (15%)
  starting transfers between devices  26.5 us (8%)
  between operations  13.5 us (4%)
  local copies, waits for them, and re-layouts  4.28 us (1%)
    all_to_all x4, waiting for transfers between devices, turn(): return lax.all_to_all(blocks, axis, split_axis=0, concat_axis=0, tiled=True)  176 us
    all_to_all x1, blocking collectives, turn(): return lax.all_to_all(blocks, axis, split_axis=0, concat_axis=0, tiled=True)  54.2 us
    pallas_call x2, Pallas kernels, azimuth_filter(): pl.pallas_call(functools.partial(azimuth_kernel, count), in_specs=[vmem]...  37.8 us
    pallas_call x2, Pallas kernels, range_compress(): pl.pallas_call(range_kernel, grid_spec=pltpu.PrefetchScalarGridSpec(num_s...  30.3 us
    all_to_all x4, starting transfers between devices, turn(): return lax.all_to_all(blocks, axis, split_axis=0, concat_axis=0, tiled=True)  26.4 us
  transfers between devices with their start and end apart: 5, of which 4 were waited for; matrix products, arithmetic and copies ran while one was open for 1% of the time, Pallas kernels for 16%

profile of v1, /device:TPU:27, one launch (start us, length us, event | category | flops | bytes accessed | tf_op | source)
XLA Modules:
  0.0 350.4 jit_solution(4388524811885248780)
XLA Ops:
  6.5 1.3 broadcast_in_dim.12
  7.8 9.9 %all-to-all-start = ((s32[16,1,2]{2,1,0:T(1,128)}), s32[16,1,2]{2,1,0:T(1,128)S(1)}, u32[]{:S(2)}, u32[]{:S(2)}) async-start(s32[16,1,2]{2,1,0:T(1,128)} %broadcast_in_dim.12), calls=%async_computation | async-start | bytes 16384 | tf_op jit(solution)/shard_map/all_to_all | solution.py:294
  17.7 0.8 fusion.6
  18.5 0.1 sin.14
  18.5 0.1 copy.27
  18.6 0.1 cos.14
  18.7 0.1 copy.26
  18.8 0.6 maximum_multiply_fusion.chirp_ref
  19.4 6.9 %all-to-all-done = s32[16,1,2]{2,1,0:T(1,128)S(1)} async-done(((s32[16,1,2]{2,1,0:T(1,128)}), s32[16,1,2]{2,1,0:T(1,128)S(1)}, u32[]{:S(2)}, u32[]{:S(2)}) %all-to-all-start) | async-done | bytes 160 | tf_op jit(solution)/shard_map/all_to_all | solution.py:294
  26.4 0.5 broadcast.18
  26.8 0.6 reduce.3
  27.4 0.6 reshape.26.offset_ref
  28.0 15.2 %range_compress.2 = (f32[16,2,128,128]{3,2,1,0:T(8,128)}, f32[16,2,2,128,128]{4,3,2,1,0:T(8,128)}) custom-call(s32[32]{0:T(128)} %reshape.26.offset_ref, f32[1,2,256,4096]{3,2,1,0:T(8,128)} %x_ref.3, bf16[2,256,256]{2,1,0:T(8,128)(2,1)} %constant.4.clone.fwd_ref.refs_1_.refs_2_, bf16[2,256,256]{2,1,0:T(8,128)(2,1)} %constant.12.clone.inv_ref.refs_2_.refs_3_, ...), custom_call_target="tpu_custom_call" | custom-call | tf_op jit(solution)/shard_map/range_compress/pallas_call | solution.py:171
  43.2 3.7 %all-to-all-start.3 = ((f32[16,2,128,128]{3,2,1,0:T(8,128)}), f32[16,2,128,128]{3,2,1,0:T(8,128)S(1)}, u32[]{:S(2)}, u32[]{:S(2)}) async-start(f32[16,2,128,128]{3,2,1,0:T(8,128)} %get-tuple-element.11), calls=%async_computation.3 | async-start | bytes 4194304 | tf_op jit(solution)/shard_map/all_to_all | solution.py:294
  47.0 15.2 %range_compress.3 = (f32[16,2,128,128]{3,2,1,0:T(8,128)}, f32[16,2,2,128,128]{4,3,2,1,0:T(8,128)}) custom-call(s32[32]{0:T(128)} %reshape.26.offset_ref, f32[1,2,256,4096]{3,2,1,0:T(8,128)} %x_ref.3, bf16[2,256,256]{2,1,0:T(8,128)(2,1)} %constant.4.clone.fwd_ref.refs_1_.refs_2_, ...), custom_call_target="tpu_custom_call", output_to_operand_aliasing={{1}: (6, {})} | custom-call | tf_op jit(solution)/shard_map/range_compress/pallas_call | solution.py:171
  62.1 33.6 %all-to-all-done.3.refs_0_ = f32[16,2,128,128]{3,2,1,0:T(8,128)S(1)} async-done(((f32[16,2,128,128]{3,2,1,0:T(8,128)}), f32[16,2,128,128]{3,2,1,0:T(8,128)S(1)}, u32[]{:S(2)}, u32[]{:S(2)}) %all-to-all-start.3) | async-done | bytes 2097184 | tf_op jit(solution)/shard_map/all_to_all | solution.py:294
  95.7 54.2 %all_to_all.26.refs_1_ = f32[16,2,128,128]{3,2,1,0:T(8,128)} all-to-all(f32[16,2,128,128]{3,2,1,0:T(8,128)} %get-tuple-element.12), channel_id=1, replica_groups=mesh['chan'=16,'pulse'=16] {'pulse'}, dimensions={0} | all-to-all | bytes 4194304 | tf_op jit(solution)/shard_map/all_to_all | solution.py:294
  149.9 6.3 %all-to-all-start.1 = ((f32[16,2,2,128,128]{4,3,2,1,0:T(8,128)}), f32[16,2,2,128,128]{4,3,2,1,0:T(8,128)}, u32[]{:S(2)}, u32[]{:S(2)}) async-start(f32[16,2,2,128,128]{4,3,2,1,0:T(8,128)} %get-tuple-element.10), calls=%async_computation.1 | async-start | bytes 8388608 | tf_op jit(solution)/shard_map/all_to_all | solution.py:294
  156.2 0.0 reduce-scatter.2.cloned.1.call-start
  156.3 0.2 fusion
  156.5 0.1 broadcast_bitcast_fusion
  156.6 0.5 fusion.5
  157.1 0.1 stack.22
  157.2 0.1 stack.21
  157.3 0.7 fusion.3
  158.1 18.9 %azimuth_filter.3 = f32[16,2,256,128]{3,2,1,0:T(8,128)} custom-call(f32[16,2,128,128]{3,2,1,0:T(8,128)} %copy-done.1, f32[16,2,128,128]{3,2,1,0:T(8,128)} %all_to_all.26.refs_1_, bf16[2,256,256]{2,1,0:T(8,128)(2,1)} %constant.4.clone.fwd_ref.refs_1_.refs_2_, bf16[2,256,256]{2,1,0:T(8,128)(2,1)} %constant.12.clone.inv_ref.refs_2_.refs_3_, ...), custom_call_target="tpu_custom_call" | custom-call | tf_op jit(solution)/shard_map/azimuth_filter/pallas_call | solution.py:251
  176.9 75.5 %all-to-all-done.1.refs_0_ = f32[16,2,2,128,128]{4,3,2,1,0:T(8,128)} async-done(((f32[16,2,2,128,128]{4,3,2,1,0:T(8,128)}), f32[16,2,2,128,128]{4,3,2,1,0:T(8,128)}, u32[]{:S(2)}, u32[]{:S(2)}) %all-to-all-start.1) | async-done | bytes 4194336 | tf_op jit(solution)/shard_map/all_to_all | solution.py:294
  252.5 19.0 %azimuth_filter.2 = f32[16,2,256,128]{3,2,1,0:T(8,128)} custom-call(f32[16,2,2,128,128]{4,3,2,1,0:T(8,128)} %all-to-all-done.1.refs_0_, bf16[2,256,256]{2,1,0:T(8,128)(2,1)} %constant.4.clone.fwd_ref.refs_1_.refs_2_, bf16[2,256,256]{2,1,0:T(8,128)(2,1)} %constant.12.clone.inv_ref.refs_2_.refs_3_, f32[2,128,32]{2,1,0:T(8,128)} %constant.14.clone.refs_3_.refs_4_, ...), custom_call_target="tpu_custom_call" | custom-call | tf_op jit(solution)/shard_map/azimuth_filter/pallas_call | solution.py:251
  271.5 6.6 %all-to-all-start.2 = ((f32[16,2,256,128]{3,2,1,0:T(8,128)}), f32[16,2,256,128]{3,2,1,0:T(8,128)}, u32[]{:S(2)}, u32[]{:S(2)}) async-start(f32[16,2,256,128]{3,2,1,0:T(8,128)} %azimuth_filter.2), calls=%async_computation.2 | async-start | bytes 8388608 | tf_op jit(solution)/shard_map/all_to_all | solution.py:294
  278.1 2.0 migrate.2.refs_0_
  280.1 60.1 %all-to-all-done.2.s_ref = f32[16,2,256,128]{3,2,1,0:T(8,128)} async-done(((f32[16,2,256,128]{3,2,1,0:T(8,128)}), f32[16,2,256,128]{3,2,1,0:T(8,128)}, u32[]{:S(2)}, u32[]{:S(2)}) %all-to-all-start.2) | async-done | bytes 4194336 | tf_op jit(solution)/shard_map/all_to_all | solution.py:294
  340.2 3.4 migrate.3
  (12 shorter events, 0.1 us)
Async XLA Ops:
  6.5 149.7 %copy-start = (f32[2,64]{1,0:T(2,128)S(1)}, f32[2,64]{1,0:T(2,128)}, u32[]{:S(2)}) copy-start(f32[2,64]{1,0:T(2,128)} %param.18) | copy-start | bytes 1540
  7.8 18.5 %all-to-all-start = ((s32[16,1,2]{2,1,0:T(1,128)}), s32[16,1,2]{2,1,0:T(1,128)S(1)}, u32[]{:S(2)}, u32[]{:S(2)}) async-start(s32[16,1,2]{2,1,0:T(1,128)} %broadcast_in_dim.12), calls=%async_computation | async-start | bytes 16384 | tf_op jit(solution)/shard_map/all_to_all | solution.py:294
  43.2 52.5 %all-to-all-start.3 = ((f32[16,2,128,128]{3,2,1,0:T(8,128)}), f32[16,2,128,128]{3,2,1,0:T(8,128)S(1)}, u32[]{:S(2)}, u32[]{:S(2)}) async-start(f32[16,2,128,128]{3,2,1,0:T(8,128)} %get-tuple-element.11), calls=%async_computation.3 | async-start | bytes 4194304 | tf_op jit(solution)/shard_map/all_to_all | solution.py:294
  95.7 54.2 %copy-start.1 = (f32[16,2,128,128]{3,2,1,0:T(8,128)}, f32[16,2,128,128]{3,2,1,0:T(8,128)S(1)}, u32[]{:S(2)}) copy-start(f32[16,2,128,128]{3,2,1,0:T(8,128)S(1)} %all-to-all-done.3.refs_0_) | copy-start | bytes 6291460
  149.9 6.3 %copy-start.3 = (s32[1,32]{1,0:T(1,128)S(1)}, s32[1,32]{1,0:T(1,128)}, u32[]{:S(2)}) copy-start(s32[1,32]{1,0:T(1,128)} %param.19) | copy-start | bytes 388
  149.9 6.6 %copy-start.2 = (f32[4096,2]{0,1:T(2,128)S(1)}, f32[4096,2]{0,1:T(2,128)}, u32[]{:S(2)}) copy-start(f32[4096,2]{0,1:T(2,128)} %param.17) | copy-start | bytes 98308
  149.9 102.5 %all-to-all-start.1 = ((f32[16,2,2,128,128]{4,3,2,1,0:T(8,128)}), f32[16,2,2,128,128]{4,3,2,1,0:T(8,128)}, u32[]{:S(2)}, u32[]{:S(2)}) async-start(f32[16,2,2,128,128]{4,3,2,1,0:T(8,128)} %get-tuple-element.10), calls=%async_computation.1 | async-start | bytes 8388608 | tf_op jit(solution)/shard_map/all_to_all | solution.py:294
  156.2 121.8 %reduce-scatter.2.cloned.1.call-start = ((), (), s32[]{:S(2)}) async-start(), calls=%async_computation.6 | async-start | bytes 4456448 | tf_op jit(solution)/shard_map/reduce_scatter | solution.py:323
  271.5 68.7 %all-to-all-start.2 = ((f32[16,2,256,128]{3,2,1,0:T(8,128)}), f32[16,2,256,128]{3,2,1,0:T(8,128)}, u32[]{:S(2)}, u32[]{:S(2)}) async-start(f32[16,2,256,128]{3,2,1,0:T(8,128)} %azimuth_filter.2), calls=%async_computation.2 | async-start | bytes 8388608 | tf_op jit(solution)/shard_map/all_to_all | solution.py:294
Sparse Core Ops, SparseCore 0:
  177.1 85.2 reduce-scatter.1

commit v2 on v1

--- a/solution.py
+++ b/solution.py
@@ -14,6 +14,7 @@
 SLABS = 32
 INNER = 128
 ROWS = 32
+EARLY = 2
 
 
 def split(values):
@@ -81,9 +82,7 @@
     return re * cr - im * ci, re * ci + im * cr
 
 
-def range_kernel(offset_ref, x_ref, fwd_ref, inv_ref, tw_ref, chirp_ref, *refs):
-    z0_ref, z1_ref, mid_ref, y_ref = refs[-4:]
-
+def compress(x_ref, fwd_ref, inv_ref, tw_ref, chirp_ref, mid_ref, y_ref):
     def first(tile, carry):
         rows = pl.ds(pl.multiple_of(tile * 8, 8), 8)
         values = [
@@ -131,78 +130,137 @@
 
     lax.fori_loop(0, ROWS // 8, last, 0)
     y_ref[SLABS] = jnp.zeros((2 * ROWS, INNER), jnp.float32)
+
+
+def windows(offset_ref, y_ref, z0_ref, z1_ref):
     lanes = lax.broadcasted_iota(jnp.int32, (2 * ROWS, INNER), 1)
 
     def window(step, carry):
         for part in range(4):
             dest = step * 4 + part
-            for block, z_ref in ((0, z0_ref), (1, z1_ref)):
+            for block in range(2):
                 slab = 2 * dest + block
                 back = INNER - offset_ref[slab]
                 here = pltpu.roll(y_ref[slab], back, 1)
                 after = pltpu.roll(y_ref[slab + 1], back, 1)
                 shifted = jnp.where(lanes < back, here, after).reshape(2, ROWS, INNER)
                 if block:
-                    z_ref[dest, 0] = shifted
+                    z1_ref[dest, 0] = shifted
                 else:
-                    z_ref[dest] = shifted
+                    z0_ref[dest] = shifted
         return carry
 
     lax.fori_loop(0, SLABS // 8, window, 0)
 
 
-def range_compress(half, offsets, echoes, fwd, inv, chirp, other=None):
-    pulses, gates = echoes.shape[2] // 2, echoes.shape[3]
-    dests = gates // (2 * BLOCK)
-    steps = pulses // ROWS
-    outs = [
-        jax.ShapeDtypeStruct((dests, 2, pulses, BLOCK), jnp.float32),
-        jax.ShapeDtypeStruct((dests, 2, 2, pulses, BLOCK), jnp.float32),
+def early_kernel(x_ref, fwd_ref, inv_ref, tw_ref, chirp_ref, y_ref, mid_ref):
+    compress(x_ref, fwd_ref, inv_ref, tw_ref, chirp_ref, mid_ref, y_ref.at[0])
+
+
+def window_kernel(offset_ref, y_ref, z0_ref, z1_ref):
+    windows(offset_ref, y_ref.at[0], z0_ref, z1_ref)
+
+
+def late_kernel(offset_ref, x_ref, fwd_ref, inv_ref, tw_ref, chirp_ref, other_ref, z0_ref, z1_ref, mid_ref, y_ref):
+    compress(x_ref, fwd_ref, inv_ref, tw_ref, chirp_ref, mid_ref, y_ref)
+    windows(offset_ref, y_ref, z0_ref, z1_ref)
+
+
+def table_specs():
+    whole = pl.BlockSpec((2, 2 * INNER, 2 * INNER), lambda i, *_: (0, 0, 0))
+    table = pl.BlockSpec((2, SLABS, INNER), lambda i, *_: (0, 0, 0))
+    return [whole, whole, table, table]
+
+
+def range_early(steps, echoes, tables):
+    gates = echoes.shape[3]
+    slabs = (SLABS + 1, 2 * ROWS, INNER)
+    return pl.pallas_call(
+        early_kernel,
+        grid=(steps,),
+        in_specs=[pl.BlockSpec((1, 2, ROWS, gates), lambda i: (0, 0, i, 0))] + table_specs(),
+        out_specs=pl.BlockSpec((1, *slabs), lambda i: (i, 0, 0, 0)),
+        out_shape=jax.ShapeDtypeStruct((steps, *slabs), jnp.float32),
+        scratch_shapes=[pltpu.VMEM((SLABS, ROWS, 2 * INNER), jnp.float32)],
+        name="range_early",
+    )(echoes, *tables)
+
+
+def block_shapes(dests, rows):
+    return [
+        jax.ShapeDtypeStruct((dests, 2, rows, BLOCK), jnp.float32),
+        jax.ShapeDtypeStruct((dests, 2, 2, INNER, BLOCK), jnp.float32),
     ]
-    whole3 = pl.BlockSpec((2, 2 * INNER, 2 * INNER), lambda i, *_: (0, 0, 0))
-    table = pl.BlockSpec((2, SLABS, INNER), lambda i, *_: (0, 0, 0))
-    in_specs = [pl.BlockSpec((1, 2, ROWS, gates), lambda i, *_: (0, 0, half * steps + i, 0)), whole3, whole3, table, table]
-    args = [offsets, echoes, fwd, inv, jnp.asarray(twiddles()), chirp]
-    aliases = {}
-    if other is not None:
-        in_specs.append(pl.BlockSpec(memory_space=pl.ANY))
-        aliases = {len(args): 1}
-        args.append(other)
+
+
+def block_specs(dests, start):
+    tiles = INNER // ROWS
+    return [
+        pl.BlockSpec((dests, 2, ROWS, BLOCK), lambda i, *_: (0, 0, i, 0)),
+        pl.BlockSpec((dests, 1, 2, ROWS, BLOCK), lambda i, *_: (0, (start + i) // tiles, 0, (start + i) % tiles, 0)),
+    ]
+
+
+def range_window(offsets, early):
+    steps, slabs, _, _ = early.shape
+    dests = slabs // 2
     return pl.pallas_call(
-        range_kernel,
+        window_kernel,
         grid_spec=pltpu.PrefetchScalarGridSpec(
             num_scalar_prefetch=1,
             grid=(steps,),
-            in_specs=in_specs,
-            out_specs=[
-                pl.BlockSpec((dests, 2, ROWS, BLOCK), lambda i, *_: (0, 0, i, 0)),
-                pl.BlockSpec((dests, 1, 2, ROWS, BLOCK), lambda i, *_: (0, half, 0, i, 0)),
-            ],
+            in_specs=[pl.BlockSpec((1, slabs, 2 * ROWS, INNER), lambda i, *_: (i, 0, 0, 0))],
+            out_specs=block_specs(dests, 0),
+        ),
+        out_shape=block_shapes(dests, steps * ROWS),
+        name="range_window",
+    )(offsets, early)
+
+
+def range_late(start, offsets, echoes, tables, other):
+    pulses, gates = echoes.shape[2], echoes.shape[3]
+    dests = gates // (2 * BLOCK)
+    steps = pulses // ROWS - start
+    return pl.pallas_call(
+        late_kernel,
+        grid_spec=pltpu.PrefetchScalarGridSpec(
+            num_scalar_prefetch=1,
+            grid=(steps,),
+            in_specs=[pl.BlockSpec((1, 2, ROWS, gates), lambda i, *_: (0, 0, start + i, 0))]
+            + table_specs()
+            + [pl.BlockSpec(memory_space=pl.ANY)],
+            out_specs=block_specs(dests, start),
             scratch_shapes=[
                 pltpu.VMEM((SLABS, ROWS, 2 * INNER), jnp.float32),
                 pltpu.VMEM((SLABS + 1, 2 * ROWS, INNER), jnp.float32),
             ],
         ),
-        out_shape=outs,
-        input_output_aliases=aliases,
-        name="range_compress",
-    )(*args)
-
-
-def azimuth_kernel(count, *refs):
+        out_shape=block_shapes(dests, steps * ROWS),
+        input_output_aliases={6: 1},
+        name="range_late",
+    )(offsets, echoes, *tables, other)
+
+
+def azimuth_kernel(count, place_ref, *refs):
     x_refs = refs[:count]
-    fwd_ref, inv_ref, tw_ref, gain_ref, o_ref, mid_ref, wide_ref = refs[count:]
-
-    def slab(a, part, rows):
-        if count == 2:
-            return x_refs[a % 2][a // 2, part, rows, :]
-        return x_refs[0][a // 2, a % 2, part, rows, :]
-
-    def first(tile, carry):
+    fwd_ref, inv_ref, tw_ref, gain_ref = refs[count : count + 4]
+    out_refs = refs[count + 4 : -4]
+    mid_ref, wide_ref, o_ref, sem = refs[-4:]
+
+    def slab(a, part, tile, upper):
+        start = pl.multiple_of(tile * 8, 8)
+        if count == 1:
+            return x_refs[0][a // 2, a % 2, part, pl.ds(start, 8), :]
+        rows = x_refs[0].shape[2]
+        if a % 2 == 0 and not upper:
+            return x_refs[0][a // 2, part, pl.ds(start, 8), :]
+        return x_refs[1][a // 2, part, pl.ds(pl.multiple_of(start + (a % 2) * INNER - rows, 8), 8), :]
+
+    def first(upper, tile, carry):
         start = pl.multiple_of(tile * 8, 8)
         rows = pl.ds(start, 8)
         lower = pl.ds(pl.multiple_of(INNER + tile * 8, 8), 8)
-        values = [(slab(a, 0, rows), slab(a, 1, rows)) for a in range(SLABS)]
+        values = [(slab(a, 0, tile, upper), slab(a, 1, tile, upper)) for a in range(SLABS)]
         tr, ti = tw_ref[0, rows, :], tw_ref[1, rows, :]
         gr, gi = gain_ref[0, rows, :], gain_ref[1, rows, :]
         for k, (re, im) in enumerate(butterflies(values, -1)):
@@ -214,7 +272,11 @@
             wide_ref[k // 2, lower, lane] = jnp.broadcast_to(gi[:, k : k + 1], (8, INNER))
         return carry
 
-    lax.fori_loop(0, INNER // 8, first, 0)
+    tiles = INNER // 8
+    edge = x_refs[0].shape[2] // 8 if count == 2 else tiles
+    lax.fori_loop(0, edge, functools.partial(first, False), 0)
+    if edge < tiles:
+        lax.fori_loop(edge, tiles, functools.partial(first, True), 0)
 
     def middle(step, carry):
         pairs = [2 * step, 2 * step + 1]
@@ -243,44 +305,68 @@
 
     lax.fori_loop(0, INNER // 8, last, 0)
 
-
-def azimuth_filter(received, fwd, inv, gain):
+    place = place_ref[0]
+    blocks = o_ref.shape[0]
+    copies = []
+    for block in range(blocks):
+        source = o_ref.at[jnp.bitwise_xor(place, block)]
+        if len(out_refs) == blocks:
+            target = out_refs[block]
+        else:
+            source = o_ref.at[jnp.bitwise_xor(jnp.bitwise_and(place, 1), block)]
+            target = out_refs[block % 2].at[block // 2]
+        copies.append(pltpu.make_async_copy(source, target, sem.at[block]))
+    for copy in copies:
+        copy.start()
+    for copy in copies:
+        copy.wait()
+
+
+def azimuth_filter(outs, place, received, fwd, inv, gain):
     vmem = pl.BlockSpec(memory_space=pltpu.VMEM)
     count = len(received)
     devices = received[0].shape[0]
+    shape = (2, 2 * INNER, BLOCK)
+    each = shape if outs == devices else (devices // outs, *shape)
     return pl.pallas_call(
         functools.partial(azimuth_kernel, count),
-        in_specs=[vmem] * (count + 4),
-        out_specs=vmem,
-        out_shape=jax.ShapeDtypeStruct((devices, 2, 2 * INNER, BLOCK), jnp.float32),
+        in_specs=[pl.BlockSpec(memory_space=pltpu.SMEM)] + [vmem] * (count + 4),
+        out_specs=[pl.BlockSpec(memory_space=pl.ANY)] * outs,
+        out_shape=[jax.ShapeDtypeStruct(each, jnp.float32)] * outs,
         scratch_shapes=[
             pltpu.VMEM((SLABS // 2, 2 * INNER, 2 * INNER), jnp.float32),
             pltpu.VMEM((SLABS // 2, 2 * INNER, 2 * INNER), jnp.float32),
+            pltpu.VMEM((devices, *shape), jnp.float32),
+            pltpu.SemaphoreType.DMA((devices,)),
         ],
         name="azimuth_filter",
-    )(*received, fwd, inv, jnp.asarray(twiddles().transpose(0, 2, 1)), gain)
-
-
-def migrate_kernel(s_ref, kernel_ref, *refs):
-    rows = jnp.sum(s_ref[...], axis=0).reshape(-1, BLOCK)
-    moved = jnp.dot(rows, kernel_ref[0], precision=lax.Precision.HIGHEST, preferred_element_type=jnp.float32)
+    )(place, *received, fwd, inv, jnp.asarray(twiddles().transpose(0, 2, 1)), gain)
+
+
+def migrate_kernel(count, *refs):
+    total = refs[0][...]
+    if count == 1:
+        total = jnp.sum(total, axis=0)
+    for ref in refs[1:count]:
+        total = total + ref[...]
+    moved = jnp.dot(
+        total.reshape(-1, BLOCK), refs[count][0], precision=lax.Precision.HIGHEST, preferred_element_type=jnp.float32
+    )
     refs[-1][...] = moved.reshape(2, -1, BLOCK)
 
 
 def migrate(block, parts, kernel, other=None):
-    devices, _, pulses, _ = parts.shape
-    args = [parts, kernel]
-    in_specs = [
-        pl.BlockSpec((devices, 2, pulses, BLOCK), lambda i: (0, 0, 0, 0)),
-        pl.BlockSpec((1, BLOCK, BLOCK), lambda i: (block, 0, 0)),
-    ]
+    pulses = parts[0].shape[-2]
+    args = [*parts, kernel]
+    in_specs = [pl.BlockSpec(part.shape, lambda i, n=part.ndim: (0,) * n) for part in parts]
+    in_specs.append(pl.BlockSpec((1, BLOCK, BLOCK), lambda i: (block, 0, 0)))
     aliases = {}
     if other is not None:
         in_specs.append(pl.BlockSpec(memory_space=pl.ANY))
-        aliases = {2: 0}
+        aliases = {len(args): 0}
         args.append(other)
     return pl.pallas_call(
-        migrate_kernel,
+        functools.partial(migrate_kernel, len(parts)),
         grid=(1,),
         in_specs=in_specs,
         out_specs=pl.BlockSpec((2, pulses, BLOCK), lambda i: (0, 0, block)),
@@ -290,8 +376,13 @@
     )(*args)
 
 
-def turn(blocks, axis):
-    return lax.all_to_all(blocks, axis, split_axis=0, concat_axis=0, tiled=True)
+def turn(blocks, axis, groups=None):
+    return lax.all_to_all(blocks, axis, split_axis=0, concat_axis=0, tiled=True, axis_index_groups=groups)
+
+
+def swap(block, distance):
+    devices = range(lax.axis_size("chan"))
+    return lax.ppermute(block, "chan", [(i, i ^ distance) for i in devices])
 
 
 def body(echoes, chirp_phase, rcmc_kernel, rcmc_offset, az_phase, weight_table, weight_index):
@@ -304,8 +395,10 @@
     offsets = turn(jnp.broadcast_to(rcmc_offset, (devices, rcmc_offset.shape[0])), "pulse").reshape(-1)
     by_slab = chirp_phase.reshape(INNER, SLABS).T
     chirp = jnp.stack([jnp.cos(by_slab), jnp.sin(by_slab)]) * (1.0 / gates)
-    early, partial = range_compress(0, offsets, echoes, fwd, inv, chirp)
-    late, full = range_compress(1, offsets, echoes, fwd, inv, chirp, partial)
+    tables = (fwd, inv, jnp.asarray(twiddles()), chirp)
+    compressed = range_early(EARLY, echoes, tables)
+    early, partial = range_window(offsets, compressed)
+    late, full = range_late(EARLY, offsets, echoes, tables, partial)
 
     table_count = weight_table.shape[1]
     entry_ids = lax.broadcasted_iota(jnp.int32, (weight_index.shape[1], table_count), 1)
@@ -319,12 +412,16 @@
     early = turn(early, "pulse")
     late = turn(late, "pulse")
     full = turn(full, "pulse")
-    first = azimuth_filter([early, late], fwd, inv, gain[:, 0])
-    first = lax.psum_scatter(first, "chan", scatter_dimension=0, tiled=True)
+    place = lax.axis_index("chan").astype(jnp.int32).reshape(1)
+    channels = lax.axis_size("chan")
+    first = azimuth_filter(channels, place, [early, late], fwd, inv, gain[:, 0])
+    first = [first[0]] + [swap(first[k], k) for k in range(1, channels)]
     image = migrate(0, first, rcmc_kernel)
-    second = azimuth_filter([full], fwd, inv, gain[:, 1])
-    second = turn(second, "chan")
-    return migrate(1, second, rcmc_kernel, image)
+    keep, give = azimuth_filter(2, place, [full], fwd, inv, gain[:, 1])
+    pair = keep + swap(give, 1)
+    groups = [list(range(core, channels, 2)) for core in range(2)]
+    second = turn(pair, "chan", groups)
+    return migrate(1, [second], rcmc_kernel, image)
 
 
 def solution(mesh):

time: 351 us -> 341 us (0.972)
  the two profiles are of different devices: /device:TPU:27 before, /device:TPU:4 now
where the time goes in v2:
time: 341 us; the launch traced here: 337 us
  blocking collectives  101 us (30%)
  waiting for transfers between devices  93.7 us (27%)
  Pallas kernels  76.8 us (23%)
  starting transfers between devices  55.3 us (16%)
  other arithmetic  5.23 us (2%)
  local copies, waits for them, and re-layouts  4.35 us (1%)
    all_to_all x1, blocking collectives, turn(): lax.all_to_all(blocks, axis, split_axis=0, concat_axis=0, tiled=True, axi...  101 us
    ppermute x16, waiting for transfers between devices, swap(): return lax.ppermute(block, 'chan', [(i, i ^ distance) for i in devices])  49.7 us
    all_to_all x4, waiting for transfers between devices, turn(): lax.all_to_all(blocks, axis, split_axis=0, concat_axis=0, tiled=True, axi...  44 us
    pallas_call x2, Pallas kernels, azimuth_filter(): pl.pallas_call(functools.partial(azimuth_kernel, count), in_specs=[pl.Blo...  38.1 us
    all_to_all x4, starting transfers between devices, turn(): lax.all_to_all(blocks, axis, split_axis=0, concat_axis=0, tiled=True, axi...  33.5 us
    ppermute x16, starting transfers between devices, swap(): return lax.ppermute(block, 'chan', [(i, i ^ distance) for i in devices])  21.8 us
    pallas_call x1, Pallas kernels, range_late(): pl.pallas_call(late_kernel, grid_spec=pltpu.PrefetchScalarGridSpec(num_sc...  21.4 us
  transfers between devices with their start and end apart: 20, of which 13 were waited for; matrix products, arithmetic and copies ran while one was open for 2% of the time, Pallas kernels for 21%

profile of v2, /device:TPU:4, one launch (start us, length us, event | category | flops | bytes accessed | tf_op | source)
XLA Modules:
  0.0 336.9 jit_solution(8129320263226029445)
XLA Ops:
  1.3 11.4 %all-to-all-start = ((s32[16,1,2]{2,1,0:T(1,128)}), s32[16,1,2]{2,1,0:T(1,128)S(1)}, u32[]{:S(2)}, u32[]{:S(2)}) async-start(s32[16,1,2]{2,1,0:T(1,128)} %broadcast_in_dim.12), calls=%async_computation | async-start | bytes 16384 | tf_op jit(solution)/shard_map/all_to_all | solution.py:380
  14.5 6.7 %range_early.1.y_ref = f32[2,33,64,128]{3,2,1,0:T(8,128)} custom-call(f32[1,2,256,4096]{3,2,1,0:T(8,128)} %x_ref.3, bf16[2,256,256]{2,1,0:T(8,128)(2,1)} %constant.16.clone.fwd_ref.refs_1_.refs_2_, bf16[2,256,256]{2,1,0:T(8,128)(2,1)} %constant.17.clone.inv_ref.refs_2_.refs_3_, f32[2,32,128]{2,1,0:T(8,128)} %constant.18.clone.tw_ref, ...), custom_call_target="tpu_custom_call" | custom-call | tf_op jit(solution)/shard_map/range_early/pallas_call | solution.py:178
  23.0 4.6 %range_window.1 = (f32[16,2,64,128]{3,2,1,0:T(8,128)}, f32[16,2,2,128,128]{4,3,2,1,0:T(8,128)}) custom-call(s32[32]{0:T(128)} %reshape.30.offset_ref, f32[2,33,64,128]{3,2,1,0:T(8,128)} %range_early.1.y_ref), custom_call_target="tpu_custom_call" | custom-call | tf_op jit(solution)/shard_map/range_window/pallas_call | solution.py:207
  27.6 9.6 %all-to-all-start.3 = ((f32[16,2,64,128]{3,2,1,0:T(8,128)}), f32[16,2,64,128]{3,2,1,0:T(8,128)S(1)}, u32[]{:S(2)}, u32[]{:S(2)}) async-start(f32[16,2,64,128]{3,2,1,0:T(8,128)} %get-tuple-element.31), calls=%async_computation.3 | async-start | bytes 2097152 | tf_op jit(solution)/shard_map/all_to_all | solution.py:380
  37.2 21.4 %range_late.1 = (f32[16,2,192,128]{3,2,1,0:T(8,128)}, f32[16,2,2,128,128]{4,3,2,1,0:T(8,128)}) custom-call(s32[32]{0:T(128)} %reshape.30.offset_ref, f32[1,2,256,4096]{3,2,1,0:T(8,128)} %x_ref.3, bf16[2,256,256]{2,1,0:T(8,128)(2,1)} %constant.16.clone.fwd_ref.refs_1_.refs_2_, ...), custom_call_target="tpu_custom_call", output_to_operand_aliasing={{1}: (6, {})} | custom-call | tf_op jit(solution)/shard_map/range_late/pallas_call | solution.py:224
  58.6 3.3 all-to-all-done.3.refs_0_
  61.9 101.2 %all_to_all.26.refs_0_ = f32[16,2,2,128,128]{4,3,2,1,0:T(8,128)} all-to-all(f32[16,2,2,128,128]{4,3,2,1,0:T(8,128)} %get-tuple-element.28), channel_id=1, replica_groups=mesh['chan'=16,'pulse'=16] {'pulse'}, dimensions={0} | all-to-all | bytes 8388608 | tf_op jit(solution)/shard_map/all_to_all | solution.py:380
  163.1 7.3 %all-to-all-start.4 = ((f32[16,2,192,128]{3,2,1,0:T(8,128)}), f32[16,2,192,128]{3,2,1,0:T(8,128)S(1)}, u32[]{:S(2)}, u32[]{:S(2)}) async-start(f32[16,2,192,128]{3,2,1,0:T(8,128)} %get-tuple-element.32), calls=%async_computation.4 | async-start | bytes 6291456 | tf_op jit(solution)/shard_map/all_to_all | solution.py:380
  172.2 19.0 %azimuth_filter.2 = (f32[8,2,256,128]{3,2,1,0:T(8,128)}, f32[8,2,256,128]{3,2,1,0:T(8,128)}) custom-call(s32[1]{0:T(128)} %bitcast.place_ref, f32[16,2,2,128,128]{4,3,2,1,0:T(8,128)} %all_to_all.26.refs_0_, bf16[2,256,256]{2,1,0:T(8,128)(2,1)} %constant.16.clone.fwd_ref.refs_1_.refs_2_, bf16[2,256,256]{2,1,0:T(8,128)(2,1)} %constant.17.clone.inv_ref.refs_2_.refs_3_, ...), custom_call_target="tpu_custom_call" | custom-call | tf_op jit(solution)/shard_map/azimuth_filter/pallas_call | solution.py:331
  191.4 4.4 %collective-permute-done = f32[8,2,256,128]{3,2,1,0:T(8,128)S(1)} collective-permute-done((f32[8,2,256,128]{3,2,1,0:T(8,128)}, f32[8,2,256,128]{3,2,1,0:T(8,128)S(1)}, u32[]{:S(2)}, u32[]{:S(2)}) %collective-permute-start) | collective-permute-done | bytes 2097184 | tf_op jit(solution)/shard_map/ppermute | solution.py:385
  195.8 3.2 add.11
  198.9 40.7 %all-to-all-done.4.refs_1_ = f32[16,2,192,128]{3,2,1,0:T(8,128)S(1)} async-done(((f32[16,2,192,128]{3,2,1,0:T(8,128)}), f32[16,2,192,128]{3,2,1,0:T(8,128)S(1)}, u32[]{:S(2)}, u32[]{:S(2)}) %all-to-all-start.4) | async-done | bytes 3145760 | tf_op jit(solution)/shard_map/all_to_all | solution.py:380
  239.6 5.1 %all-to-all-start.2 = ((f32[8,2,256,128]{3,2,1,0:T(8,128)}), f32[8,2,256,128]{3,2,1,0:T(8,128)}, u32[]{:S(2)}, u32[]{:S(2)}) async-start(f32[8,2,256,128]{3,2,1,0:T(8,128)} %add.11), calls=%async_computation.2 | async-start | bytes 4194304 | tf_op jit(solution)/shard_map/all_to_all | solution.py:380
  244.7 19.0 %azimuth_filter.3 = (f32[2,256,128]{2,1,0:T(8,128)}, f32[2,256,128]{2,1,0:T(8,128)}, f32[2,256,128]{2,1,0:T(8,128)}, f32[2,256,128]{2,1,0:T(8,128)}, f32[2,256,1...) custom-call(s32[1]{0:T(128)} %bitcast.place_ref, ...), custom_call_target="tpu_custom_call" | custom-call | tf_op jit(solution)/shard_map/azimuth_filter/pallas_call | solution.py:331
  263.9 2.1 collective-permute-start.2
  266.0 3.2 collective-permute-start.4
  269.2 2.9 collective-permute-start.6
  272.2 3.3 collective-permute-done.2.refs_2_
  275.7 3.3 collective-permute-done.3.refs_3_
  279.0 2.4 collective-permute-start.8
  281.4 6.4 %collective-permute-done.4.refs_4_ = f32[2,256,128]{2,1,0:T(8,128)S(1)} collective-permute-done((f32[2,256,128]{2,1,0:T(8,128)}, f32[2,256,128]{2,1,0:T(8,128)S(1)}, u32[]{:S(2)}, u32[]{:S(2)}) %collective-permute-start.4) | collective-permute-done | bytes 262176 | tf_op jit(solution)/shard_map/ppermute | solution.py:385
  287.9 4.5 %collective-permute-done.5.refs_5_ = f32[2,256,128]{2,1,0:T(8,128)S(1)} collective-permute-done((f32[2,256,128]{2,1,0:T(8,128)}, f32[2,256,128]{2,1,0:T(8,128)S(1)}, u32[]{:S(2)}, u32[]{:S(2)}) %collective-permute-start.5) | collective-permute-done | bytes 262176 | tf_op jit(solution)/shard_map/ppermute | solution.py:385
  292.4 1.9 collective-permute-start.10
  296.1 2.4 collective-permute-start.12
  299.4 4.3 %collective-permute-start.14 = (f32[2,256,128]{2,1,0:T(8,128)}, f32[2,256,128]{2,1,0:T(8,128)}, u32[]{:S(2)}, u32[]{:S(2)}) collective-permute-start(f32[2,256,128]{2,1,0:T(8,128)} %get-tuple-element.47), channel_id=1, source_target_pairs={{0,224},{16,240},{32,192},{48,208},{64,160},{80,176},{96,128},{112... | collective-permute-start | bytes 786440 | tf_op jit(solution)/shard_map/ppermute | solution.py:385
  304.1 3.0 collective-permute-done.11.refs_11_
  307.1 6.9 %collective-permute-done.12.refs_12_ = f32[2,256,128]{2,1,0:T(8,128)S(1)} collective-permute-done((f32[2,256,128]{2,1,0:T(8,128)}, f32[2,256,128]{2,1,0:T(8,128)S(1)}, u32[]{:S(2)}, u32[]{:S(2)}) %collective-permute-start.12) | collective-permute-done | bytes 262176 | tf_op jit(solution)/shard_map/ppermute | solution.py:385
  314.0 5.5 %collective-permute-done.13.refs_13_ = f32[2,256,128]{2,1,0:T(8,128)S(1)} collective-permute-done((f32[2,256,128]{2,1,0:T(8,128)}, f32[2,256,128]{2,1,0:T(8,128)S(1)}, u32[]{:S(2)}, u32[]{:S(2)}) %collective-permute-start.13) | collective-permute-done | bytes 262176 | tf_op jit(solution)/shard_map/ppermute | solution.py:385
  319.5 5.5 %collective-permute-done.14.refs_14_ = f32[2,256,128]{2,1,0:T(8,128)} collective-permute-done((f32[2,256,128]{2,1,0:T(8,128)}, f32[2,256,128]{2,1,0:T(8,128)}, u32[]{:S(2)}, u32[]{:S(2)}) %collective-permute-start.14) | collective-permute-done | bytes 262176 | tf_op jit(solution)/shard_map/ppermute | solution.py:385
  325.0 5.8 %collective-permute-done.15.refs_15_ = f32[2,256,128]{2,1,0:T(8,128)} collective-permute-done((f32[2,256,128]{2,1,0:T(8,128)}, f32[2,256,128]{2,1,0:T(8,128)}, u32[]{:S(2)}, u32[]{:S(2)}) %collective-permute-start.15) | collective-permute-done | bytes 262176 | tf_op jit(solution)/shard_map/ppermute | solution.py:385
  330.9 3.3 migrate.2.refs_2_
  334.3 2.7 migrate.3
  (71 shorter events, 10.4 us)
Async XLA Ops:
  0.0 170.5 %copy-start = (f32[2,64]{1,0:T(2,128)S(1)}, f32[2,64]{1,0:T(2,128)}, u32[]{:S(2)}) copy-start(f32[2,64]{1,0:T(2,128)} %param.17) | copy-start | bytes 1540
  1.3 19.9 %all-to-all-start = ((s32[16,1,2]{2,1,0:T(1,128)}), s32[16,1,2]{2,1,0:T(1,128)S(1)}, u32[]{:S(2)}, u32[]{:S(2)}) async-start(s32[16,1,2]{2,1,0:T(1,128)} %broadcast_in_dim.12), calls=%async_computation | async-start | bytes 16384 | tf_op jit(solution)/shard_map/all_to_all | solution.py:380
  27.6 34.3 %all-to-all-start.3 = ((f32[16,2,64,128]{3,2,1,0:T(8,128)}), f32[16,2,64,128]{3,2,1,0:T(8,128)S(1)}, u32[]{:S(2)}, u32[]{:S(2)}) async-start(f32[16,2,64,128]{3,2,1,0:T(8,128)} %get-tuple-element.31), calls=%async_computation.3 | async-start | bytes 2097152 | tf_op jit(solution)/shard_map/all_to_all | solution.py:380
  61.9 101.2 %copy-start.2 = (f32[16,2,64,128]{3,2,1,0:T(8,128)}, f32[16,2,64,128]{3,2,1,0:T(8,128)S(1)}, u32[]{:S(2)}) copy-start(f32[16,2,64,128]{3,2,1,0:T(8,128)S(1)} %all-to-all-done.3.refs_0_) | copy-start | bytes 3145732
  163.1 76.5 %all-to-all-start.4 = ((f32[16,2,192,128]{3,2,1,0:T(8,128)}), f32[16,2,192,128]{3,2,1,0:T(8,128)S(1)}, u32[]{:S(2)}, u32[]{:S(2)}) async-start(f32[16,2,192,128]{3,2,1,0:T(8,128)} %get-tuple-element.32), calls=%async_computation.4 | async-start | bytes 6291456 | tf_op jit(solution)/shard_map/all_to_all | solution.py:380
  191.3 4.5 %collective-permute-start = (f32[8,2,256,128]{3,2,1,0:T(8,128)}, f32[8,2,256,128]{3,2,1,0:T(8,128)S(1)}, u32[]{:S(2)}, u32[]{:S(2)}) collective-permute-start(f32[8,2,256,128]{3,2,1,0:T(8,128)} %get-tuple-element.30), channel_id=1, source_target_pairs={{0,16},{16,0},{32,48},{48,32},{64,80},{80,64},{96,112},{112,96},{1... | collective-permute-start | bytes 6291464 | tf_op jit(solution)/shard_map/ppermute | solution.py:385
  239.6 94.6 %all-to-all-start.2 = ((f32[8,2,256,128]{3,2,1,0:T(8,128)}), f32[8,2,256,128]{3,2,1,0:T(8,128)}, u32[]{:S(2)}, u32[]{:S(2)}) async-start(f32[8,2,256,128]{3,2,1,0:T(8,128)} %add.11), calls=%async_computation.2 | async-start | bytes 4194304 | tf_op jit(solution)/shard_map/all_to_all | solution.py:380
  263.8 5.5 %collective-permute-start.1 = (f32[2,256,128]{2,1,0:T(8,128)}, f32[2,256,128]{2,1,0:T(8,128)S(1)}, u32[]{:S(2)}, u32[]{:S(2)}) collective-permute-start(f32[2,256,128]{2,1,0:T(8,128)} %get-tuple-element.34), channel_id=1, source_target_pairs={{0,16},{16,0},{32,48},{48,32},{64,80},{80,64},{96,112},{112,96},{1... | collective-permute-start | bytes 786440 | tf_op jit(solution)/shard_map/ppermute | solution.py:385
  263.9 11.6 %collective-permute-start.2 = (f32[2,256,128]{2,1,0:T(8,128)}, f32[2,256,128]{2,1,0:T(8,128)S(1)}, u32[]{:S(2)}, u32[]{:S(2)}) collective-permute-start(f32[2,256,128]{2,1,0:T(8,128)} %get-tuple-element.35), channel_id=1, source_target_pairs={{0,32},{16,48},{32,0},{48,16},{64,96},{80,112},{96,64},{112,80},{1... | collective-permute-start | bytes 786440 | tf_op jit(solution)/shard_map/ppermute | solution.py:385
  266.0 13.1 %collective-permute-start.3 = (f32[2,256,128]{2,1,0:T(8,128)}, f32[2,256,128]{2,1,0:T(8,128)S(1)}, u32[]{:S(2)}, u32[]{:S(2)}) collective-permute-start(f32[2,256,128]{2,1,0:T(8,128)} %get-tuple-element.36), channel_id=1, source_target_pairs={{0,48},{16,32},{32,16},{48,0},{64,112},{80,96},{96,80},{112,64},{1... | collective-permute-start | bytes 786440 | tf_op jit(solution)/shard_map/ppermute | solution.py:385
  266.0 21.9 %collective-permute-start.4 = (f32[2,256,128]{2,1,0:T(8,128)}, f32[2,256,128]{2,1,0:T(8,128)S(1)}, u32[]{:S(2)}, u32[]{:S(2)}) collective-permute-start(f32[2,256,128]{2,1,0:T(8,128)} %get-tuple-element.37), channel_id=1, source_target_pairs={{0,64},{16,80},{32,96},{48,112},{64,0},{80,16},{96,32},{112,48},{1... | collective-permute-start | bytes 786440 | tf_op jit(solution)/shard_map/ppermute | solution.py:385
  269.2 23.2 %collective-permute-start.5 = (f32[2,256,128]{2,1,0:T(8,128)}, f32[2,256,128]{2,1,0:T(8,128)S(1)}, u32[]{:S(2)}, u32[]{:S(2)}) collective-permute-start(f32[2,256,128]{2,1,0:T(8,128)} %get-tuple-element.38), channel_id=1, source_target_pairs={{0,80},{16,64},{32,112},{48,96},{64,16},{80,0},{96,48},{112,32},{1... | collective-permute-start | bytes 786440 | tf_op jit(solution)/shard_map/ppermute | solution.py:385
  269.2 61.6 %copy-start.3 = (f32[2,256,128]{2,1,0:T(8,128)}, f32[2,256,128]{2,1,0:T(8,128)S(1)}, u32[]{:S(2)}) copy-start(f32[2,256,128]{2,1,0:T(8,128)S(1)} %collective-permute-done.1.refs_1_) | copy-start | bytes 786436
  269.2 25.0 %collective-permute-start.6 = (f32[2,256,128]{2,1,0:T(8,128)}, f32[2,256,128]{2,1,0:T(8,128)S(1)}, u32[]{:S(2)}, u32[]{:S(2)}) collective-permute-start(f32[2,256,128]{2,1,0:T(8,128)} %get-tuple-element.39), channel_id=1, source_target_pairs={{0,96},{16,112},{32,64},{48,80},{64,32},{80,48},{96,0},{112,16},{1... | collective-permute-start | bytes 786440 | tf_op jit(solution)/shard_map/ppermute | solution.py:385
  275.4 55.4 %copy-start.4 = (f32[2,256,128]{2,1,0:T(8,128)}, f32[2,256,128]{2,1,0:T(8,128)S(1)}, u32[]{:S(2)}) copy-start(f32[2,256,128]{2,1,0:T(8,128)S(1)} %collective-permute-done.2.refs_2_) | copy-start | bytes 786436
  275.4 20.7 %collective-permute-start.7 = (f32[2,256,128]{2,1,0:T(8,128)}, f32[2,256,128]{2,1,0:T(8,128)S(1)}, u32[]{:S(2)}, u32[]{:S(2)}) collective-permute-start(f32[2,256,128]{2,1,0:T(8,128)} %get-tuple-element.40), channel_id=1, source_target_pairs={{0,112},{16,96},{32,80},{48,64},{64,48},{80,32},{96,16},{112,0},{1... | collective-permute-start | bytes 786440 | tf_op jit(solution)/shard_map/ppermute | solution.py:385
  279.0 51.8 %copy-start.5 = (f32[2,256,128]{2,1,0:T(8,128)}, f32[2,256,128]{2,1,0:T(8,128)S(1)}, u32[]{:S(2)}) copy-start(f32[2,256,128]{2,1,0:T(8,128)S(1)} %collective-permute-done.3.refs_3_) | copy-start | bytes 786436
  279.0 19.4 %collective-permute-start.8 = (f32[2,256,128]{2,1,0:T(8,128)}, f32[2,256,128]{2,1,0:T(8,128)S(1)}, u32[]{:S(2)}, u32[]{:S(2)}) collective-permute-start(f32[2,256,128]{2,1,0:T(8,128)} %get-tuple-element.41), channel_id=1, source_target_pairs={{0,128},{16,144},{32,160},{48,176},{64,192},{80,208},{96,224},{112... | collective-permute-start | bytes 786440 | tf_op jit(solution)/shard_map/ppermute | solution.py:385
  287.9 43.0 %copy-start.6 = (f32[2,256,128]{2,1,0:T(8,128)}, f32[2,256,128]{2,1,0:T(8,128)S(1)}, u32[]{:S(2)}) copy-start(f32[2,256,128]{2,1,0:T(8,128)S(1)} %collective-permute-done.4.refs_4_) | copy-start | bytes 786436
  287.9 11.5 %collective-permute-start.9 = (f32[2,256,128]{2,1,0:T(8,128)}, f32[2,256,128]{2,1,0:T(8,128)S(1)}, u32[]{:S(2)}, u32[]{:S(2)}) collective-permute-start(f32[2,256,128]{2,1,0:T(8,128)} %get-tuple-element.42), channel_id=1, source_target_pairs={{0,144},{16,128},{32,176},{48,160},{64,208},{80,192},{96,240},{112... | collective-permute-start | bytes 786440 | tf_op jit(solution)/shard_map/ppermute | solution.py:385
  292.4 38.5 %copy-start.7 = (f32[2,256,128]{2,1,0:T(8,128)}, f32[2,256,128]{2,1,0:T(8,128)S(1)}, u32[]{:S(2)}) copy-start(f32[2,256,128]{2,1,0:T(8,128)S(1)} %collective-permute-done.5.refs_5_) | copy-start | bytes 786436
  292.4 11.3 %collective-permute-start.10 = (f32[2,256,128]{2,1,0:T(8,128)}, f32[2,256,128]{2,1,0:T(8,128)S(1)}, u32[]{:S(2)}, u32[]{:S(2)}) collective-permute-start(f32[2,256,128]{2,1,0:T(8,128)} %get-tuple-element.43), channel_id=1, source_target_pairs={{0,160},{16,176},{32,128},{48,144},{64,224},{80,240},{96,192},{112... | collective-permute-start | bytes 786440 | tf_op jit(solution)/shard_map/ppermute | solution.py:385
  294.3 36.6 %copy-start.8 = (f32[2,256,128]{2,1,0:T(8,128)}, f32[2,256,128]{2,1,0:T(8,128)S(1)}, u32[]{:S(2)}) copy-start(f32[2,256,128]{2,1,0:T(8,128)S(1)} %collective-permute-done.6.refs_6_) | copy-start | bytes 786436
  294.3 12.8 %collective-permute-start.11 = (f32[2,256,128]{2,1,0:T(8,128)}, f32[2,256,128]{2,1,0:T(8,128)S(1)}, u32[]{:S(2)}, u32[]{:S(2)}) collective-permute-start(f32[2,256,128]{2,1,0:T(8,128)} %get-tuple-element.44), channel_id=1, source_target_pairs={{0,176},{16,160},{32,144},{48,128},{64,240},{80,224},{96,208},{112... | collective-permute-start | bytes 786440 | tf_op jit(solution)/shard_map/ppermute | solution.py:385
  296.1 34.8 %copy-start.9 = (f32[2,256,128]{2,1,0:T(8,128)}, f32[2,256,128]{2,1,0:T(8,128)S(1)}, u32[]{:S(2)}) copy-start(f32[2,256,128]{2,1,0:T(8,128)S(1)} %collective-permute-done.7.refs_7_) | copy-start | bytes 786436
  296.1 17.9 %collective-permute-start.12 = (f32[2,256,128]{2,1,0:T(8,128)}, f32[2,256,128]{2,1,0:T(8,128)S(1)}, u32[]{:S(2)}, u32[]{:S(2)}) collective-permute-start(f32[2,256,128]{2,1,0:T(8,128)} %get-tuple-element.45), channel_id=1, source_target_pairs={{0,192},{16,208},{32,224},{48,240},{64,128},{80,144},{96,160},{112... | collective-permute-start | bytes 786440 | tf_op jit(solution)/shard_map/ppermute | solution.py:385
  298.5 32.4 %copy-start.10 = (f32[2,256,128]{2,1,0:T(8,128)}, f32[2,256,128]{2,1,0:T(8,128)S(1)}, u32[]{:S(2)}) copy-start(f32[2,256,128]{2,1,0:T(8,128)S(1)} %collective-permute-done.8.refs_8_) | copy-start | bytes 786436
  298.5 21.0 %collective-permute-start.13 = (f32[2,256,128]{2,1,0:T(8,128)}, f32[2,256,128]{2,1,0:T(8,128)S(1)}, u32[]{:S(2)}, u32[]{:S(2)}) collective-permute-start(f32[2,256,128]{2,1,0:T(8,128)} %get-tuple-element.46), channel_id=1, source_target_pairs={{0,208},{16,192},{32,240},{48,224},{64,144},{80,128},{96,176},{112... | collective-permute-start | bytes 786440 | tf_op jit(solution)/shard_map/ppermute | solution.py:385
  299.4 31.5 %copy-start.11 = (f32[2,256,128]{2,1,0:T(8,128)}, f32[2,256,128]{2,1,0:T(8,128)S(1)}, u32[]{:S(2)}) copy-start(f32[2,256,128]{2,1,0:T(8,128)S(1)} %collective-permute-done.9.refs_9_) | copy-start | bytes 786436
  299.4 25.6 %collective-permute-start.14 = (f32[2,256,128]{2,1,0:T(8,128)}, f32[2,256,128]{2,1,0:T(8,128)}, u32[]{:S(2)}, u32[]{:S(2)}) collective-permute-start(f32[2,256,128]{2,1,0:T(8,128)} %get-tuple-element.47), channel_id=1, source_target_pairs={{0,224},{16,240},{32,192},{48,208},{64,160},{80,176},{96,128},{112... | collective-permute-start | bytes 786440 | tf_op jit(solution)/shard_map/ppermute | solution.py:385
  303.7 27.2 %copy-start.12 = (f32[2,256,128]{2,1,0:T(8,128)}, f32[2,256,128]{2,1,0:T(8,128)S(1)}, u32[]{:S(2)}) copy-start(f32[2,256,128]{2,1,0:T(8,128)S(1)} %collective-permute-done.10.refs_10_) | copy-start | bytes 786436
  303.7 27.1 %collective-permute-start.15 = (f32[2,256,128]{2,1,0:T(8,128)}, f32[2,256,128]{2,1,0:T(8,128)}, u32[]{:S(2)}, u32[]{:S(2)}) collective-permute-start(f32[2,256,128]{2,1,0:T(8,128)} %get-tuple-element.48), channel_id=1, source_target_pairs={{0,240},{16,224},{32,208},{48,192},{64,176},{80,160},{96,144},{112... | collective-permute-start | bytes 786440 | tf_op jit(solution)/shard_map/ppermute | solution.py:385
  (6 other events, 72.3 us)

commit v3 on v2

--- a/solution.py
+++ b/solution.py
@@ -14,7 +14,7 @@
 SLABS = 32
 INNER = 128
 ROWS = 32
-EARLY = 2
+EARLY = 1
 
 
 def split(values):
@@ -132,38 +132,47 @@
     y_ref[SLABS] = jnp.zeros((2 * ROWS, INNER), jnp.float32)
 
 
-def windows(offset_ref, y_ref, z0_ref, z1_ref):
+def windows(offset_ref, y_ref, z0_ref, za_ref, zb_ref):
     lanes = lax.broadcasted_iota(jnp.int32, (2 * ROWS, INNER), 1)
+    upper = pl.program_id(0) % 2
+    mine = lanes // (INNER // 2) == upper
 
     def window(step, carry):
-        for part in range(4):
-            dest = step * 4 + part
+        for part in range(2):
+            dest = step * 2 + part
             for block in range(2):
                 slab = 2 * dest + block
                 back = INNER - offset_ref[slab]
                 here = pltpu.roll(y_ref[slab], back, 1)
                 after = pltpu.roll(y_ref[slab + 1], back, 1)
-                shifted = jnp.where(lanes < back, here, after).reshape(2, ROWS, INNER)
-                if block:
-                    z1_ref[dest, 0] = shifted
+                gates = jnp.where(lanes < back, here, after)
+                if block == 0:
+                    z0_ref[dest, 0] = gates.reshape(2, ROWS, INNER)
                 else:
-                    z0_ref[dest] = shifted
-        return carry
-
-    lax.fori_loop(0, SLABS // 8, window, 0)
+                    other = pltpu.roll(gates, INNER // 2, 1)
+                    for z_ref, value in (
+                        (za_ref, jnp.where(upper == 0, gates, other)),
+                        (zb_ref, jnp.where(upper == 0, other, gates)),
+                    ):
+                        held = z_ref[dest].reshape(2 * ROWS, INNER)
+                        z_ref[dest] = jnp.where(mine, value, held).reshape(2, ROWS, INNER)
+        return carry
+
+    lax.fori_loop(0, SLABS // 4, window, 0)
 
 
 def early_kernel(x_ref, fwd_ref, inv_ref, tw_ref, chirp_ref, y_ref, mid_ref):
     compress(x_ref, fwd_ref, inv_ref, tw_ref, chirp_ref, mid_ref, y_ref.at[0])
 
 
-def window_kernel(offset_ref, y_ref, z0_ref, z1_ref):
-    windows(offset_ref, y_ref.at[0], z0_ref, z1_ref)
-
-
-def late_kernel(offset_ref, x_ref, fwd_ref, inv_ref, tw_ref, chirp_ref, other_ref, z0_ref, z1_ref, mid_ref, y_ref):
+def window_kernel(offset_ref, y_ref, z0_ref, za_ref, zb_ref):
+    windows(offset_ref, y_ref.at[0], z0_ref, za_ref, zb_ref)
+
+
+def late_kernel(offset_ref, x_ref, fwd_ref, inv_ref, tw_ref, chirp_ref, *refs):
+    z0_ref, za_ref, zb_ref, mid_ref, y_ref = refs[2:]
     compress(x_ref, fwd_ref, inv_ref, tw_ref, chirp_ref, mid_ref, y_ref)
-    windows(offset_ref, y_ref, z0_ref, z1_ref)
+    windows(offset_ref, y_ref, z0_ref, za_ref, zb_ref)
 
 
 def table_specs():
@@ -172,33 +181,31 @@
     return [whole, whole, table, table]
 
 
-def range_early(steps, echoes, tables):
-    gates = echoes.shape[3]
+def echo_spec(start, gates):
+    return pl.BlockSpec((1, 2, ROWS, gates), lambda i, *_: (0, 0, (i % 2) * (INNER // ROWS) + start + i // 2, 0))
+
+
+def range_early(tiles, echoes, tables):
     slabs = (SLABS + 1, 2 * ROWS, INNER)
     return pl.pallas_call(
         early_kernel,
-        grid=(steps,),
-        in_specs=[pl.BlockSpec((1, 2, ROWS, gates), lambda i: (0, 0, i, 0))] + table_specs(),
+        grid=(2 * tiles,),
+        in_specs=[echo_spec(0, echoes.shape[3])] + table_specs(),
         out_specs=pl.BlockSpec((1, *slabs), lambda i: (i, 0, 0, 0)),
-        out_shape=jax.ShapeDtypeStruct((steps, *slabs), jnp.float32),
+        out_shape=jax.ShapeDtypeStruct((2 * tiles, *slabs), jnp.float32),
         scratch_shapes=[pltpu.VMEM((SLABS, ROWS, 2 * INNER), jnp.float32)],
         name="range_early",
     )(echoes, *tables)
 
 
 def block_shapes(dests, rows):
-    return [
-        jax.ShapeDtypeStruct((dests, 2, rows, BLOCK), jnp.float32),
-        jax.ShapeDtypeStruct((dests, 2, 2, INNER, BLOCK), jnp.float32),
-    ]
+    part = jax.ShapeDtypeStruct((dests, 2, INNER, BLOCK), jnp.float32)
+    return [jax.ShapeDtypeStruct((dests, 2, 2, rows, BLOCK), jnp.float32), part, part]
 
 
 def block_specs(dests, start):
-    tiles = INNER // ROWS
-    return [
-        pl.BlockSpec((dests, 2, ROWS, BLOCK), lambda i, *_: (0, 0, i, 0)),
-        pl.BlockSpec((dests, 1, 2, ROWS, BLOCK), lambda i, *_: (0, (start + i) // tiles, 0, (start + i) % tiles, 0)),
-    ]
+    part = pl.BlockSpec((dests, 2, ROWS, BLOCK), lambda i, *_: (0, 0, start + i // 2, 0))
+    return [pl.BlockSpec((dests, 1, 2, ROWS, BLOCK), lambda i, *_: (0, i % 2, 0, i // 2, 0)), part, part]
 
 
 def range_window(offsets, early):
@@ -212,55 +219,55 @@
             in_specs=[pl.BlockSpec((1, slabs, 2 * ROWS, INNER), lambda i, *_: (i, 0, 0, 0))],
             out_specs=block_specs(dests, 0),
         ),
-        out_shape=block_shapes(dests, steps * ROWS),
+        out_shape=block_shapes(dests, steps // 2 * ROWS),
         name="range_window",
     )(offsets, early)
 
 
-def range_late(start, offsets, echoes, tables, other):
-    pulses, gates = echoes.shape[2], echoes.shape[3]
+def range_late(start, offsets, echoes, tables, parts):
+    gates = echoes.shape[3]
     dests = gates // (2 * BLOCK)
-    steps = pulses // ROWS - start
+    tiles = INNER // ROWS - start
     return pl.pallas_call(
         late_kernel,
         grid_spec=pltpu.PrefetchScalarGridSpec(
             num_scalar_prefetch=1,
-            grid=(steps,),
-            in_specs=[pl.BlockSpec((1, 2, ROWS, gates), lambda i, *_: (0, 0, start + i, 0))]
-            + table_specs()
-            + [pl.BlockSpec(memory_space=pl.ANY)],
+            grid=(2 * tiles,),
+            in_specs=[echo_spec(start, gates)] + table_specs() + [pl.BlockSpec(memory_space=pl.ANY)] * 2,
             out_specs=block_specs(dests, start),
             scratch_shapes=[
                 pltpu.VMEM((SLABS, ROWS, 2 * INNER), jnp.float32),
                 pltpu.VMEM((SLABS + 1, 2 * ROWS, INNER), jnp.float32),
             ],
         ),
-        out_shape=block_shapes(dests, steps * ROWS),
-        input_output_aliases={6: 1},
+        out_shape=block_shapes(dests, tiles * ROWS),
+        input_output_aliases={6: 1, 7: 2},
         name="range_late",
-    )(offsets, echoes, *tables, other)
-
-
-def azimuth_kernel(count, place_ref, *refs):
-    x_refs = refs[:count]
-    fwd_ref, inv_ref, tw_ref, gain_ref = refs[count : count + 4]
-    out_refs = refs[count + 4 : -4]
-    mid_ref, wide_ref, o_ref, sem = refs[-4:]
-
-    def slab(a, part, tile, upper):
-        start = pl.multiple_of(tile * 8, 8)
-        if count == 1:
-            return x_refs[0][a // 2, a % 2, part, pl.ds(start, 8), :]
-        rows = x_refs[0].shape[2]
-        if a % 2 == 0 and not upper:
-            return x_refs[0][a // 2, part, pl.ds(start, 8), :]
-        return x_refs[1][a // 2, part, pl.ds(pl.multiple_of(start + (a % 2) * INNER - rows, 8), 8), :]
-
-    def first(upper, tile, carry):
+    )(offsets, echoes, *tables, *parts)
+
+
+def hand_out(place_ref, o_ref, keep_ref, give_ref, sem):
+    core = jnp.bitwise_and(place_ref[0], 1)
+    copies = []
+    for block in range(o_ref.shape[0]):
+        source = o_ref.at[jnp.bitwise_xor(core, block)]
+        target = (keep_ref, give_ref)[block % 2].at[block // 2]
+        copies.append(pltpu.make_async_copy(source, target, sem.at[block]))
+    for copy in copies:
+        copy.start()
+    for copy in copies:
+        copy.wait()
+
+
+def azimuth_kernel(place_ref, early_ref, late_ref, fwd_ref, inv_ref, tw_ref, gain_ref, keep_ref, give_ref, mid_ref, wide_ref, o_ref, sem):
+    edge = early_ref.shape[3] // 8
+
+    def first(x_ref, base, tile, carry):
         start = pl.multiple_of(tile * 8, 8)
         rows = pl.ds(start, 8)
         lower = pl.ds(pl.multiple_of(INNER + tile * 8, 8), 8)
-        values = [(slab(a, 0, tile, upper), slab(a, 1, tile, upper)) for a in range(SLABS)]
+        here = pl.ds(pl.multiple_of((tile - base) * 8, 8), 8)
+        values = [(x_ref[a // 2, a % 2, 0, here, :], x_ref[a // 2, a % 2, 1, here, :]) for a in range(SLABS)]
         tr, ti = tw_ref[0, rows, :], tw_ref[1, rows, :]
         gr, gi = gain_ref[0, rows, :], gain_ref[1, rows, :]
         for k, (re, im) in enumerate(butterflies(values, -1)):
@@ -272,11 +279,8 @@
             wide_ref[k // 2, lower, lane] = jnp.broadcast_to(gi[:, k : k + 1], (8, INNER))
         return carry
 
-    tiles = INNER // 8
-    edge = x_refs[0].shape[2] // 8 if count == 2 else tiles
-    lax.fori_loop(0, edge, functools.partial(first, False), 0)
-    if edge < tiles:
-        lax.fori_loop(edge, tiles, functools.partial(first, True), 0)
+    lax.fori_loop(0, edge, functools.partial(first, early_ref, 0), 0)
+    lax.fori_loop(edge, INNER // 8, functools.partial(first, late_ref, edge), 0)
 
     def middle(step, carry):
         pairs = [2 * step, 2 * step + 1]
@@ -305,58 +309,179 @@
 
     lax.fori_loop(0, INNER // 8, last, 0)
 
-    place = place_ref[0]
-    blocks = o_ref.shape[0]
-    copies = []
-    for block in range(blocks):
-        source = o_ref.at[jnp.bitwise_xor(place, block)]
-        if len(out_refs) == blocks:
-            target = out_refs[block]
-        else:
-            source = o_ref.at[jnp.bitwise_xor(jnp.bitwise_and(place, 1), block)]
-            target = out_refs[block % 2].at[block // 2]
-        copies.append(pltpu.make_async_copy(source, target, sem.at[block]))
-    for copy in copies:
-        copy.start()
-    for copy in copies:
-        copy.wait()
-
-
-def azimuth_filter(outs, place, received, fwd, inv, gain):
+    hand_out(place_ref, o_ref, keep_ref, give_ref, sem)
+
+
+def narrow_kernel(place_ref, x_ref, fwd_ref, inv_ref, tw_ref, gain_ref, keep_ref, give_ref, mid_ref, o_ref, sem):
+    half = SLABS // 2
+    high = lax.broadcasted_iota(jnp.int32, (8, INNER), 1) >= INNER // 2
+    sign = jnp.where(high, -1.0, 1.0)
+
+    def turned(re, im, k, direction):
+        cosine = math.cos(2.0 * math.pi * k / SLABS)
+        sine = direction * math.sin(2.0 * math.pi * k / SLABS)
+        return times(re, im, jnp.where(high, cosine, 1.0), jnp.where(high, sine, 0.0))
+
+    def crossed(value):
+        return pltpu.roll(value, INNER // 2, 1) + sign * value
+
+    def place_of(k):
+        return k // 2, slice((k % 2) * INNER, (k % 2 + 1) * INNER)
+
+    def first(tile, carry):
+        rows = pl.ds(pl.multiple_of(tile * 8, 8), 8)
+        lower = pl.ds(pl.multiple_of(INNER + tile * 8, 8), 8)
+        values = [(x_ref[i, 0, rows, :], x_ref[i, 1, rows, :]) for i in range(half)]
+        for k, (re, im) in enumerate(butterflies(values, -1)):
+            pair, lane = place_of(k)
+            re, im = turned(re, im, k, -1)
+            re, im = times(crossed(re), crossed(im), tw_ref[pair, rows, lane], tw_ref[pair, lower, lane])
+            mid_ref[pair, rows, lane] = re
+            mid_ref[pair, lower, lane] = im
+        return carry
+
+    lax.fori_loop(0, INNER // 8, first, 0)
+
+    def middle(step, carry):
+        pairs = [2 * step, 2 * step + 1]
+        spectra = [dot3((inv_ref[0], inv_ref[1]), split(mid_ref[pair])) for pair in pairs]
+        for pair, spec in zip(pairs, spectra):
+            re, im = times(spec[:INNER], spec[INNER:], gain_ref[pair, :INNER, :], gain_ref[pair, INNER:, :])
+            mid_ref[pair] = dot3((fwd_ref[0], fwd_ref[1]), split(jnp.concatenate([re, im], axis=0)))
+        return carry
+
+    lax.fori_loop(0, half // 4, middle, 0)
+
+    def last(tile, carry):
+        rows = pl.ds(pl.multiple_of(tile * 8, 8), 8)
+        lower = pl.ds(pl.multiple_of(INNER + tile * 8, 8), 8)
+        values = []
+        for k in range(half):
+            pair, lane = place_of(k)
+            re, im = times(
+                mid_ref[pair, rows, lane], mid_ref[pair, lower, lane], tw_ref[pair, rows, lane], -tw_ref[pair, lower, lane]
+            )
+            values.append(turned(crossed(re), crossed(im), k, 1))
+        for i, (re, im) in enumerate(butterflies(values, 1)):
+            o_ref[i, 0, rows, :] = re
+            o_ref[i, 1, rows, :] = im
+        return carry
+
+    lax.fori_loop(0, INNER // 8, last, 0)
+    hand_out(place_ref, o_ref, keep_ref, give_ref, sem)
+
+
+def widen_kernel(tw_ref, gain_ref, tw_wide_ref, gain_wide_ref):
+    half = SLABS // 2
+    high = lax.broadcasted_iota(jnp.int32, (8, INNER), 1) >= INNER // 2
+
+    def spread(tile, carry):
+        rows = pl.ds(pl.multiple_of(tile * 8, 8), 8)
+        for source, target in ((tw_ref, tw_wide_ref), (gain_ref, gain_wide_ref)):
+            for part in range(2):
+                value = source[part, rows, :]
+                where = pl.ds(pl.multiple_of(part * INNER + tile * 8, 8), 8)
+                for k in range(half):
+                    lane = slice((k % 2) * INNER, (k % 2 + 1) * INNER)
+                    target[k // 2, where, lane] = jnp.where(high, value[:, k + half : k + half + 1], value[:, k : k + 1])
+        return carry
+
+    lax.fori_loop(0, INNER // 8, spread, 0)
+
+
+def azimuth_twiddles():
+    return jnp.asarray(twiddles().transpose(0, 2, 1))
+
+
+def widen(gain):
+    wide = jax.ShapeDtypeStruct((SLABS // 4, 2 * INNER, 2 * INNER), jnp.float32)
+    return pl.pallas_call(widen_kernel, out_shape=[wide, wide], name="widen")(azimuth_twiddles(), gain)
+
+
+def filter_call(kernel, place, operands, rows, pairs, extra):
     vmem = pl.BlockSpec(memory_space=pltpu.VMEM)
-    count = len(received)
-    devices = received[0].shape[0]
-    shape = (2, 2 * INNER, BLOCK)
-    each = shape if outs == devices else (devices // outs, *shape)
-    return pl.pallas_call(
-        functools.partial(azimuth_kernel, count),
-        in_specs=[pl.BlockSpec(memory_space=pltpu.SMEM)] + [vmem] * (count + 4),
-        out_specs=[pl.BlockSpec(memory_space=pl.ANY)] * outs,
-        out_shape=[jax.ShapeDtypeStruct(each, jnp.float32)] * outs,
-        scratch_shapes=[
-            pltpu.VMEM((SLABS // 2, 2 * INNER, 2 * INNER), jnp.float32),
-            pltpu.VMEM((SLABS // 2, 2 * INNER, 2 * INNER), jnp.float32),
-            pltpu.VMEM((devices, *shape), jnp.float32),
-            pltpu.SemaphoreType.DMA((devices,)),
-        ],
-        name="azimuth_filter",
-    )(place, *received, fwd, inv, jnp.asarray(twiddles().transpose(0, 2, 1)), gain)
-
-
-def migrate_kernel(count, *refs):
+    devices = operands[0].shape[0]
+    blocks = jax.ShapeDtypeStruct((devices // 2, 2, rows, BLOCK), jnp.float32)
+    mid = pltpu.VMEM((pairs, 2 * INNER, 2 * INNER), jnp.float32)
+    return pl.pallas_call(
+        kernel,
+        in_specs=[pl.BlockSpec(memory_space=pltpu.SMEM)] + [vmem] * len(operands),
+        out_specs=[pl.BlockSpec(memory_space=pl.ANY)] * 2,
+        out_shape=[blocks, blocks],
+        scratch_shapes=[mid] * (1 + extra)
+        + [pltpu.VMEM((devices, 2, rows, BLOCK), jnp.float32), pltpu.SemaphoreType.DMA((devices,))],
+    )(place, *operands)
+
+
+def azimuth_filter(place, early, late, fwd, inv, gain):
+    operands = (early, late, fwd, inv, azimuth_twiddles(), gain)
+    return filter_call(azimuth_kernel, place, operands, 2 * INNER, SLABS // 2, 1)
+
+
+def narrow_filter(place, received, fwd, inv, wide):
+    operands = (received, fwd, inv, *wide)
+    return filter_call(narrow_kernel, place, operands, INNER, SLABS // 4, 0)
+
+
+def pair_kernel(place_ref, keep_ref, other_ref, *out_refs):
+    chip = place_ref[0] // 2
+    for k, out_ref in enumerate(out_refs):
+        block = jnp.bitwise_xor(chip, k)
+        out_ref[...] = keep_ref[block] + other_ref[block]
+
+
+def pair_add(place, keep, other):
+    vmem = pl.BlockSpec(memory_space=pltpu.VMEM)
+    chips, *block = keep.shape
+    return pl.pallas_call(
+        pair_kernel,
+        in_specs=[pl.BlockSpec(memory_space=pltpu.SMEM), vmem, vmem],
+        out_specs=[vmem] * chips,
+        out_shape=[jax.ShapeDtypeStruct(tuple(block), jnp.float32)] * chips,
+        name="pair_add",
+    )(place, keep, other)
+
+
+def settle_kernel(*refs):
     total = refs[0][...]
-    if count == 1:
-        total = jnp.sum(total, axis=0)
-    for ref in refs[1:count]:
+    for ref in refs[1:-1]:
         total = total + ref[...]
-    moved = jnp.dot(
-        total.reshape(-1, BLOCK), refs[count][0], precision=lax.Precision.HIGHEST, preferred_element_type=jnp.float32
-    )
-    refs[-1][...] = moved.reshape(2, -1, BLOCK)
-
-
-def migrate(block, parts, kernel, other=None):
-    pulses = parts[0].shape[-2]
+    refs[-1][...] = total
+
+
+def settle(parts):
+    return pl.pallas_call(
+        settle_kernel, out_shape=jax.ShapeDtypeStruct(parts[0].shape, jnp.float32), name="settle"
+    )(*parts)
+
+
+def exact_dot(left, right):
+    return jnp.dot(left, right, precision=lax.Precision.HIGHEST, preferred_element_type=jnp.float32)
+
+
+def migrate_kernel(*refs):
+    total = refs[0][...]
+    for ref in refs[1:-2]:
+        total = total + ref[...]
+    refs[-1][...] = exact_dot(total.reshape(-1, BLOCK), refs[-2][0]).reshape(2, -1, BLOCK)
+
+
+def migrate_last_kernel(a_ref, b_ref, kernel_ref, other_ref, o_ref):
+    low = lax.broadcasted_iota(jnp.int32, (INNER, BLOCK), 1) < BLOCK // 2
+    for part in range(2):
+        first = a_ref[part]
+        second = b_ref[0, part]
+        for device in range(1, b_ref.shape[0]):
+            second = second + b_ref[device, part]
+        rows = (
+            jnp.where(low, first, pltpu.roll(second, BLOCK // 2, 1)),
+            jnp.where(low, pltpu.roll(first, BLOCK // 2, 1), second),
+        )
+        for half in range(2):
+            o_ref[part, half * INNER : (half + 1) * INNER, :] = exact_dot(rows[half], kernel_ref[0])
+
+
+def migrate(block, kernel_body, parts, kernel, pulses, other=None):
     args = [*parts, kernel]
     in_specs = [pl.BlockSpec(part.shape, lambda i, n=part.ndim: (0,) * n) for part in parts]
     in_specs.append(pl.BlockSpec((1, BLOCK, BLOCK), lambda i: (block, 0, 0)))
@@ -366,7 +491,7 @@
         aliases = {len(args): 0}
         args.append(other)
     return pl.pallas_call(
-        functools.partial(migrate_kernel, len(parts)),
+        kernel_body,
         grid=(1,),
         in_specs=in_specs,
         out_specs=pl.BlockSpec((2, pulses, BLOCK), lambda i: (0, 0, block)),
@@ -397,8 +522,8 @@
     chirp = jnp.stack([jnp.cos(by_slab), jnp.sin(by_slab)]) * (1.0 / gates)
     tables = (fwd, inv, jnp.asarray(twiddles()), chirp)
     compressed = range_early(EARLY, echoes, tables)
-    early, partial = range_window(offsets, compressed)
-    late, full = range_late(EARLY, offsets, echoes, tables, partial)
+    early, *parts = range_window(offsets, compressed)
+    late, part_a, part_b = range_late(EARLY, offsets, echoes, tables, parts)
 
     table_count = weight_table.shape[1]
     entry_ids = lax.broadcasted_iota(jnp.int32, (weight_index.shape[1], table_count), 1)
@@ -411,17 +536,25 @@
 
     early = turn(early, "pulse")
     late = turn(late, "pulse")
-    full = turn(full, "pulse")
+    part_a = turn(part_a, "pulse")
+    part_b = turn(part_b, "pulse")
     place = lax.axis_index("chan").astype(jnp.int32).reshape(1)
     channels = lax.axis_size("chan")
-    first = azimuth_filter(channels, place, [early, late], fwd, inv, gain[:, 0])
-    first = [first[0]] + [swap(first[k], k) for k in range(1, channels)]
-    image = migrate(0, first, rcmc_kernel)
-    keep, give = azimuth_filter(2, place, [full], fwd, inv, gain[:, 1])
+    rows = pulses // channels
+    wide = widen(gain[:, 1])
+    keep, give = azimuth_filter(place, early, late, fwd, inv, gain[:, 0])
+    first = pair_add(place, keep, swap(give, 1))
+    first = [first[0]] + [swap(first[k], 2 * k) for k in range(1, channels // 2)]
+    image = migrate(0, migrate_kernel, first, rcmc_kernel, rows)
+    keep, give = narrow_filter(place, part_a, fwd, inv, wide)
+    sum_a = pair_add(place, keep, swap(give, 1))
+    sum_a = [sum_a[0]] + [swap(sum_a[k], 2 * k) for k in range(1, channels // 2)]
+    sum_a = settle(sum_a)
+    keep, give = narrow_filter(place, part_b, fwd, inv, wide)
     pair = keep + swap(give, 1)
     groups = [list(range(core, channels, 2)) for core in range(2)]
-    second = turn(pair, "chan", groups)
-    return migrate(1, [second], rcmc_kernel, image)
+    sum_b = turn(pair, "chan", groups)
+    return migrate(1, migrate_last_kernel, [sum_a, sum_b], rcmc_kernel, rows, image)
 
 
 def solution(mesh):

time: 341 us -> 341 us (level)
  waiting for transfers between devices: 93.7 us -> 24.3 us
  blocking collectives: 101 us -> 134 us
  Pallas kernels: 76.8 us -> 103 us
  starting transfers between devices: 55.3 us -> 61.8 us
  local copies, waits for them, and re-layouts: 4.35 us -> 9.8 us
    all_to_all x4, waiting for transfers between devices: 44 us -> 5.41 us  [turn(): lax.all_to_all(blocks, axis, split_axis=0, concat_axis=0, tiled=True, axi...]
    all_to_all x1 -> x2, blocking collectives: 101 us -> 134 us  [turn(): lax.all_to_all(blocks, axis, split_axis=0, concat_axis=0, tiled=True, axi...]
    ppermute x16 -> x17, waiting for transfers between devices: 49.7 us -> 18.9 us  [swap(): return lax.ppermute(block, 'chan', [(i, i ^ distance) for i in devices])]
    pallas_call x5 -> x10, Pallas kernels: 50.8 us -> 71 us  [the longest x3 43.3 us: filter_call(): pl.pallas_call(kernel, in_specs=[pl.BlockSpec(memory_space=pltpu.SMEM)] +...]
    ppermute x16 -> x17, starting transfers between devices: 21.8 us -> 28.2 us  [swap(): return lax.ppermute(block, 'chan', [(i, i ^ distance) for i in devices])]
    unnamed x36 -> x52, local copies, waits for them, and re-layouts: 0.07 us -> 5.57 us
    pallas_call x1, Pallas kernels: 21.4 us -> 26.1 us  [range_late(): pl.pallas_call(late_kernel, grid_spec=pltpu.PrefetchScalarGridSpec(num_sc...]
  transfers between devices with their start and end apart: 20 -> 21, of which waited for: 13 -> 8; matrix products, arithmetic and copies ran while one was open for 2% -> 2% of each run, Pallas kernels for 21% -> 28%
where the time goes in v3:
time: 341 us; the launch traced here: 338 us
  blocking collectives  134 us (39%)
  Pallas kernels  103 us (30%)
  starting transfers between devices  61.8 us (18%)
  waiting for transfers between devices  24.3 us (7%)
  local copies, waits for them, and re-layouts  9.8 us (3%)
  other arithmetic  4.38 us (1%)
    all_to_all x2, blocking collectives, turn(): lax.all_to_all(blocks, axis, split_axis=0, concat_axis=0, tiled=True, axi...  134 us
    pallas_call x3, Pallas kernels, filter_call(): pl.pallas_call(kernel, in_specs=[pl.BlockSpec(memory_space=pltpu.SMEM)] +...  43.3 us
    all_to_all x4, starting transfers between devices, turn(): lax.all_to_all(blocks, axis, split_axis=0, concat_axis=0, tiled=True, axi...  33.6 us
    ppermute x17, starting transfers between devices, swap(): return lax.ppermute(block, 'chan', [(i, i ^ distance) for i in devices])  28.2 us
    pallas_call x1, Pallas kernels, range_late(): pl.pallas_call(late_kernel, grid_spec=pltpu.PrefetchScalarGridSpec(num_sc...  26.1 us
    ppermute x17, waiting for transfers between devices, swap(): return lax.ppermute(block, 'chan', [(i, i ^ distance) for i in devices])  18.9 us
    pallas_call x1, Pallas kernels, widen(): pl.pallas_call(widen_kernel, out_shape=[wide, wide], name='widen')  7.6 us
  transfers between devices with their start and end apart: 21, of which 8 were waited for; matrix products, arithmetic and copies ran while one was open for 2% of the time, Pallas kernels for 28%

profile of v3, /device:TPU:4, one launch (start us, length us, event | category | flops | bytes accessed | tf_op | source)
XLA Modules:
  0.0 337.8 jit_solution(8412647009212185291)
XLA Ops:
  1.3 11.4 %all-to-all-start = ((s32[16,1,2]{2,1,0:T(1,128)}), s32[16,1,2]{2,1,0:T(1,128)S(1)}, u32[]{:S(2)}, u32[]{:S(2)}) async-start(s32[16,1,2]{2,1,0:T(1,128)} %broadcast_in_dim.12), calls=%async_computation | async-start | bytes 16384 | tf_op jit(solution)/shard_map/all_to_all | solution.py:505
  14.5 6.8 %range_early.1.y_ref = f32[2,33,64,128]{3,2,1,0:T(8,128)} custom-call(f32[1,2,256,4096]{3,2,1,0:T(8,128)} %x_ref.3, bf16[2,256,256]{2,1,0:T(8,128)(2,1)} %constant.16.clone.fwd_ref, bf16[2,256,256]{2,1,0:T(8,128)(2,1)} %constant.17.clone.inv_ref, f32[2,32,128]{2,1,0:T(8,128)} %constant.18.clone.tw_ref, f32[2,32,128]{2,1,0:T(8,128)} %maximum_multiply_fusion.chirp_ref), custom_call_target="tpu_custom_call" | custom-call | tf_op jit(solution)/shard_map/range_early/pallas_call | solution.py:190
  22.9 6.3 %range_window.1 = (f32[16,2,2,32,128]{4,3,2,1,0:T(8,128)}, f32[16,2,128,128]{3,2,1,0:T(8,128)}, f32[16,2,128,128]{3,2,1,0:T(8,128)}) custom-call(s32[32]{0:T(128)} %reshape.30.offset_ref, f32[2,33,64,128]{3,2,1,0:T(8,128)} %range_early.1.y_ref), custom_call_target="tpu_custom_call" | custom-call | tf_op jit(solution)/shard_map/range_window/pallas_call | solution.py:214
  29.2 9.6 %all-to-all-start.4 = ((f32[16,2,2,32,128]{4,3,2,1,0:T(8,128)}), f32[16,2,2,32,128]{4,3,2,1,0:T(8,128)S(1)}, u32[]{:S(2)}, u32[]{:S(2)}) async-start(f32[16,2,2,32,128]{4,3,2,1,0:T(8,128)} %get-tuple-element.53), calls=%async_computation.4 | async-start | bytes 2097152 | tf_op jit(solution)/shard_map/all_to_all | solution.py:505
  38.8 26.1 %range_late.1 = (f32[16,2,2,96,128]{4,3,2,1,0:T(8,128)}, f32[16,2,128,128]{3,2,1,0:T(8,128)}, f32[16,2,128,128]{3,2,1,0:T(8,128)}) custom-call(s32[32]{0:T(128)} %reshape.30.offset_ref, f32[1,2,256,4096]{3,2,1,0:T(8,128)} %x_ref.3, bf16[2,256,256]{2,1,0:T(8,128)(2,1)} %constant.16.clone.fwd_ref, ...), custom_call_target="tpu_custom_call", output_to_operand_aliasing={{1}: (6, {}), {2}: (7, {})} | custom-call | tf_op jit(solution)/shard_map/range_late/pallas_call | solution.py:231
  65.0 57.1 %all_to_all.31.x_ref = f32[16,2,128,128]{3,2,1,0:T(8,128)} all-to-all(f32[16,2,128,128]{3,2,1,0:T(8,128)} %get-tuple-element.50), channel_id=1, replica_groups=mesh['chan'=16,'pulse'=16] {'pulse'}, dimensions={0} | all-to-all | bytes 4194304 | tf_op jit(solution)/shard_map/all_to_all | solution.py:505
  122.1 76.7 %all_to_all.32.late_ref = f32[16,2,2,96,128]{4,3,2,1,0:T(8,128)} all-to-all(f32[16,2,2,96,128]{4,3,2,1,0:T(8,128)S(1)} %copy-done.4), channel_id=1, replica_groups=mesh['chan'=16,'pulse'=16] {'pulse'}, dimensions={0} | all-to-all | bytes 6291456 | tf_op jit(solution)/shard_map/all_to_all | solution.py:505
  198.7 7.4 %all-to-all-start.1 = ((f32[16,2,128,128]{3,2,1,0:T(8,128)}), f32[16,2,128,128]{3,2,1,0:T(8,128)S(1)}, u32[]{:S(2)}, u32[]{:S(2)}) async-start(f32[16,2,128,128]{3,2,1,0:T(8,128)} %get-tuple-element.37), calls=%async_computation.1 | async-start | bytes 4194304 | tf_op jit(solution)/shard_map/all_to_all | solution.py:505
  207.9 19.0 %shard_map.120 = (f32[8,2,256,128]{3,2,1,0:T(8,128)}, f32[8,2,256,128]{3,2,1,0:T(8,128)}) custom-call(s32[1]{0:T(128)} %bitcast.place_ref, f32[16,2,2,32,128]{4,3,2,1,0:T(8,128)} %copy-done.2, f32[16,2,2,96,128]{4,3,2,1,0:T(8,128)} %all_to_all.32.late_ref, bf16[2,256,256]{2,1,0:T(8,128)(2,1)} %constant.16.clone.fwd_ref, ...), custom_call_target="tpu_custom_call" | custom-call | tf_op jit(solution)/shard_map/pallas_call | solution.py:406
  227.0 7.6 %widen.1 = (f32[8,256,256]{2,1,0:T(8,128)}, f32[8,256,256]{2,1,0:T(8,128)}) custom-call(f32[2,128,32]{2,1,0:T(8,128)} %constant.19.clone.tw_ref, f32[2,128,32]{2,1,0:T(8,128)} %get-tuple-element.66.gain_ref), custom_call_target="tpu_custom_call" | custom-call | tf_op jit(solution)/shard_map/widen/pallas_call | solution.py:398
  234.6 12.1 %shard_map.119 = (f32[8,2,128,128]{3,2,1,0:T(8,128)}, f32[8,2,128,128]{3,2,1,0:T(8,128)}) custom-call(s32[1]{0:T(128)} %bitcast.place_ref, f32[16,2,128,128]{3,2,1,0:T(8,128)} %all_to_all.31.x_ref, bf16[2,256,256]{2,1,0:T(8,128)(2,1)} %constant.16.clone.fwd_ref, bf16[2,256,256]{2,1,0:T(8,128)(2,1)} %constant.17.clone.inv_ref, ...), custom_call_target="tpu_custom_call" | custom-call | tf_op jit(solution)/shard_map/pallas_call | solution.py:406
  247.4 5.4 %all-to-all-done.1.x_ref = f32[16,2,128,128]{3,2,1,0:T(8,128)S(1)} async-done(((f32[16,2,128,128]{3,2,1,0:T(8,128)}), f32[16,2,128,128]{3,2,1,0:T(8,128)S(1)}, u32[]{:S(2)}, u32[]{:S(2)}) %all-to-all-start.1) | async-done | bytes 2097184 | tf_op jit(solution)/shard_map/all_to_all | solution.py:505
  254.2 12.1 %shard_map.118 = (f32[8,2,128,128]{3,2,1,0:T(8,128)}, f32[8,2,128,128]{3,2,1,0:T(8,128)}) custom-call(s32[1]{0:T(128)} %bitcast.place_ref, f32[16,2,128,128]{3,2,1,0:T(8,128)} %copy-done.1, bf16[2,256,256]{2,1,0:T(8,128)(2,1)} %constant.16.clone.fwd_ref, bf16[2,256,256]{2,1,0:T(8,128)(2,1)} %constant.17.clone.inv_ref, ...), custom_call_target="tpu_custom_call" | custom-call | tf_op jit(solution)/shard_map/pallas_call | solution.py:406
  266.5 2.4 add.11
  268.9 5.1 %all-to-all-start.3 = ((f32[8,2,128,128]{3,2,1,0:T(8,128)}), f32[8,2,128,128]{3,2,1,0:T(8,128)S(1)}, u32[]{:S(2)}, u32[]{:S(2)}) async-start(f32[8,2,128,128]{3,2,1,0:T(8,128)} %add.11), calls=%async_computation.3 | async-start | bytes 2097152 | tf_op jit(solution)/shard_map/all_to_all | solution.py:505
  275.0 2.6 pair_add.2
  277.7 2.0 collective-permute-start.1
  279.7 2.7 collective-permute-start.2
  284.4 3.8 %pair_add.3 = (f32[2,256,128]{2,1,0:T(8,128)}, f32[2,256,128]{2,1,0:T(8,128)}, f32[2,256,128]{2,1,0:T(8,128)}, f32[2,256,128]{2,1,0:T(8,128)}, f32[2,256,128]{2,...) custom-call(s32[1]{0:T(128)} %bitcast.place_ref, ...), custom_call_target="tpu_custom_call" | custom-call | tf_op jit(solution)/shard_map/pair_add/pallas_call | solution.py:436
  288.4 3.3 collective-permute-done.1.refs_1_
  291.8 2.7 collective-permute-start.11
  296.9 2.8 collective-permute-start.6
  299.7 3.1 collective-permute-start.7
  304.1 3.1 collective-permute-done.6.refs_6_
  311.0 3.7 %collective-permute-start.15 = (f32[2,256,128]{2,1,0:T(8,128)}, f32[2,256,128]{2,1,0:T(8,128)S(1)}, u32[]{:S(2)}, u32[]{:S(2)}) collective-permute-start(f32[2,256,128]{2,1,0:T(8,128)} %get-tuple-element.63), channel_id=1, source_target_pairs={{0,192},{16,208},{32,224},{48,240},{64,128},{80,144},{96,160},{112... | collective-permute-start | bytes 786440 | tf_op jit(solution)/shard_map/ppermute | solution.py:510
  314.8 4.2 %collective-permute-start.16 = (f32[2,256,128]{2,1,0:T(8,128)}, f32[2,256,128]{2,1,0:T(8,128)S(1)}, u32[]{:S(2)}, u32[]{:S(2)}) collective-permute-start(f32[2,256,128]{2,1,0:T(8,128)} %get-tuple-element.64), channel_id=1, source_target_pairs={{0,224},{16,240},{32,192},{48,208},{64,160},{80,176},{96,128},{112... | collective-permute-start | bytes 786440 | tf_op jit(solution)/shard_map/ppermute | solution.py:510
  319.0 2.0 settle.1.a_ref
  321.0 2.2 collective-permute-done.14.refs_5_
  323.2 5.5 %collective-permute-done.15.refs_6_ = f32[2,256,128]{2,1,0:T(8,128)S(1)} collective-permute-done((f32[2,256,128]{2,1,0:T(8,128)}, f32[2,256,128]{2,1,0:T(8,128)S(1)}, u32[]{:S(2)}, u32[]{:S(2)}) %collective-permute-start.15) | collective-permute-done | bytes 262176 | tf_op jit(solution)/shard_map/ppermute | solution.py:510
  328.6 2.5 collective-permute-done.16.refs_7_
  331.9 2.6 migrate.2.other_ref
  335.5 2.3 migrate.3
  (95 shorter events, 21.3 us)
Async XLA Ops:
  0.0 206.2 %copy-start = (f32[2,64]{1,0:T(2,128)S(1)}, f32[2,64]{1,0:T(2,128)}, u32[]{:S(2)}) copy-start(f32[2,64]{1,0:T(2,128)} %param.17) | copy-start | bytes 1540
  1.3 20.0 %all-to-all-start = ((s32[16,1,2]{2,1,0:T(1,128)}), s32[16,1,2]{2,1,0:T(1,128)S(1)}, u32[]{:S(2)}, u32[]{:S(2)}) async-start(s32[16,1,2]{2,1,0:T(1,128)} %broadcast_in_dim.12), calls=%async_computation | async-start | bytes 16384 | tf_op jit(solution)/shard_map/all_to_all | solution.py:505
  29.2 35.8 %all-to-all-start.4 = ((f32[16,2,2,32,128]{4,3,2,1,0:T(8,128)}), f32[16,2,2,32,128]{4,3,2,1,0:T(8,128)S(1)}, u32[]{:S(2)}, u32[]{:S(2)}) async-start(f32[16,2,2,32,128]{4,3,2,1,0:T(8,128)} %get-tuple-element.53), calls=%async_computation.4 | async-start | bytes 2097152 | tf_op jit(solution)/shard_map/all_to_all | solution.py:505
  65.0 57.1 %copy-start.2 = (f32[16,2,2,32,128]{4,3,2,1,0:T(8,128)}, f32[16,2,2,32,128]{4,3,2,1,0:T(8,128)S(1)}, u32[]{:S(2)}) copy-start(f32[16,2,2,32,128]{4,3,2,1,0:T(8,128)S(1)} %all-to-all-done.4.early_ref) | copy-start | bytes 3145732
  65.0 57.1 %copy-start.4 = (f32[16,2,2,96,128]{4,3,2,1,0:T(8,128)S(1)}, f32[16,2,2,96,128]{4,3,2,1,0:T(8,128)}, u32[]{:S(2)}) copy-start(f32[16,2,2,96,128]{4,3,2,1,0:T(8,128)} %get-tuple-element.54) | copy-start | bytes 9437188
  198.7 54.1 %all-to-all-start.1 = ((f32[16,2,128,128]{3,2,1,0:T(8,128)}), f32[16,2,128,128]{3,2,1,0:T(8,128)S(1)}, u32[]{:S(2)}, u32[]{:S(2)}) async-start(f32[16,2,128,128]{3,2,1,0:T(8,128)} %get-tuple-element.37), calls=%async_computation.1 | async-start | bytes 4194304 | tf_op jit(solution)/shard_map/all_to_all | solution.py:505
  226.9 57.4 %collective-permute-start.9 = (f32[8,2,256,128]{3,2,1,0:T(8,128)}, f32[8,2,256,128]{3,2,1,0:T(8,128)}, u32[]{:S(2)}, u32[]{:S(2)}) collective-permute-start(f32[8,2,256,128]{3,2,1,0:T(8,128)} %get-tuple-element.56), channel_id=1, source_target_pairs={{0,16},{16,0},{32,48},{48,32},{64,80},{80,64},{96,112},{112,96},{1... | collective-permute-start | bytes 6291464 | tf_op jit(solution)/shard_map/ppermute | solution.py:510
  246.8 19.7 %copy-start.5 = (f32[8,2,128,128]{3,2,1,0:T(8,128)S(1)}, f32[8,2,128,128]{3,2,1,0:T(8,128)}, u32[]{:S(2)}) copy-start(f32[8,2,128,128]{3,2,1,0:T(8,128)} %get-tuple-element.51) | copy-start | bytes 3145732
  246.8 19.6 %collective-permute-start.8 = (f32[8,2,128,128]{3,2,1,0:T(8,128)}, f32[8,2,128,128]{3,2,1,0:T(8,128)}, u32[]{:S(2)}, u32[]{:S(2)}) collective-permute-start(f32[8,2,128,128]{3,2,1,0:T(8,128)} %get-tuple-element.52), channel_id=1, source_target_pairs={{0,16},{16,0},{32,48},{48,32},{64,80},{80,64},{96,112},{112,96},{1... | collective-permute-start | bytes 3145736 | tf_op jit(solution)/shard_map/ppermute | solution.py:510
  266.4 7.6 %collective-permute-start = (f32[8,2,128,128]{3,2,1,0:T(8,128)}, f32[8,2,128,128]{3,2,1,0:T(8,128)S(1)}, u32[]{:S(2)}, u32[]{:S(2)}) collective-permute-start(f32[8,2,128,128]{3,2,1,0:T(8,128)} %get-tuple-element.41), channel_id=1, source_target_pairs={{0,16},{16,0},{32,48},{48,32},{64,80},{80,64},{96,112},{112,96},{1... | collective-permute-start | bytes 3145736 | tf_op jit(solution)/shard_map/ppermute | solution.py:510
  268.9 65.6 %all-to-all-start.3 = ((f32[8,2,128,128]{3,2,1,0:T(8,128)}), f32[8,2,128,128]{3,2,1,0:T(8,128)S(1)}, u32[]{:S(2)}, u32[]{:S(2)}) async-start(f32[8,2,128,128]{3,2,1,0:T(8,128)} %add.11), calls=%async_computation.3 | async-start | bytes 2097152 | tf_op jit(solution)/shard_map/all_to_all | solution.py:505
  277.7 14.1 %collective-permute-start.1 = (f32[2,128,128]{2,1,0:T(8,128)}, f32[2,128,128]{2,1,0:T(8,128)S(1)}, u32[]{:S(2)}, u32[]{:S(2)}) collective-permute-start(f32[2,128,128]{2,1,0:T(8,128)} %get-tuple-element.43), channel_id=1, source_target_pairs={{0,32},{16,48},{32,0},{48,16},{64,96},{80,112},{96,64},{112,80},{1... | collective-permute-start | bytes 393224 | tf_op jit(solution)/shard_map/ppermute | solution.py:510
  279.7 16.5 %collective-permute-start.2 = (f32[2,128,128]{2,1,0:T(8,128)}, f32[2,128,128]{2,1,0:T(8,128)S(1)}, u32[]{:S(2)}, u32[]{:S(2)}) collective-permute-start(f32[2,128,128]{2,1,0:T(8,128)} %get-tuple-element.44), channel_id=1, source_target_pairs={{0,64},{16,80},{32,96},{48,112},{64,0},{80,16},{96,32},{112,48},{1... | collective-permute-start | bytes 393224 | tf_op jit(solution)/shard_map/ppermute | solution.py:510
  282.3 14.6 %collective-permute-start.3 = (f32[2,128,128]{2,1,0:T(8,128)}, f32[2,128,128]{2,1,0:T(8,128)S(1)}, u32[]{:S(2)}, u32[]{:S(2)}) collective-permute-start(f32[2,128,128]{2,1,0:T(8,128)} %get-tuple-element.45), channel_id=1, source_target_pairs={{0,96},{16,112},{32,64},{48,80},{64,32},{80,48},{96,0},{112,16},{1... | collective-permute-start | bytes 393224 | tf_op jit(solution)/shard_map/ppermute | solution.py:510
  282.4 17.3 %collective-permute-start.4 = (f32[2,128,128]{2,1,0:T(8,128)}, f32[2,128,128]{2,1,0:T(8,128)S(1)}, u32[]{:S(2)}, u32[]{:S(2)}) collective-permute-start(f32[2,128,128]{2,1,0:T(8,128)} %get-tuple-element.46), channel_id=1, source_target_pairs={{0,128},{16,144},{32,160},{48,176},{64,192},{80,208},{96,224},{112... | collective-permute-start | bytes 393224 | tf_op jit(solution)/shard_map/ppermute | solution.py:510
  288.2 22.8 %collective-permute-start.10 = (f32[2,256,128]{2,1,0:T(8,128)}, f32[2,256,128]{2,1,0:T(8,128)S(1)}, u32[]{:S(2)}, u32[]{:S(2)}) collective-permute-start(f32[2,256,128]{2,1,0:T(8,128)} %get-tuple-element.58), channel_id=1, source_target_pairs={{0,32},{16,48},{32,0},{48,16},{64,96},{80,112},{96,64},{112,80},{1... | collective-permute-start | bytes 786440 | tf_op jit(solution)/shard_map/ppermute | solution.py:510
  291.8 27.2 %copy-start.14 = (f32[2,128,128]{2,1,0:T(8,128)}, f32[2,128,128]{2,1,0:T(8,128)S(1)}, u32[]{:S(2)}) copy-start(f32[2,128,128]{2,1,0:T(8,128)S(1)} %collective-permute-done.1.refs_1_) | copy-start | bytes 393220
  291.8 23.0 %collective-permute-start.11 = (f32[2,256,128]{2,1,0:T(8,128)}, f32[2,256,128]{2,1,0:T(8,128)S(1)}, u32[]{:S(2)}, u32[]{:S(2)}) collective-permute-start(f32[2,256,128]{2,1,0:T(8,128)} %get-tuple-element.59), channel_id=1, source_target_pairs={{0,64},{16,80},{32,96},{48,112},{64,0},{80,16},{96,32},{112,48},{1... | collective-permute-start | bytes 786440 | tf_op jit(solution)/shard_map/ppermute | solution.py:510
  296.1 22.8 %copy-start.15 = (f32[2,128,128]{2,1,0:T(8,128)}, f32[2,128,128]{2,1,0:T(8,128)S(1)}, u32[]{:S(2)}) copy-start(f32[2,128,128]{2,1,0:T(8,128)S(1)} %collective-permute-done.2.refs_2_) | copy-start | bytes 393220
  296.1 7.3 %collective-permute-start.5 = (f32[2,128,128]{2,1,0:T(8,128)S(1)}, f32[2,128,128]{2,1,0:T(8,128)S(1)}, u32[]{:S(2)}, u32[]{:S(2)}) collective-permute-start(f32[2,128,128]{2,1,0:T(8,128)S(1)} %copy-done.24), channel_id=1, source_target_pairs={{0,160},{16,176},{32,128},{48,144},{64,224},{80,240},{96,192},{112... | collective-permute-start | bytes 393224 | tf_op jit(solution)/shard_map/ppermute | solution.py:510
  296.9 22.1 %copy-start.16 = (f32[2,128,128]{2,1,0:T(8,128)}, f32[2,128,128]{2,1,0:T(8,128)S(1)}, u32[]{:S(2)}) copy-start(f32[2,128,128]{2,1,0:T(8,128)S(1)} %collective-permute-done.3.refs_3_) | copy-start | bytes 393220
  296.9 10.3 %collective-permute-start.6 = (f32[2,128,128]{2,1,0:T(8,128)S(1)}, f32[2,128,128]{2,1,0:T(8,128)S(1)}, u32[]{:S(2)}, u32[]{:S(2)}) collective-permute-start(f32[2,128,128]{2,1,0:T(8,128)S(1)} %copy-done.23), channel_id=1, source_target_pairs={{0,192},{16,208},{32,224},{48,240},{64,128},{80,144},{96,160},{112... | collective-permute-start | bytes 393224 | tf_op jit(solution)/shard_map/ppermute | solution.py:510
  299.7 19.3 %copy-start.17 = (f32[2,128,128]{2,1,0:T(8,128)}, f32[2,128,128]{2,1,0:T(8,128)S(1)}, u32[]{:S(2)}) copy-start(f32[2,128,128]{2,1,0:T(8,128)S(1)} %collective-permute-done.4.refs_4_) | copy-start | bytes 393220
  299.7 9.3 %collective-permute-start.7 = (f32[2,128,128]{2,1,0:T(8,128)S(1)}, f32[2,128,128]{2,1,0:T(8,128)S(1)}, u32[]{:S(2)}, u32[]{:S(2)}) collective-permute-start(f32[2,128,128]{2,1,0:T(8,128)S(1)} %copy-done.22), channel_id=1, source_target_pairs={{0,224},{16,240},{32,192},{48,208},{64,160},{80,176},{96,128},{112... | collective-permute-start | bytes 393224 | tf_op jit(solution)/shard_map/ppermute | solution.py:510
  303.4 15.6 %copy-start.18 = (f32[2,128,128]{2,1,0:T(8,128)}, f32[2,128,128]{2,1,0:T(8,128)S(1)}, u32[]{:S(2)}) copy-start(f32[2,128,128]{2,1,0:T(8,128)S(1)} %collective-permute-done.5.refs_5_) | copy-start | bytes 393220
  303.4 17.6 %collective-permute-start.12 = (f32[2,256,128]{2,1,0:T(8,128)}, f32[2,256,128]{2,1,0:T(8,128)S(1)}, u32[]{:S(2)}, u32[]{:S(2)}) collective-permute-start(f32[2,256,128]{2,1,0:T(8,128)} %get-tuple-element.60), channel_id=1, source_target_pairs={{0,96},{16,112},{32,64},{48,80},{64,32},{80,48},{96,0},{112,16},{1... | collective-permute-start | bytes 786440 | tf_op jit(solution)/shard_map/ppermute | solution.py:510
  307.9 13.1 %collective-permute-start.13 = (f32[2,256,128]{2,1,0:T(8,128)}, f32[2,256,128]{2,1,0:T(8,128)S(1)}, u32[]{:S(2)}, u32[]{:S(2)}) collective-permute-start(f32[2,256,128]{2,1,0:T(8,128)} %get-tuple-element.61), channel_id=1, source_target_pairs={{0,128},{16,144},{32,160},{48,176},{64,192},{80,208},{96,224},{112... | collective-permute-start | bytes 786440 | tf_op jit(solution)/shard_map/ppermute | solution.py:510
  309.7 13.5 %collective-permute-start.14 = (f32[2,256,128]{2,1,0:T(8,128)}, f32[2,256,128]{2,1,0:T(8,128)S(1)}, u32[]{:S(2)}, u32[]{:S(2)}) collective-permute-start(f32[2,256,128]{2,1,0:T(8,128)} %get-tuple-element.62), channel_id=1, source_target_pairs={{0,160},{16,176},{32,128},{48,144},{64,224},{80,240},{96,192},{112... | collective-permute-start | bytes 786440 | tf_op jit(solution)/shard_map/ppermute | solution.py:510
  311.0 20.1 %copy-start.7 = (f32[2,256,128]{2,1,0:T(8,128)}, f32[2,256,128]{2,1,0:T(8,128)S(1)}, u32[]{:S(2)}) copy-start(f32[2,256,128]{2,1,0:T(8,128)S(1)} %collective-permute-done.10.refs_1_) | copy-start | bytes 786436
  311.0 17.6 %collective-permute-start.15 = (f32[2,256,128]{2,1,0:T(8,128)}, f32[2,256,128]{2,1,0:T(8,128)S(1)}, u32[]{:S(2)}, u32[]{:S(2)}) collective-permute-start(f32[2,256,128]{2,1,0:T(8,128)} %get-tuple-element.63), channel_id=1, source_target_pairs={{0,192},{16,208},{32,224},{48,240},{64,128},{80,144},{96,160},{112... | collective-permute-start | bytes 786440 | tf_op jit(solution)/shard_map/ppermute | solution.py:510
  314.8 16.4 %copy-start.8 = (f32[2,256,128]{2,1,0:T(8,128)}, f32[2,256,128]{2,1,0:T(8,128)S(1)}, u32[]{:S(2)}) copy-start(f32[2,256,128]{2,1,0:T(8,128)S(1)} %collective-permute-done.11.refs_2_) | copy-start | bytes 786436
  314.8 16.4 %collective-permute-start.16 = (f32[2,256,128]{2,1,0:T(8,128)}, f32[2,256,128]{2,1,0:T(8,128)S(1)}, u32[]{:S(2)}, u32[]{:S(2)}) collective-permute-start(f32[2,256,128]{2,1,0:T(8,128)} %get-tuple-element.64), channel_id=1, source_target_pairs={{0,224},{16,240},{32,192},{48,208},{64,160},{80,176},{96,128},{112... | collective-permute-start | bytes 786440 | tf_op jit(solution)/shard_map/ppermute | solution.py:510
  (15 other events, 91.3 us)

commit v4 on v3

--- a/solution.py
+++ b/solution.py
@@ -15,6 +15,10 @@
 INNER = 128
 ROWS = 32
 EARLY = 1
+
+
+def granted(mebibytes):
+    return pltpu.CompilerParams(vmem_limit_bytes=mebibytes * 2**20)
 
 
 def split(values):
@@ -142,7 +146,7 @@
             dest = step * 2 + part
             for block in range(2):
                 slab = 2 * dest + block
-                back = INNER - offset_ref[slab]
+                back = INNER - offset_ref[dest, 0, block]
                 here = pltpu.roll(y_ref[slab], back, 1)
                 after = pltpu.roll(y_ref[slab + 1], back, 1)
                 gates = jnp.where(lanes < back, here, after)
@@ -395,7 +399,7 @@
 
 def widen(gain):
     wide = jax.ShapeDtypeStruct((SLABS // 4, 2 * INNER, 2 * INNER), jnp.float32)
-    return pl.pallas_call(widen_kernel, out_shape=[wide, wide], name="widen")(azimuth_twiddles(), gain)
+    return pl.pallas_call(widen_kernel, out_shape=[wide, wide], name="widen", compiler_params=granted(16))(azimuth_twiddles(), gain)
 
 
 def filter_call(kernel, place, operands, rows, pairs, extra):
@@ -410,6 +414,7 @@
         out_shape=[blocks, blocks],
         scratch_shapes=[mid] * (1 + extra)
         + [pltpu.VMEM((devices, 2, rows, BLOCK), jnp.float32), pltpu.SemaphoreType.DMA((devices,))],
+        compiler_params=granted(20 + 8 * extra),
     )(place, *operands)
 
 
@@ -439,6 +444,7 @@
         out_specs=[vmem] * chips,
         out_shape=[jax.ShapeDtypeStruct(tuple(block), jnp.float32)] * chips,
         name="pair_add",
+        compiler_params=granted(16),
     )(place, keep, other)
 
 
@@ -451,7 +457,10 @@
 
 def settle(parts):
     return pl.pallas_call(
-        settle_kernel, out_shape=jax.ShapeDtypeStruct(parts[0].shape, jnp.float32), name="settle"
+        settle_kernel,
+        out_shape=jax.ShapeDtypeStruct(parts[0].shape, jnp.float32),
+        name="settle",
+        compiler_params=granted(16),
     )(*parts)
 
 
@@ -466,13 +475,15 @@
     refs[-1][...] = exact_dot(total.reshape(-1, BLOCK), refs[-2][0]).reshape(2, -1, BLOCK)
 
 
-def migrate_last_kernel(a_ref, b_ref, kernel_ref, other_ref, o_ref):
+def migrate_last_kernel(a_ref, *refs):
+    b_refs = refs[:-3]
+    kernel_ref, o_ref = refs[-3], refs[-1]
     low = lax.broadcasted_iota(jnp.int32, (INNER, BLOCK), 1) < BLOCK // 2
     for part in range(2):
         first = a_ref[part]
-        second = b_ref[0, part]
-        for device in range(1, b_ref.shape[0]):
-            second = second + b_ref[device, part]
+        second = b_refs[0][part]
+        for b_ref in b_refs[1:]:
+            second = second + b_ref[part]
         rows = (
             jnp.where(low, first, pltpu.roll(second, BLOCK // 2, 1)),
             jnp.where(low, pltpu.roll(first, BLOCK // 2, 1), second),
@@ -498,11 +509,12 @@
         out_shape=jax.ShapeDtypeStruct((2, pulses, 2 * BLOCK), jnp.float32),
         input_output_aliases=aliases,
         name="migrate",
+        compiler_params=granted(16),
     )(*args)
 
 
-def turn(blocks, axis, groups=None):
-    return lax.all_to_all(blocks, axis, split_axis=0, concat_axis=0, tiled=True, axis_index_groups=groups)
+def turn(blocks, axis):
+    return lax.all_to_all(blocks, axis, split_axis=0, concat_axis=0, tiled=True)
 
 
 def swap(block, distance):
@@ -517,7 +529,7 @@
     fwd_np, inv_np = inner_tables()
     fwd, inv = jnp.asarray(fwd_np), jnp.asarray(inv_np)
     devices = lax.axis_size("pulse")
-    offsets = turn(jnp.broadcast_to(rcmc_offset, (devices, rcmc_offset.shape[0])), "pulse").reshape(-1)
+    offsets = turn(jnp.broadcast_to(rcmc_offset, (devices, 1, rcmc_offset.shape[0])), "pulse")
     by_slab = chirp_phase.reshape(INNER, SLABS).T
     chirp = jnp.stack([jnp.cos(by_slab), jnp.sin(by_slab)]) * (1.0 / gates)
     tables = (fwd, inv, jnp.asarray(twiddles()), chirp)
@@ -551,10 +563,9 @@
     sum_a = [sum_a[0]] + [swap(sum_a[k], 2 * k) for k in range(1, channels // 2)]
     sum_a = settle(sum_a)
     keep, give = narrow_filter(place, part_b, fwd, inv, wide)
-    pair = keep + swap(give, 1)
-    groups = [list(range(core, channels, 2)) for core in range(2)]
-    sum_b = turn(pair, "chan", groups)
-    return migrate(1, migrate_last_kernel, [sum_a, sum_b], rcmc_kernel, rows, image)
+    sum_b = pair_add(place, keep, swap(give, 1))
+    sum_b = [sum_b[0]] + [swap(sum_b[k], 2 * k) for k in range(1, channels // 2)]
+    return migrate(1, migrate_last_kernel, [sum_a, *sum_b], rcmc_kernel, rows, image)
 
 
 def solution(mesh):

time: 341 us -> 341 us (level)
  Pallas kernels: 103 us -> 87.8 us
  waiting for transfers between devices: 24.3 us -> 33.9 us
  starting transfers between devices: 61.8 us -> 66.7 us
    ppermute x17 -> x24, starting transfers between devices: 28.2 us -> 38.2 us  [swap(): return lax.ppermute(block, 'chan', [(i, i ^ distance) for i in devices])]
    ppermute x17 -> x24, waiting for transfers between devices: 18.9 us -> 27.7 us  [swap(): return lax.ppermute(block, 'chan', [(i, i ^ distance) for i in devices])]
    pallas_call x3, Pallas kernels: 43.3 us -> 38.1 us  [filter_call(): pl.pallas_call(kernel, in_specs=[pl.BlockSpec(memory_space=pltpu.SMEM)] +...]
    all_to_all x4 -> x3, starting transfers between devices: 33.6 us -> 28.5 us  [turn(): return lax.all_to_all(blocks, axis, split_axis=0, concat_axis=0, tiled=True)]
  transfers between devices with their start and end apart: 21 -> 27, of which waited for: 8 -> 13; matrix products, arithmetic and copies ran while one was open for 2% -> 2% of each run, Pallas kernels for 28% -> 24%
where the time goes in v4:
time: 341 us; the launch traced here: 337 us
  blocking collectives  134 us (39%)
  Pallas kernels  87.8 us (26%)
  starting transfers between devices  66.7 us (20%)
  waiting for transfers between devices  33.9 us (10%)
  local copies, waits for them, and re-layouts  12.1 us (4%)
    all_to_all x2, blocking collectives, turn(): return lax.all_to_all(blocks, axis, split_axis=0, concat_axis=0, tiled=True)  134 us
    ppermute x24, starting transfers between devices, swap(): return lax.ppermute(block, 'chan', [(i, i ^ distance) for i in devices])  38.2 us
    pallas_call x3, Pallas kernels, filter_call(): pl.pallas_call(kernel, in_specs=[pl.BlockSpec(memory_space=pltpu.SMEM)] +...  38.1 us
    all_to_all x3, starting transfers between devices, turn(): return lax.all_to_all(blocks, axis, split_axis=0, concat_axis=0, tiled=True)  28.5 us
    ppermute x24, waiting for transfers between devices, swap(): return lax.ppermute(block, 'chan', [(i, i ^ distance) for i in devices])  27.7 us
    pallas_call x1, Pallas kernels, range_late(): pl.pallas_call(late_kernel, grid_spec=pltpu.PrefetchScalarGridSpec(num_sc...  26.3 us
  transfers between devices with their start and end apart: 27, of which 13 were waited for; matrix products, arithmetic and copies ran while one was open for 2% of the time, Pallas kernels for 24%

profile of v4, /device:TPU:4, one launch (start us, length us, event | category | flops | bytes accessed | tf_op | source)
XLA Modules:
  0.0 336.8 jit_solution(182281714314950400)
XLA Ops:
  1.3 11.4 %all-to-all-start = ((s32[16,1,2]{2,1,0:T(1,128)}), s32[16,1,2]{2,1,0:T(1,128)S(1)}, u32[]{:S(2)}, u32[]{:S(2)}) async-start(s32[16,1,2]{2,1,0:T(1,128)} %broadcast_in_dim.12), calls=%async_computation | async-start | bytes 16384 | tf_op jit(solution)/shard_map/all_to_all | solution.py:517
  14.5 6.8 %range_early.1.y_ref = f32[2,33,64,128]{3,2,1,0:T(8,128)} custom-call(f32[1,2,256,4096]{3,2,1,0:T(8,128)} %x_ref.3, bf16[2,256,256]{2,1,0:T(8,128)(2,1)} %constant.16.clone.fwd_ref, bf16[2,256,256]{2,1,0:T(8,128)(2,1)} %constant.17.clone.inv_ref, f32[2,32,128]{2,1,0:T(8,128)} %constant.18.clone.tw_ref, f32[2,32,128]{2,1,0:T(8,128)} %maximum_multiply_fusion.chirp_ref), custom_call_target="tpu_custom_call" | custom-call | tf_op jit(solution)/shard_map/range_early/pallas_call | solution.py:194
  21.8 6.4 %range_window.1 = (f32[16,2,2,32,128]{4,3,2,1,0:T(8,128)}, f32[16,2,128,128]{3,2,1,0:T(8,128)}, f32[16,2,128,128]{3,2,1,0:T(8,128)}) custom-call(s32[16,1,2]{2,1,0:T(1,128)} %copy-done.17, f32[2,33,64,128]{3,2,1,0:T(8,128)} %range_early.1.y_ref), custom_call_target="tpu_custom_call" | custom-call | tf_op jit(solution)/shard_map/range_window/pallas_call | solution.py:218
  28.2 9.6 %all-to-all-start.3 = ((f32[16,2,2,32,128]{4,3,2,1,0:T(8,128)}), f32[16,2,2,32,128]{4,3,2,1,0:T(8,128)S(1)}, u32[]{:S(2)}, u32[]{:S(2)}) async-start(f32[16,2,2,32,128]{4,3,2,1,0:T(8,128)} %get-tuple-element.69), calls=%async_computation.3 | async-start | bytes 2097152 | tf_op jit(solution)/shard_map/all_to_all | solution.py:517
  37.8 26.3 %range_late.1 = (f32[16,2,2,96,128]{4,3,2,1,0:T(8,128)}, f32[16,2,128,128]{3,2,1,0:T(8,128)}, f32[16,2,128,128]{3,2,1,0:T(8,128)}) custom-call(s32[16,1,2]{2,1,0:T(1,128)} %copy-done.17, f32[1,2,256,4096]{3,2,1,0:T(8,128)} %x_ref.3, bf16[2,256,256]{2,1,0:T(8,128)(2,1)} %constant.16.clone.fwd_ref, ...), custom_call_target="tpu_custom_call", output_to_operand_aliasing={{1}: (6, {}), {2}: (7, {})} | custom-call | tf_op jit(solution)/shard_map/range_late/pallas_call | solution.py:235
  64.1 57.0 %all_to_all.25.x_ref = f32[16,2,128,128]{3,2,1,0:T(8,128)} all-to-all(f32[16,2,128,128]{3,2,1,0:T(8,128)} %get-tuple-element.45), channel_id=1, replica_groups=mesh['chan'=16,'pulse'=16] {'pulse'}, dimensions={0} | all-to-all | bytes 4194304 | tf_op jit(solution)/shard_map/all_to_all | solution.py:517
  121.2 76.6 %all_to_all.26.late_ref = f32[16,2,2,96,128]{4,3,2,1,0:T(8,128)S(1)} all-to-all(f32[16,2,2,96,128]{4,3,2,1,0:T(8,128)S(1)} %copy-done.16), channel_id=1, replica_groups=mesh['chan'=16,'pulse'=16] {'pulse'}, dimensions={0} | all-to-all | bytes 6291456 | tf_op jit(solution)/shard_map/all_to_all | solution.py:517
  197.8 7.4 %all-to-all-start.2 = ((f32[16,2,128,128]{3,2,1,0:T(8,128)}), f32[16,2,128,128]{3,2,1,0:T(8,128)}, u32[]{:S(2)}, u32[]{:S(2)}) async-start(f32[16,2,128,128]{3,2,1,0:T(8,128)} %get-tuple-element.58), calls=%async_computation.2 | async-start | bytes 4194304 | tf_op jit(solution)/shard_map/all_to_all | solution.py:517
  213.6 16.0 %shard_map.120 = (f32[8,2,256,128]{3,2,1,0:T(8,128)S(1)}, f32[8,2,256,128]{3,2,1,0:T(8,128)}) custom-call(s32[1]{0:T(128)} %bitcast.place_ref, f32[16,2,2,32,128]{4,3,2,1,0:T(8,128)S(1)} %copy-done.9, f32[16,2,2,96,128]{4,3,2,1,0:T(8,128)S(1)} %all_to_all.26.late_ref, bf16[2,256,256]{2,1,0:T(8,128)(2,1)S(1)} %copy-done.4, ...), custom_call_target="tpu_custom_call" | custom-call | tf_op jit(solution)/shard_map/pallas_call | solution.py:410
  229.7 4.7 %widen.1 = (f32[8,256,256]{2,1,0:T(8,128)S(1)}, f32[8,256,256]{2,1,0:T(8,128)S(1)}) custom-call(f32[2,128,32]{2,1,0:T(8,128)S(1)} %copy-done.14, f32[2,128,32]{2,1,0:T(8,128)S(1)} %get-tuple-element.82.gain_ref), custom_call_target="tpu_custom_call" | custom-call | tf_op jit(solution)/shard_map/widen/pallas_call | solution.py:402
  234.4 9.8 %shard_map.118 = (f32[8,2,128,128]{3,2,1,0:T(8,128)S(1)}, f32[8,2,128,128]{3,2,1,0:T(8,128)}) custom-call(s32[1]{0:T(128)} %bitcast.place_ref, f32[16,2,128,128]{3,2,1,0:T(8,128)S(1)} %copy-done.1, bf16[2,256,256]{2,1,0:T(8,128)(2,1)S(1)} %copy-done.4, bf16[2,256,256]{2,1,0:T(8,128)(2,1)S(1)} %copy-done.6, f32[8,256,256]{2,1,0:T(8,128)S(1)} %get-tuple-element.46.tw_ref, ...), custom_call_target="tpu_custom_call" | custom-call | tf_op jit(solution)/shard_map/pallas_call | solution.py:410
  245.8 6.2 %all-to-all-done.2.x_ref = f32[16,2,128,128]{3,2,1,0:T(8,128)} async-done(((f32[16,2,128,128]{3,2,1,0:T(8,128)}), f32[16,2,128,128]{3,2,1,0:T(8,128)}, u32[]{:S(2)}, u32[]{:S(2)}) %all-to-all-start.2) | async-done | bytes 2097184 | tf_op jit(solution)/shard_map/all_to_all | solution.py:517
  253.5 12.2 %shard_map.119 = (f32[8,2,128,128]{3,2,1,0:T(8,128)S(1)}, f32[8,2,128,128]{3,2,1,0:T(8,128)S(1)}) custom-call(s32[1]{0:T(128)} %bitcast.place_ref, f32[16,2,128,128]{3,2,1,0:T(8,128)} %all-to-all-done.2.x_ref, bf16[2,256,256]{2,1,0:T(8,128)(2,1)S(1)} %copy-done.4, bf16[2,256,256]{2,1,0:T(8,128)(2,1)S(1)} %copy-done.7, ...), custom_call_target="tpu_custom_call" | custom-call | tf_op jit(solution)/shard_map/pallas_call | solution.py:410
  267.3 1.7 collective-permute-start.1
  269.0 2.9 collective-permute-start.2
  273.7 1.9 collective-permute-start.5
  275.6 3.6 %collective-permute-start.6 = (f32[2,128,128]{2,1,0:T(8,128)S(1)}, f32[2,128,128]{2,1,0:T(8,128)S(1)}, u32[]{:S(2)}, u32[]{:S(2)}) collective-permute-start(f32[2,128,128]{2,1,0:T(8,128)S(1)} %get-tuple-element.56), channel_id=1, source_target_pairs={{0,192},{16,208},{32,224},{48,240},{64,128},{80,144},{96,160},{112... | collective-permute-start | bytes 393224 | tf_op jit(solution)/shard_map/ppermute | solution.py:522
  279.2 1.8 pair_add.5
  282.8 3.9 %collective-permute-start.7 = (f32[2,128,128]{2,1,0:T(8,128)S(1)}, f32[2,128,128]{2,1,0:T(8,128)S(1)}, u32[]{:S(2)}, u32[]{:S(2)}) collective-permute-start(f32[2,128,128]{2,1,0:T(8,128)S(1)} %get-tuple-element.57), channel_id=1, source_target_pairs={{0,224},{16,240},{32,192},{48,208},{64,160},{80,176},{96,128},{112... | collective-permute-start | bytes 393224 | tf_op jit(solution)/shard_map/ppermute | solution.py:522
  286.6 2.6 collective-permute-start.11
  290.1 4.1 %collective-permute-start.19 = (f32[2,256,128]{2,1,0:T(8,128)S(1)}, f32[2,256,128]{2,1,0:T(8,128)S(1)}, u32[]{:S(2)}, u32[]{:S(2)}) collective-permute-start(f32[2,256,128]{2,1,0:T(8,128)S(1)} %get-tuple-element.76), channel_id=1, source_target_pairs={{0,96},{16,112},{32,64},{48,80},{64,32},{80,48},{96,0},{112,16},{1... | collective-permute-start | bytes 786440 | tf_op jit(solution)/shard_map/ppermute | solution.py:522
  294.2 4.2 %collective-permute-done.10.refs_2_ = f32[2,128,128]{2,1,0:T(8,128)S(1)} collective-permute-done((f32[2,128,128]{2,1,0:T(8,128)S(1)}, f32[2,128,128]{2,1,0:T(8,128)S(1)}, u32[]{:S(2)}, u32[]{:S(2)}) %collective-permute-start.10) | collective-permute-done | bytes 131104 | tf_op jit(solution)/shard_map/ppermute | solution.py:522
  301.3 1.9 collective-permute-start.21
  303.2 2.5 collective-permute-start.22
  305.6 1.9 collective-permute-start.23
  309.9 4.4 %collective-permute-done.21.refs_5_ = f32[2,256,128]{2,1,0:T(8,128)S(1)} collective-permute-done((f32[2,256,128]{2,1,0:T(8,128)S(1)}, f32[2,256,128]{2,1,0:T(8,128)S(1)}, u32[]{:S(2)}, u32[]{:S(2)}) %collective-permute-start.21) | collective-permute-done | bytes 262176 | tf_op jit(solution)/shard_map/ppermute | solution.py:522
  314.3 2.0 collective-permute-start.14
  316.3 4.7 %collective-permute-done.22.refs_6_ = f32[2,256,128]{2,1,0:T(8,128)S(1)} collective-permute-done((f32[2,256,128]{2,1,0:T(8,128)S(1)}, f32[2,256,128]{2,1,0:T(8,128)S(1)}, u32[]{:S(2)}, u32[]{:S(2)}) %collective-permute-start.22) | collective-permute-done | bytes 262176 | tf_op jit(solution)/shard_map/ppermute | solution.py:522
  321.1 2.9 collective-permute-start.15
  324.0 2.4 collective-permute-done.23.refs_7_
  328.3 3.0 collective-permute-done.13.refs_5_
  331.3 3.4 %collective-permute-done.14.refs_6_ = f32[2,128,128]{2,1,0:T(8,128)S(1)} collective-permute-done((f32[2,128,128]{2,1,0:T(8,128)S(1)}, f32[2,128,128]{2,1,0:T(8,128)S(1)}, u32[]{:S(2)}, u32[]{:S(2)}) %collective-permute-start.14) | collective-permute-done | bytes 131104 | tf_op jit(solution)/shard_map/ppermute | solution.py:522
  (90 shorter events, 30.3 us)
Async XLA Ops:
  0.0 205.2 %copy-start = (f32[2,64]{1,0:T(2,128)S(1)}, f32[2,64]{1,0:T(2,128)}, u32[]{:S(2)}) copy-start(f32[2,64]{1,0:T(2,128)} %param.17) | copy-start | bytes 1540
  1.3 19.9 %all-to-all-start = ((s32[16,1,2]{2,1,0:T(1,128)}), s32[16,1,2]{2,1,0:T(1,128)S(1)}, u32[]{:S(2)}, u32[]{:S(2)}) async-start(s32[16,1,2]{2,1,0:T(1,128)} %broadcast_in_dim.12), calls=%async_computation | async-start | bytes 16384 | tf_op jit(solution)/shard_map/all_to_all | solution.py:517
  28.2 35.9 %all-to-all-start.3 = ((f32[16,2,2,32,128]{4,3,2,1,0:T(8,128)}), f32[16,2,2,32,128]{4,3,2,1,0:T(8,128)S(1)}, u32[]{:S(2)}, u32[]{:S(2)}) async-start(f32[16,2,2,32,128]{4,3,2,1,0:T(8,128)} %get-tuple-element.69), calls=%async_computation.3 | async-start | bytes 2097152 | tf_op jit(solution)/shard_map/all_to_all | solution.py:517
  64.1 57.0 %copy-start.8 = (f32[16,2,2,32,128]{4,3,2,1,0:T(8,128)}, f32[16,2,2,32,128]{4,3,2,1,0:T(8,128)S(1)}, u32[]{:S(2)}) copy-start(f32[16,2,2,32,128]{4,3,2,1,0:T(8,128)S(1)} %all-to-all-done.3.early_ref) | copy-start | bytes 3145732
  64.1 57.0 %copy-start.16 = (f32[16,2,2,96,128]{4,3,2,1,0:T(8,128)S(1)}, f32[16,2,2,96,128]{4,3,2,1,0:T(8,128)}, u32[]{:S(2)}) copy-start(f32[16,2,2,96,128]{4,3,2,1,0:T(8,128)} %get-tuple-element.70) | copy-start | bytes 9437188
  197.8 54.2 %all-to-all-start.2 = ((f32[16,2,128,128]{3,2,1,0:T(8,128)}), f32[16,2,128,128]{3,2,1,0:T(8,128)}, u32[]{:S(2)}, u32[]{:S(2)}) async-start(f32[16,2,128,128]{3,2,1,0:T(8,128)} %get-tuple-element.58), calls=%async_computation.2 | async-start | bytes 4194304 | tf_op jit(solution)/shard_map/all_to_all | solution.py:517
  213.6 20.8 %copy-start.6 = (bf16[2,256,256]{2,1,0:T(8,128)(2,1)S(1)}, bf16[2,256,256]{2,1,0:T(8,128)(2,1)}, u32[]{:S(2)}) copy-start(bf16[2,256,256]{2,1,0:T(8,128)(2,1)} %constant.17.clone.inv_ref) | copy-start | bytes 786436
  229.6 45.9 %collective-permute-start.16 = (f32[8,2,256,128]{3,2,1,0:T(8,128)}, f32[8,2,256,128]{3,2,1,0:T(8,128)}, u32[]{:S(2)}, u32[]{:S(2)}) collective-permute-start(f32[8,2,256,128]{3,2,1,0:T(8,128)} %get-tuple-element.72), channel_id=1, source_target_pairs={{0,16},{16,0},{32,48},{48,32},{64,80},{80,64},{96,112},{112,96},{1... | collective-permute-start | bytes 6291464 | tf_op jit(solution)/shard_map/ppermute | solution.py:522
  245.3 20.6 %collective-permute-start = (f32[8,2,128,128]{3,2,1,0:T(8,128)}, f32[8,2,128,128]{3,2,1,0:T(8,128)}, u32[]{:S(2)}, u32[]{:S(2)}) collective-permute-start(f32[8,2,128,128]{3,2,1,0:T(8,128)} %get-tuple-element.49), channel_id=1, source_target_pairs={{0,16},{16,0},{32,48},{48,32},{64,80},{80,64},{96,112},{112,96},{1... | collective-permute-start | bytes 3145736 | tf_op jit(solution)/shard_map/ppermute | solution.py:522
  265.7 6.4 %collective-permute-start.8 = (f32[8,2,128,128]{3,2,1,0:T(8,128)S(1)}, f32[8,2,128,128]{3,2,1,0:T(8,128)S(1)}, u32[]{:S(2)}, u32[]{:S(2)}) collective-permute-start(f32[8,2,128,128]{3,2,1,0:T(8,128)S(1)} %get-tuple-element.60), channel_id=1, source_target_pairs={{0,16},{16,0},{32,48},{48,32},{64,80},{80,64},{96,112},{112,96},{1... | collective-permute-start | bytes 3145736 | tf_op jit(solution)/shard_map/ppermute | solution.py:522
  267.3 6.3 %collective-permute-start.1 = (f32[2,128,128]{2,1,0:T(8,128)S(1)}, f32[2,128,128]{2,1,0:T(8,128)S(1)}, u32[]{:S(2)}, u32[]{:S(2)}) collective-permute-start(f32[2,128,128]{2,1,0:T(8,128)S(1)} %get-tuple-element.51), channel_id=1, source_target_pairs={{0,32},{16,48},{32,0},{48,16},{64,96},{80,112},{96,64},{112,80},{1... | collective-permute-start | bytes 393224 | tf_op jit(solution)/shard_map/ppermute | solution.py:522
  269.0 12.0 %collective-permute-start.2 = (f32[2,128,128]{2,1,0:T(8,128)S(1)}, f32[2,128,128]{2,1,0:T(8,128)S(1)}, u32[]{:S(2)}, u32[]{:S(2)}) collective-permute-start(f32[2,128,128]{2,1,0:T(8,128)S(1)} %get-tuple-element.52), channel_id=1, source_target_pairs={{0,64},{16,80},{32,96},{48,112},{64,0},{80,16},{96,32},{112,48},{1... | collective-permute-start | bytes 393224 | tf_op jit(solution)/shard_map/ppermute | solution.py:522
  271.9 10.4 %collective-permute-start.3 = (f32[2,128,128]{2,1,0:T(8,128)S(1)}, f32[2,128,128]{2,1,0:T(8,128)S(1)}, u32[]{:S(2)}, u32[]{:S(2)}) collective-permute-start(f32[2,128,128]{2,1,0:T(8,128)S(1)} %get-tuple-element.53), channel_id=1, source_target_pairs={{0,96},{16,112},{32,64},{48,80},{64,32},{80,48},{96,0},{112,16},{1... | collective-permute-start | bytes 393224 | tf_op jit(solution)/shard_map/ppermute | solution.py:522
  272.1 10.6 %collective-permute-start.4 = (f32[2,128,128]{2,1,0:T(8,128)S(1)}, f32[2,128,128]{2,1,0:T(8,128)S(1)}, u32[]{:S(2)}, u32[]{:S(2)}) collective-permute-start(f32[2,128,128]{2,1,0:T(8,128)S(1)} %get-tuple-element.54), channel_id=1, source_target_pairs={{0,128},{16,144},{32,160},{48,176},{64,192},{80,208},{96,224},{112... | collective-permute-start | bytes 393224 | tf_op jit(solution)/shard_map/ppermute | solution.py:522
  273.7 13.0 %collective-permute-start.5 = (f32[2,128,128]{2,1,0:T(8,128)S(1)}, f32[2,128,128]{2,1,0:T(8,128)S(1)}, u32[]{:S(2)}, u32[]{:S(2)}) collective-permute-start(f32[2,128,128]{2,1,0:T(8,128)S(1)} %get-tuple-element.55), channel_id=1, source_target_pairs={{0,160},{16,176},{32,128},{48,144},{64,224},{80,240},{96,192},{112... | collective-permute-start | bytes 393224 | tf_op jit(solution)/shard_map/ppermute | solution.py:522
  275.6 11.1 %collective-permute-start.6 = (f32[2,128,128]{2,1,0:T(8,128)S(1)}, f32[2,128,128]{2,1,0:T(8,128)S(1)}, u32[]{:S(2)}, u32[]{:S(2)}) collective-permute-start(f32[2,128,128]{2,1,0:T(8,128)S(1)} %get-tuple-element.56), channel_id=1, source_target_pairs={{0,192},{16,208},{32,224},{48,240},{64,128},{80,144},{96,160},{112... | collective-permute-start | bytes 393224 | tf_op jit(solution)/shard_map/ppermute | solution.py:522
  281.0 45.5 %copy-start.15 = (f32[2,128,128]{2,1,0:T(8,128)S(1)}, f32[2,128,128]{2,1,0:T(8,128)}, u32[]{:S(2)}) copy-start(f32[2,128,128]{2,1,0:T(8,128)} %refs_8_.3) | copy-start | bytes 393220
  281.0 22.2 %collective-permute-start.17 = (f32[2,256,128]{2,1,0:T(8,128)S(1)}, f32[2,256,128]{2,1,0:T(8,128)S(1)}, u32[]{:S(2)}, u32[]{:S(2)}) collective-permute-start(f32[2,256,128]{2,1,0:T(8,128)S(1)} %get-tuple-element.74), channel_id=1, source_target_pairs={{0,32},{16,48},{32,0},{48,16},{64,96},{80,112},{96,64},{112,80},{1... | collective-permute-start | bytes 786440 | tf_op jit(solution)/shard_map/ppermute | solution.py:522
  282.3 23.4 %collective-permute-start.18 = (f32[2,256,128]{2,1,0:T(8,128)S(1)}, f32[2,256,128]{2,1,0:T(8,128)S(1)}, u32[]{:S(2)}, u32[]{:S(2)}) collective-permute-start(f32[2,256,128]{2,1,0:T(8,128)S(1)} %get-tuple-element.75), channel_id=1, source_target_pairs={{0,64},{16,80},{32,96},{48,112},{64,0},{80,16},{96,32},{112,48},{1... | collective-permute-start | bytes 786440 | tf_op jit(solution)/shard_map/ppermute | solution.py:522
  282.8 7.4 %collective-permute-start.7 = (f32[2,128,128]{2,1,0:T(8,128)S(1)}, f32[2,128,128]{2,1,0:T(8,128)S(1)}, u32[]{:S(2)}, u32[]{:S(2)}) collective-permute-start(f32[2,128,128]{2,1,0:T(8,128)S(1)} %get-tuple-element.57), channel_id=1, source_target_pairs={{0,224},{16,240},{32,192},{48,208},{64,160},{80,176},{96,128},{112... | collective-permute-start | bytes 393224 | tf_op jit(solution)/shard_map/ppermute | solution.py:522
  286.6 11.8 %collective-permute-start.10 = (f32[2,128,128]{2,1,0:T(8,128)S(1)}, f32[2,128,128]{2,1,0:T(8,128)S(1)}, u32[]{:S(2)}, u32[]{:S(2)}) collective-permute-start(f32[2,128,128]{2,1,0:T(8,128)S(1)} %get-tuple-element.63), channel_id=1, source_target_pairs={{0,64},{16,80},{32,96},{48,112},{64,0},{80,16},{96,32},{112,48},{1... | collective-permute-start | bytes 393224 | tf_op jit(solution)/shard_map/ppermute | solution.py:522
  286.6 14.6 %collective-permute-start.11 = (f32[2,128,128]{2,1,0:T(8,128)S(1)}, f32[2,128,128]{2,1,0:T(8,128)S(1)}, u32[]{:S(2)}, u32[]{:S(2)}) collective-permute-start(f32[2,128,128]{2,1,0:T(8,128)S(1)} %get-tuple-element.64), channel_id=1, source_target_pairs={{0,96},{16,112},{32,64},{48,80},{64,32},{80,48},{96,0},{112,16},{1... | collective-permute-start | bytes 393224 | tf_op jit(solution)/shard_map/ppermute | solution.py:522
  290.1 17.4 %collective-permute-start.19 = (f32[2,256,128]{2,1,0:T(8,128)S(1)}, f32[2,256,128]{2,1,0:T(8,128)S(1)}, u32[]{:S(2)}, u32[]{:S(2)}) collective-permute-start(f32[2,256,128]{2,1,0:T(8,128)S(1)} %get-tuple-element.76), channel_id=1, source_target_pairs={{0,96},{16,112},{32,64},{48,80},{64,32},{80,48},{96,0},{112,16},{1... | collective-permute-start | bytes 786440 | tf_op jit(solution)/shard_map/ppermute | solution.py:522
  298.5 9.9 %collective-permute-start.20 = (f32[2,256,128]{2,1,0:T(8,128)S(1)}, f32[2,256,128]{2,1,0:T(8,128)S(1)}, u32[]{:S(2)}, u32[]{:S(2)}) collective-permute-start(f32[2,256,128]{2,1,0:T(8,128)S(1)} %get-tuple-element.77), channel_id=1, source_target_pairs={{0,128},{16,144},{32,160},{48,176},{64,192},{80,208},{96,224},{112... | collective-permute-start | bytes 786440 | tf_op jit(solution)/shard_map/ppermute | solution.py:522
  301.3 13.1 %collective-permute-start.21 = (f32[2,256,128]{2,1,0:T(8,128)S(1)}, f32[2,256,128]{2,1,0:T(8,128)S(1)}, u32[]{:S(2)}, u32[]{:S(2)}) collective-permute-start(f32[2,256,128]{2,1,0:T(8,128)S(1)} %get-tuple-element.78), channel_id=1, source_target_pairs={{0,160},{16,176},{32,128},{48,144},{64,224},{80,240},{96,192},{112... | collective-permute-start | bytes 786440 | tf_op jit(solution)/shard_map/ppermute | solution.py:522
  303.2 17.9 %collective-permute-start.22 = (f32[2,256,128]{2,1,0:T(8,128)S(1)}, f32[2,256,128]{2,1,0:T(8,128)S(1)}, u32[]{:S(2)}, u32[]{:S(2)}) collective-permute-start(f32[2,256,128]{2,1,0:T(8,128)S(1)} %get-tuple-element.79), channel_id=1, source_target_pairs={{0,192},{16,208},{32,224},{48,240},{64,128},{80,144},{96,160},{112... | collective-permute-start | bytes 786440 | tf_op jit(solution)/shard_map/ppermute | solution.py:522
  305.6 20.8 %collective-permute-start.23 = (f32[2,256,128]{2,1,0:T(8,128)S(1)}, f32[2,256,128]{2,1,0:T(8,128)S(1)}, u32[]{:S(2)}, u32[]{:S(2)}) collective-permute-start(f32[2,256,128]{2,1,0:T(8,128)S(1)} %get-tuple-element.80), channel_id=1, source_target_pairs={{0,224},{16,240},{32,192},{48,208},{64,160},{80,176},{96,128},{112... | collective-permute-start | bytes 786440 | tf_op jit(solution)/shard_map/ppermute | solution.py:522
  307.6 20.8 %collective-permute-start.12 = (f32[2,128,128]{2,1,0:T(8,128)S(1)}, f32[2,128,128]{2,1,0:T(8,128)S(1)}, u32[]{:S(2)}, u32[]{:S(2)}) collective-permute-start(f32[2,128,128]{2,1,0:T(8,128)S(1)} %get-tuple-element.65), channel_id=1, source_target_pairs={{0,128},{16,144},{32,160},{48,176},{64,192},{80,208},{96,224},{112... | collective-permute-start | bytes 393224 | tf_op jit(solution)/shard_map/ppermute | solution.py:522
  308.3 22.9 %collective-permute-start.13 = (f32[2,128,128]{2,1,0:T(8,128)S(1)}, f32[2,128,128]{2,1,0:T(8,128)S(1)}, u32[]{:S(2)}, u32[]{:S(2)}) collective-permute-start(f32[2,128,128]{2,1,0:T(8,128)S(1)} %get-tuple-element.66), channel_id=1, source_target_pairs={{0,160},{16,176},{32,128},{48,144},{64,224},{80,240},{96,192},{112... | collective-permute-start | bytes 393224 | tf_op jit(solution)/shard_map/ppermute | solution.py:522
  314.3 20.3 %collective-permute-start.14 = (f32[2,128,128]{2,1,0:T(8,128)S(1)}, f32[2,128,128]{2,1,0:T(8,128)S(1)}, u32[]{:S(2)}, u32[]{:S(2)}) collective-permute-start(f32[2,128,128]{2,1,0:T(8,128)S(1)} %get-tuple-element.67), channel_id=1, source_target_pairs={{0,192},{16,208},{32,224},{48,240},{64,128},{80,144},{96,160},{112... | collective-permute-start | bytes 393224 | tf_op jit(solution)/shard_map/ppermute | solution.py:522
  321.1 14.6 %collective-permute-start.15 = (f32[2,128,128]{2,1,0:T(8,128)S(1)}, f32[2,128,128]{2,1,0:T(8,128)S(1)}, u32[]{:S(2)}, u32[]{:S(2)}) collective-permute-start(f32[2,128,128]{2,1,0:T(8,128)S(1)} %get-tuple-element.68), channel_id=1, source_target_pairs={{0,224},{16,240},{32,192},{48,208},{64,160},{80,176},{96,128},{112... | collective-permute-start | bytes 393224 | tf_op jit(solution)/shard_map/ppermute | solution.py:522
  326.5 9.2 %collective-permute-start.9 = (f32[2,128,128]{2,1,0:T(8,128)S(1)}, f32[2,128,128]{2,1,0:T(8,128)S(1)}, u32[]{:S(2)}, u32[]{:S(2)}) collective-permute-start(f32[2,128,128]{2,1,0:T(8,128)S(1)} %get-tuple-element.62), channel_id=1, source_target_pairs={{0,32},{16,48},{32,0},{48,16},{64,96},{80,112},{96,64},{112,80},{1... | collective-permute-start | bytes 393224 | tf_op jit(solution)/shard_map/ppermute | solution.py:522
  (14 other events, 128.6 us)

commit v5 on v4

--- a/solution.py
+++ b/solution.py
@@ -136,7 +136,27 @@
     y_ref[SLABS] = jnp.zeros((2 * ROWS, INNER), jnp.float32)
 
 
-def windows(offset_ref, y_ref, z0_ref, za_ref, zb_ref):
+def window_at(offset_ref, y_ref, dest, block, lanes):
+    slab = 2 * dest + block
+    back = INNER - offset_ref[dest, 0, block]
+    here = pltpu.roll(y_ref[slab], back, 1)
+    after = pltpu.roll(y_ref[slab + 1], back, 1)
+    return jnp.where(lanes < back, here, after)
+
+
+def first_windows(offset_ref, y_ref, z0_ref):
+    lanes = lax.broadcasted_iota(jnp.int32, (2 * ROWS, INNER), 1)
+
+    def window(step, carry):
+        for part in range(4):
+            dest = step * 4 + part
+            z0_ref[dest, 0] = window_at(offset_ref, y_ref, dest, 0, lanes).reshape(2, ROWS, INNER)
+        return carry
+
+    lax.fori_loop(0, SLABS // 8, window, 0)
+
+
+def second_windows(offset_ref, y_ref, za_ref, zb_ref):
     lanes = lax.broadcasted_iota(jnp.int32, (2 * ROWS, INNER), 1)
     upper = pl.program_id(0) % 2
     mine = lanes // (INNER // 2) == upper
@@ -144,22 +164,14 @@
     def window(step, carry):
         for part in range(2):
             dest = step * 2 + part
-            for block in range(2):
-                slab = 2 * dest + block
-                back = INNER - offset_ref[dest, 0, block]
-                here = pltpu.roll(y_ref[slab], back, 1)
-                after = pltpu.roll(y_ref[slab + 1], back, 1)
-                gates = jnp.where(lanes < back, here, after)
-                if block == 0:
-                    z0_ref[dest, 0] = gates.reshape(2, ROWS, INNER)
-                else:
-                    other = pltpu.roll(gates, INNER // 2, 1)
-                    for z_ref, value in (
-                        (za_ref, jnp.where(upper == 0, gates, other)),
-                        (zb_ref, jnp.where(upper == 0, other, gates)),
-                    ):
-                        held = z_ref[dest].reshape(2 * ROWS, INNER)
-                        z_ref[dest] = jnp.where(mine, value, held).reshape(2, ROWS, INNER)
+            gates = window_at(offset_ref, y_ref, dest, 1, lanes)
+            other = pltpu.roll(gates, INNER // 2, 1)
+            for z_ref, value in (
+                (za_ref, jnp.where(upper == 0, gates, other)),
+                (zb_ref, jnp.where(upper == 0, other, gates)),
+            ):
+                held = z_ref[dest].reshape(2 * ROWS, INNER)
+                z_ref[dest] = jnp.where(mine, value, held).reshape(2, ROWS, INNER)
         return carry
 
     lax.fori_loop(0, SLABS // 4, window, 0)
@@ -169,14 +181,17 @@
     compress(x_ref, fwd_ref, inv_ref, tw_ref, chirp_ref, mid_ref, y_ref.at[0])
 
 
-def window_kernel(offset_ref, y_ref, z0_ref, za_ref, zb_ref):
-    windows(offset_ref, y_ref.at[0], z0_ref, za_ref, zb_ref)
-
-
-def late_kernel(offset_ref, x_ref, fwd_ref, inv_ref, tw_ref, chirp_ref, *refs):
-    z0_ref, za_ref, zb_ref, mid_ref, y_ref = refs[2:]
-    compress(x_ref, fwd_ref, inv_ref, tw_ref, chirp_ref, mid_ref, y_ref)
-    windows(offset_ref, y_ref, z0_ref, za_ref, zb_ref)
+def first_kernel(offset_ref, y_ref, z0_ref):
+    first_windows(offset_ref, y_ref.at[0], z0_ref)
+
+
+def second_kernel(offset_ref, y_ref, za_ref, zb_ref):
+    second_windows(offset_ref, y_ref.at[0], za_ref, zb_ref)
+
+
+def late_kernel(offset_ref, x_ref, fwd_ref, inv_ref, tw_ref, chirp_ref, other_ref, z0_ref, y_ref, mid_ref):
+    compress(x_ref, fwd_ref, inv_ref, tw_ref, chirp_ref, mid_ref, y_ref.at[0])
+    first_windows(offset_ref, y_ref.at[0], z0_ref)
 
 
 def table_specs():
@@ -189,65 +204,73 @@
     return pl.BlockSpec((1, 2, ROWS, gates), lambda i, *_: (0, 0, (i % 2) * (INNER // ROWS) + start + i // 2, 0))
 
 
+def compressed_shape(echoes):
+    return jax.ShapeDtypeStruct((echoes.shape[2] // ROWS, SLABS + 1, 2 * ROWS, INNER), jnp.float32)
+
+
+def compressed_spec(start):
+    return pl.BlockSpec((1, SLABS + 1, 2 * ROWS, INNER), lambda i, *_: (2 * start + i, 0, 0, 0))
+
+
 def range_early(tiles, echoes, tables):
-    slabs = (SLABS + 1, 2 * ROWS, INNER)
     return pl.pallas_call(
         early_kernel,
         grid=(2 * tiles,),
         in_specs=[echo_spec(0, echoes.shape[3])] + table_specs(),
-        out_specs=pl.BlockSpec((1, *slabs), lambda i: (i, 0, 0, 0)),
-        out_shape=jax.ShapeDtypeStruct((2 * tiles, *slabs), jnp.float32),
+        out_specs=compressed_spec(0),
+        out_shape=compressed_shape(echoes),
         scratch_shapes=[pltpu.VMEM((SLABS, ROWS, 2 * INNER), jnp.float32)],
         name="range_early",
     )(echoes, *tables)
 
 
-def block_shapes(dests, rows):
-    part = jax.ShapeDtypeStruct((dests, 2, INNER, BLOCK), jnp.float32)
-    return [jax.ShapeDtypeStruct((dests, 2, 2, rows, BLOCK), jnp.float32), part, part]
-
-
-def block_specs(dests, start):
-    part = pl.BlockSpec((dests, 2, ROWS, BLOCK), lambda i, *_: (0, 0, start + i // 2, 0))
-    return [pl.BlockSpec((dests, 1, 2, ROWS, BLOCK), lambda i, *_: (0, i % 2, 0, i // 2, 0)), part, part]
-
-
-def range_window(offsets, early):
-    steps, slabs, _, _ = early.shape
-    dests = slabs // 2
-    return pl.pallas_call(
-        window_kernel,
+def first_shape(tiles):
+    return jax.ShapeDtypeStruct((SLABS // 2, 2, 2, tiles * ROWS, BLOCK), jnp.float32)
+
+
+def first_spec():
+    return pl.BlockSpec((SLABS // 2, 1, 2, ROWS, BLOCK), lambda i, *_: (0, i % 2, 0, i // 2, 0))
+
+
+def window_first(tiles, offsets, compressed):
+    return pl.pallas_call(
+        first_kernel,
         grid_spec=pltpu.PrefetchScalarGridSpec(
-            num_scalar_prefetch=1,
-            grid=(steps,),
-            in_specs=[pl.BlockSpec((1, slabs, 2 * ROWS, INNER), lambda i, *_: (i, 0, 0, 0))],
-            out_specs=block_specs(dests, 0),
+            num_scalar_prefetch=1, grid=(2 * tiles,), in_specs=[compressed_spec(0)], out_specs=first_spec()
         ),
-        out_shape=block_shapes(dests, steps // 2 * ROWS),
-        name="range_window",
-    )(offsets, early)
-
-
-def range_late(start, offsets, echoes, tables, parts):
-    gates = echoes.shape[3]
-    dests = gates // (2 * BLOCK)
+        out_shape=first_shape(tiles),
+        name="window_first",
+    )(offsets, compressed)
+
+
+def range_late(start, offsets, echoes, tables, compressed):
     tiles = INNER // ROWS - start
     return pl.pallas_call(
         late_kernel,
         grid_spec=pltpu.PrefetchScalarGridSpec(
             num_scalar_prefetch=1,
             grid=(2 * tiles,),
-            in_specs=[echo_spec(start, gates)] + table_specs() + [pl.BlockSpec(memory_space=pl.ANY)] * 2,
-            out_specs=block_specs(dests, start),
-            scratch_shapes=[
-                pltpu.VMEM((SLABS, ROWS, 2 * INNER), jnp.float32),
-                pltpu.VMEM((SLABS + 1, 2 * ROWS, INNER), jnp.float32),
-            ],
+            in_specs=[echo_spec(start, echoes.shape[3])] + table_specs() + [pl.BlockSpec(memory_space=pl.ANY)],
+            out_specs=[first_spec(), compressed_spec(start)],
+            scratch_shapes=[pltpu.VMEM((SLABS, ROWS, 2 * INNER), jnp.float32)],
         ),
-        out_shape=block_shapes(dests, tiles * ROWS),
-        input_output_aliases={6: 1, 7: 2},
+        out_shape=[first_shape(tiles), compressed_shape(echoes)],
+        input_output_aliases={6: 1},
         name="range_late",
-    )(offsets, echoes, *tables, *parts)
+    )(offsets, echoes, *tables, compressed)
+
+
+def window_second(offsets, compressed):
+    part = jax.ShapeDtypeStruct((SLABS // 2, 2, INNER, BLOCK), jnp.float32)
+    spec = pl.BlockSpec((SLABS // 2, 2, ROWS, BLOCK), lambda i, *_: (0, 0, i // 2, 0))
+    return pl.pallas_call(
+        second_kernel,
+        grid_spec=pltpu.PrefetchScalarGridSpec(
+            num_scalar_prefetch=1, grid=(compressed.shape[0],), in_specs=[compressed_spec(0)], out_specs=[spec, spec]
+        ),
+        out_shape=[part, part],
+        name="window_second",
+    )(offsets, compressed)
 
 
 def hand_out(place_ref, o_ref, keep_ref, give_ref, sem):
@@ -344,7 +367,7 @@
             mid_ref[pair, lower, lane] = im
         return carry
 
-    lax.fori_loop(0, INNER // 8, first, 0)
+    lax.fori_loop(0, INNER // 8, first, 0, unroll=2)
 
     def middle(step, carry):
         pairs = [2 * step, 2 * step + 1]
@@ -371,7 +394,7 @@
             o_ref[i, 1, rows, :] = im
         return carry
 
-    lax.fori_loop(0, INNER // 8, last, 0)
+    lax.fori_loop(0, INNER // 8, last, 0, unroll=2)
     hand_out(place_ref, o_ref, keep_ref, give_ref, sem)
 
 
@@ -399,7 +422,7 @@
 
 def widen(gain):
     wide = jax.ShapeDtypeStruct((SLABS // 4, 2 * INNER, 2 * INNER), jnp.float32)
-    return pl.pallas_call(widen_kernel, out_shape=[wide, wide], name="widen", compiler_params=granted(16))(azimuth_twiddles(), gain)
+    return pl.pallas_call(widen_kernel, out_shape=[wide, wide], name="widen", compiler_params=granted(8))(azimuth_twiddles(), gain)
 
 
 def filter_call(kernel, place, operands, rows, pairs, extra):
@@ -414,7 +437,7 @@
         out_shape=[blocks, blocks],
         scratch_shapes=[mid] * (1 + extra)
         + [pltpu.VMEM((devices, 2, rows, BLOCK), jnp.float32), pltpu.SemaphoreType.DMA((devices,))],
-        compiler_params=granted(20 + 8 * extra),
+        compiler_params=granted(16 + 8 * extra),
     )(place, *operands)
 
 
@@ -444,7 +467,7 @@
         out_specs=[vmem] * chips,
         out_shape=[jax.ShapeDtypeStruct(tuple(block), jnp.float32)] * chips,
         name="pair_add",
-        compiler_params=granted(16),
+        compiler_params=granted(8),
     )(place, keep, other)
 
 
@@ -460,7 +483,7 @@
         settle_kernel,
         out_shape=jax.ShapeDtypeStruct(parts[0].shape, jnp.float32),
         name="settle",
-        compiler_params=granted(16),
+        compiler_params=granted(8),
     )(*parts)
 
 
@@ -509,7 +532,7 @@
         out_shape=jax.ShapeDtypeStruct((2, pulses, 2 * BLOCK), jnp.float32),
         input_output_aliases=aliases,
         name="migrate",
-        compiler_params=granted(16),
+        compiler_params=granted(8),
     )(*args)
 
 
@@ -534,8 +557,9 @@
     chirp = jnp.stack([jnp.cos(by_slab), jnp.sin(by_slab)]) * (1.0 / gates)
     tables = (fwd, inv, jnp.asarray(twiddles()), chirp)
     compressed = range_early(EARLY, echoes, tables)
-    early, *parts = range_window(offsets, compressed)
-    late, part_a, part_b = range_late(EARLY, offsets, echoes, tables, parts)
+    early = window_first(EARLY, offsets, compressed)
+    late, compressed = range_late(EARLY, offsets, echoes, tables, compressed)
+    part_a, part_b = window_second(offsets, compressed)
 
     table_count = weight_table.shape[1]
     entry_ids = lax.broadcasted_iota(jnp.int32, (weight_index.shape[1], table_count), 1)

time: 341 us -> 347 us (1.018)
  waiting for transfers between devices: 33.9 us -> 40.3 us
  starting transfers between devices: 66.7 us -> 62.3 us
  Pallas kernels: 87.8 us -> 91.4 us
    pallas_call x1 -> x2, Pallas kernels: 6.38 us -> 18.9 us  [the longest x1 14.9 us: window_second(): pl.pallas_call(second_kernel, grid_spec=pltpu.PrefetchScalarGridSpec(num_...]
    pallas_call x1, Pallas kernels: 26.3 us -> 20.1 us  [range_late(): pl.pallas_call(late_kernel, grid_spec=pltpu.PrefetchScalarGridSpec(num_sc...]
    ppermute x24, waiting for transfers between devices: 27.7 us -> 32.8 us  [swap(): return lax.ppermute(block, 'chan', [(i, i ^ distance) for i in devices])]
    ppermute x24, starting transfers between devices: 38.2 us -> 33.8 us  [swap(): return lax.ppermute(block, 'chan', [(i, i ^ distance) for i in devices])]
  transfers between devices with their start and end apart: 27 -> 27, of which waited for: 13 -> 12; matrix products, arithmetic and copies ran while one was open for 2% -> 2% of each run, Pallas kernels for 24% -> 25%
where the time goes in v5:
time: 347 us; the launch traced here: 343 us
  blocking collectives  134 us (39%)
  Pallas kernels  91.4 us (26%)
  starting transfers between devices  62.3 us (18%)
  waiting for transfers between devices  40.3 us (12%)
  local copies, waits for them, and re-layouts  12.1 us (3%)
    all_to_all x2, blocking collectives, turn(): return lax.all_to_all(blocks, axis, split_axis=0, concat_axis=0, tiled=True)  134 us
    pallas_call x3, Pallas kernels, filter_call(): pl.pallas_call(kernel, in_specs=[pl.BlockSpec(memory_space=pltpu.SMEM)] +...  35.3 us
    ppermute x24, starting transfers between devices, swap(): return lax.ppermute(block, 'chan', [(i, i ^ distance) for i in devices])  33.8 us
    ppermute x24, waiting for transfers between devices, swap(): return lax.ppermute(block, 'chan', [(i, i ^ distance) for i in devices])  32.8 us
    all_to_all x3, starting transfers between devices, turn(): return lax.all_to_all(blocks, axis, split_axis=0, concat_axis=0, tiled=True)  28.5 us
    pallas_call x1, Pallas kernels, range_late(): pl.pallas_call(late_kernel, grid_spec=pltpu.PrefetchScalarGridSpec(num_sc...  20.1 us
    pallas_call x1, Pallas kernels, window_second(): pl.pallas_call(second_kernel, grid_spec=pltpu.PrefetchScalarGridSpec(num_...  14.9 us
    all_to_all x3, waiting for transfers between devices, turn(): return lax.all_to_all(blocks, axis, split_axis=0, concat_axis=0, tiled=True)  7.5 us
  transfers between devices with their start and end apart: 27, of which 12 were waited for; matrix products, arithmetic and copies ran while one was open for 2% of the time, Pallas kernels for 25%

profile of v5, /device:TPU:4, one launch (start us, length us, event | category | flops | bytes accessed | tf_op | source)
XLA Modules:
  0.0 342.5 jit_solution(2573324664825557662)
XLA Ops:
  1.3 11.4 %all-to-all-start = ((s32[16,1,2]{2,1,0:T(1,128)}), s32[16,1,2]{2,1,0:T(1,128)S(1)}, u32[]{:S(2)}, u32[]{:S(2)}) async-start(s32[16,1,2]{2,1,0:T(1,128)} %broadcast_in_dim.12), calls=%async_computation | async-start | bytes 16384 | tf_op jit(solution)/shard_map/all_to_all | solution.py:540
  14.4 6.8 %range_early.1.other_ref.y_ref = f32[8,33,64,128]{3,2,1,0:T(8,128)} custom-call(f32[1,2,256,4096]{3,2,1,0:T(8,128)} %x_ref.3, bf16[2,256,256]{2,1,0:T(8,128)(2,1)} %constant.16.clone.fwd_ref, bf16[2,256,256]{2,1,0:T(8,128)(2,1)} %constant.17.clone.inv_ref, f32[2,32,128]{2,1,0:T(8,128)} %constant.18.clone.tw_ref, f32[2,32,128]{2,1,0:T(8,128)} %maximum_multiply_fusion.chirp_ref), custom_call_target="tpu_custom_call" | custom-call | tf_op jit(solution)/shard_map/range_early/pallas_call | solution.py:216
  21.8 4.0 %window_first.1 = f32[16,2,2,32,128]{4,3,2,1,0:T(8,128)} custom-call(s32[16,1,2]{2,1,0:T(1,128)} %copy-done.17, f32[8,33,64,128]{3,2,1,0:T(8,128)} %range_early.1.other_ref.y_ref), custom_call_target="tpu_custom_call" | custom-call | tf_op jit(solution)/shard_map/window_first/pallas_call | solution.py:236
  25.8 9.6 %all-to-all-start.3 = ((f32[16,2,2,32,128]{4,3,2,1,0:T(8,128)}), f32[16,2,2,32,128]{4,3,2,1,0:T(8,128)S(1)}, u32[]{:S(2)}, u32[]{:S(2)}) async-start(f32[16,2,2,32,128]{4,3,2,1,0:T(8,128)} %window_first.1), calls=%async_computation.3 | async-start | bytes 2097152 | tf_op jit(solution)/shard_map/all_to_all | solution.py:540
  35.4 20.1 %range_late.1 = (f32[16,2,2,96,128]{4,3,2,1,0:T(8,128)}, f32[8,33,64,128]{3,2,1,0:T(8,128)}) custom-call(s32[16,1,2]{2,1,0:T(1,128)} %copy-done.17, f32[1,2,256,4096]{3,2,1,0:T(8,128)} %x_ref.3, bf16[2,256,256]{2,1,0:T(8,128)(2,1)} %constant.16.clone.fwd_ref, bf16[2,256,256]{2,1,0:T(8,128)(2,1)} %constant.17.clone.inv_ref, ...), custom_call_target="tpu_custom_call", output_to_operand_aliasing={{1}: (6, {})} | custom-call | tf_op jit(solution)/shard_map/range_late/pallas_call | solution.py:248
  55.6 14.9 %window_second.1 = (f32[16,2,128,128]{3,2,1,0:T(8,128)}, f32[16,2,128,128]{3,2,1,0:T(8,128)}) custom-call(s32[16,1,2]{2,1,0:T(1,128)} %copy-done.17, f32[8,33,64,128]{3,2,1,0:T(8,128)} %get-tuple-element.41.y_ref), custom_call_target="tpu_custom_call" | custom-call | tf_op jit(solution)/shard_map/window_second/pallas_call | solution.py:266
  70.5 57.0 %all_to_all.25.x_ref = f32[16,2,128,128]{3,2,1,0:T(8,128)} all-to-all(f32[16,2,128,128]{3,2,1,0:T(8,128)} %get-tuple-element.42), channel_id=1, replica_groups=mesh['chan'=16,'pulse'=16] {'pulse'}, dimensions={0} | all-to-all | bytes 4194304 | tf_op jit(solution)/shard_map/all_to_all | solution.py:540
  127.6 76.6 %all_to_all.26.late_ref = f32[16,2,2,96,128]{4,3,2,1,0:T(8,128)S(1)} all-to-all(f32[16,2,2,96,128]{4,3,2,1,0:T(8,128)S(1)} %copy-done.16), channel_id=1, replica_groups=mesh['chan'=16,'pulse'=16] {'pulse'}, dimensions={0} | all-to-all | bytes 6291456 | tf_op jit(solution)/shard_map/all_to_all | solution.py:540
  204.2 7.4 %all-to-all-start.2 = ((f32[16,2,128,128]{3,2,1,0:T(8,128)}), f32[16,2,128,128]{3,2,1,0:T(8,128)}, u32[]{:S(2)}, u32[]{:S(2)}) async-start(f32[16,2,128,128]{3,2,1,0:T(8,128)} %get-tuple-element.55), calls=%async_computation.2 | async-start | bytes 4194304 | tf_op jit(solution)/shard_map/all_to_all | solution.py:540
  220.0 16.1 %shard_map.120 = (f32[8,2,256,128]{3,2,1,0:T(8,128)S(1)}, f32[8,2,256,128]{3,2,1,0:T(8,128)}) custom-call(s32[1]{0:T(128)} %bitcast.place_ref, f32[16,2,2,32,128]{4,3,2,1,0:T(8,128)S(1)} %copy-done.9, f32[16,2,2,96,128]{4,3,2,1,0:T(8,128)S(1)} %all_to_all.26.late_ref, bf16[2,256,256]{2,1,0:T(8,128)(2,1)S(1)} %copy-done.4, ...), custom_call_target="tpu_custom_call" | custom-call | tf_op jit(solution)/shard_map/pallas_call | solution.py:433
  236.2 4.7 %widen.1 = (f32[8,256,256]{2,1,0:T(8,128)S(1)}, f32[8,256,256]{2,1,0:T(8,128)S(1)}) custom-call(f32[2,128,32]{2,1,0:T(8,128)S(1)} %copy-done.14, f32[2,128,32]{2,1,0:T(8,128)S(1)} %get-tuple-element.78.gain_ref), custom_call_target="tpu_custom_call" | custom-call | tf_op jit(solution)/shard_map/widen/pallas_call | solution.py:425
  240.9 8.5 %shard_map.118 = (f32[8,2,128,128]{3,2,1,0:T(8,128)S(1)}, f32[8,2,128,128]{3,2,1,0:T(8,128)}) custom-call(s32[1]{0:T(128)} %bitcast.place_ref, f32[16,2,128,128]{3,2,1,0:T(8,128)S(1)} %copy-done.1, bf16[2,256,256]{2,1,0:T(8,128)(2,1)S(1)} %copy-done.4, bf16[2,256,256]{2,1,0:T(8,128)(2,1)S(1)} %copy-done.6, f32[8,256,256]{2,1,0:T(8,128)S(1)} %get-tuple-element.43.tw_ref, ...), custom_call_target="tpu_custom_call" | custom-call | tf_op jit(solution)/shard_map/pallas_call | solution.py:433
  250.8 7.5 %all-to-all-done.2.x_ref = f32[16,2,128,128]{3,2,1,0:T(8,128)} async-done(((f32[16,2,128,128]{3,2,1,0:T(8,128)}), f32[16,2,128,128]{3,2,1,0:T(8,128)}, u32[]{:S(2)}, u32[]{:S(2)}) %all-to-all-start.2) | async-done | bytes 2097184 | tf_op jit(solution)/shard_map/all_to_all | solution.py:540
  259.9 10.8 %shard_map.119 = (f32[8,2,128,128]{3,2,1,0:T(8,128)S(1)}, f32[8,2,128,128]{3,2,1,0:T(8,128)S(1)}) custom-call(s32[1]{0:T(128)} %bitcast.place_ref, f32[16,2,128,128]{3,2,1,0:T(8,128)} %all-to-all-done.2.x_ref, bf16[2,256,256]{2,1,0:T(8,128)(2,1)S(1)} %copy-done.4, bf16[2,256,256]{2,1,0:T(8,128)(2,1)S(1)} %copy-done.7, ...), custom_call_target="tpu_custom_call" | custom-call | tf_op jit(solution)/shard_map/pallas_call | solution.py:433
  272.3 1.7 collective-permute-start.1
  274.0 2.9 collective-permute-start.2
  278.7 1.9 collective-permute-start.5
  280.6 3.6 %collective-permute-start.6 = (f32[2,128,128]{2,1,0:T(8,128)S(1)}, f32[2,128,128]{2,1,0:T(8,128)S(1)}, u32[]{:S(2)}, u32[]{:S(2)}) collective-permute-start(f32[2,128,128]{2,1,0:T(8,128)S(1)} %get-tuple-element.53), channel_id=1, source_target_pairs={{0,192},{16,208},{32,224},{48,240},{64,128},{80,144},{96,160},{112... | collective-permute-start | bytes 393224 | tf_op jit(solution)/shard_map/ppermute | solution.py:545
  284.2 1.8 pair_add.5
  287.8 3.8 %collective-permute-start.7 = (f32[2,128,128]{2,1,0:T(8,128)S(1)}, f32[2,128,128]{2,1,0:T(8,128)S(1)}, u32[]{:S(2)}, u32[]{:S(2)}) collective-permute-start(f32[2,128,128]{2,1,0:T(8,128)S(1)} %get-tuple-element.54), channel_id=1, source_target_pairs={{0,224},{16,240},{32,192},{48,208},{64,160},{80,176},{96,128},{112... | collective-permute-start | bytes 393224 | tf_op jit(solution)/shard_map/ppermute | solution.py:545
  293.2 1.9 collective-permute-done.7.refs_7_
  295.1 4.0 %collective-permute-start.19 = (f32[2,256,128]{2,1,0:T(8,128)S(1)}, f32[2,256,128]{2,1,0:T(8,128)S(1)}, u32[]{:S(2)}, u32[]{:S(2)}) collective-permute-start(f32[2,256,128]{2,1,0:T(8,128)S(1)} %get-tuple-element.72), channel_id=1, source_target_pairs={{0,96},{16,112},{32,64},{48,80},{64,32},{80,48},{96,0},{112,16},{1... | collective-permute-start | bytes 786440 | tf_op jit(solution)/shard_map/ppermute | solution.py:545
  299.0 5.1 %collective-permute-done.9.refs_1_ = f32[2,128,128]{2,1,0:T(8,128)S(1)} collective-permute-done((f32[2,128,128]{2,1,0:T(8,128)S(1)}, f32[2,128,128]{2,1,0:T(8,128)S(1)}, u32[]{:S(2)}, u32[]{:S(2)}) %collective-permute-start.9) | collective-permute-done | bytes 131104 | tf_op jit(solution)/shard_map/ppermute | solution.py:545
  306.3 2.3 collective-permute-start.21
  308.6 2.0 collective-permute-start.22
  310.6 2.0 collective-permute-start.23
  315.3 2.3 collective-permute-done.21.refs_5_
  318.7 7.9 %collective-permute-done.22.refs_6_ = f32[2,256,128]{2,1,0:T(8,128)S(1)} collective-permute-done((f32[2,256,128]{2,1,0:T(8,128)S(1)}, f32[2,256,128]{2,1,0:T(8,128)S(1)}, u32[]{:S(2)}, u32[]{:S(2)}) %collective-permute-start.22) | collective-permute-done | bytes 262176 | tf_op jit(solution)/shard_map/ppermute | solution.py:545
  326.5 4.6 %collective-permute-done.23.refs_7_ = f32[2,256,128]{2,1,0:T(8,128)S(1)} collective-permute-done((f32[2,256,128]{2,1,0:T(8,128)S(1)}, f32[2,256,128]{2,1,0:T(8,128)S(1)}, u32[]{:S(2)}, u32[]{:S(2)}) %collective-permute-start.23) | collective-permute-done | bytes 262176 | tf_op jit(solution)/shard_map/ppermute | solution.py:545
  333.3 1.6 collective-permute-done.13.refs_5_
  334.9 4.8 %collective-permute-done.14.refs_6_ = f32[2,128,128]{2,1,0:T(8,128)S(1)} collective-permute-done((f32[2,128,128]{2,1,0:T(8,128)S(1)}, f32[2,128,128]{2,1,0:T(8,128)S(1)}, u32[]{:S(2)}, u32[]{:S(2)}) %collective-permute-start.14) | collective-permute-done | bytes 131104 | tf_op jit(solution)/shard_map/ppermute | solution.py:545
  339.7 1.7 collective-permute-done.15.refs_7_
  (91 shorter events, 31.1 us)
Async XLA Ops:
  0.0 211.6 %copy-start = (f32[2,64]{1,0:T(2,128)S(1)}, f32[2,64]{1,0:T(2,128)}, u32[]{:S(2)}) copy-start(f32[2,64]{1,0:T(2,128)} %param.17) | copy-start | bytes 1540
  1.3 20.0 %all-to-all-start = ((s32[16,1,2]{2,1,0:T(1,128)}), s32[16,1,2]{2,1,0:T(1,128)S(1)}, u32[]{:S(2)}, u32[]{:S(2)}) async-start(s32[16,1,2]{2,1,0:T(1,128)} %broadcast_in_dim.12), calls=%async_computation | async-start | bytes 16384 | tf_op jit(solution)/shard_map/all_to_all | solution.py:540
  25.8 44.7 %all-to-all-start.3 = ((f32[16,2,2,32,128]{4,3,2,1,0:T(8,128)}), f32[16,2,2,32,128]{4,3,2,1,0:T(8,128)S(1)}, u32[]{:S(2)}, u32[]{:S(2)}) async-start(f32[16,2,2,32,128]{4,3,2,1,0:T(8,128)} %window_first.1), calls=%async_computation.3 | async-start | bytes 2097152 | tf_op jit(solution)/shard_map/all_to_all | solution.py:540
  70.5 57.1 %copy-start.8 = (f32[16,2,2,32,128]{4,3,2,1,0:T(8,128)}, f32[16,2,2,32,128]{4,3,2,1,0:T(8,128)S(1)}, u32[]{:S(2)}) copy-start(f32[16,2,2,32,128]{4,3,2,1,0:T(8,128)S(1)} %all-to-all-done.3.early_ref) | copy-start | bytes 3145732
  70.5 57.1 %copy-start.16 = (f32[16,2,2,96,128]{4,3,2,1,0:T(8,128)S(1)}, f32[16,2,2,96,128]{4,3,2,1,0:T(8,128)}, u32[]{:S(2)}) copy-start(f32[16,2,2,96,128]{4,3,2,1,0:T(8,128)} %get-tuple-element.66) | copy-start | bytes 9437188
  204.2 54.2 %all-to-all-start.2 = ((f32[16,2,128,128]{3,2,1,0:T(8,128)}), f32[16,2,128,128]{3,2,1,0:T(8,128)}, u32[]{:S(2)}, u32[]{:S(2)}) async-start(f32[16,2,128,128]{3,2,1,0:T(8,128)} %get-tuple-element.55), calls=%async_computation.2 | async-start | bytes 4194304 | tf_op jit(solution)/shard_map/all_to_all | solution.py:540
  220.0 20.9 %copy-start.6 = (bf16[2,256,256]{2,1,0:T(8,128)(2,1)S(1)}, bf16[2,256,256]{2,1,0:T(8,128)(2,1)}, u32[]{:S(2)}) copy-start(bf16[2,256,256]{2,1,0:T(8,128)(2,1)} %constant.17.clone.inv_ref) | copy-start | bytes 786436
  236.1 44.5 %collective-permute-start.16 = (f32[8,2,256,128]{3,2,1,0:T(8,128)}, f32[8,2,256,128]{3,2,1,0:T(8,128)}, u32[]{:S(2)}, u32[]{:S(2)}) collective-permute-start(f32[8,2,256,128]{3,2,1,0:T(8,128)} %get-tuple-element.68), channel_id=1, source_target_pairs={{0,16},{16,0},{32,48},{48,32},{64,80},{80,64},{96,112},{112,96},{1... | collective-permute-start | bytes 6291464 | tf_op jit(solution)/shard_map/ppermute | solution.py:545
  250.3 20.5 %collective-permute-start = (f32[8,2,128,128]{3,2,1,0:T(8,128)}, f32[8,2,128,128]{3,2,1,0:T(8,128)}, u32[]{:S(2)}, u32[]{:S(2)}) collective-permute-start(f32[8,2,128,128]{3,2,1,0:T(8,128)} %get-tuple-element.46), channel_id=1, source_target_pairs={{0,16},{16,0},{32,48},{48,32},{64,80},{80,64},{96,112},{112,96},{1... | collective-permute-start | bytes 3145736 | tf_op jit(solution)/shard_map/ppermute | solution.py:545
  270.7 6.4 %collective-permute-start.8 = (f32[8,2,128,128]{3,2,1,0:T(8,128)S(1)}, f32[8,2,128,128]{3,2,1,0:T(8,128)S(1)}, u32[]{:S(2)}, u32[]{:S(2)}) collective-permute-start(f32[8,2,128,128]{3,2,1,0:T(8,128)S(1)} %get-tuple-element.57), channel_id=1, source_target_pairs={{0,16},{16,0},{32,48},{48,32},{64,80},{80,64},{96,112},{112,96},{1... | collective-permute-start | bytes 3145736 | tf_op jit(solution)/shard_map/ppermute | solution.py:545
  272.3 6.4 %collective-permute-start.1 = (f32[2,128,128]{2,1,0:T(8,128)S(1)}, f32[2,128,128]{2,1,0:T(8,128)S(1)}, u32[]{:S(2)}, u32[]{:S(2)}) collective-permute-start(f32[2,128,128]{2,1,0:T(8,128)S(1)} %get-tuple-element.48), channel_id=1, source_target_pairs={{0,32},{16,48},{32,0},{48,16},{64,96},{80,112},{96,64},{112,80},{1... | collective-permute-start | bytes 393224 | tf_op jit(solution)/shard_map/ppermute | solution.py:545
  274.0 12.0 %collective-permute-start.2 = (f32[2,128,128]{2,1,0:T(8,128)S(1)}, f32[2,128,128]{2,1,0:T(8,128)S(1)}, u32[]{:S(2)}, u32[]{:S(2)}) collective-permute-start(f32[2,128,128]{2,1,0:T(8,128)S(1)} %get-tuple-element.49), channel_id=1, source_target_pairs={{0,64},{16,80},{32,96},{48,112},{64,0},{80,16},{96,32},{112,48},{1... | collective-permute-start | bytes 393224 | tf_op jit(solution)/shard_map/ppermute | solution.py:545
  276.9 10.4 %collective-permute-start.3 = (f32[2,128,128]{2,1,0:T(8,128)S(1)}, f32[2,128,128]{2,1,0:T(8,128)S(1)}, u32[]{:S(2)}, u32[]{:S(2)}) collective-permute-start(f32[2,128,128]{2,1,0:T(8,128)S(1)} %get-tuple-element.50), channel_id=1, source_target_pairs={{0,96},{16,112},{32,64},{48,80},{64,32},{80,48},{96,0},{112,16},{1... | collective-permute-start | bytes 393224 | tf_op jit(solution)/shard_map/ppermute | solution.py:545
  277.1 10.7 %collective-permute-start.4 = (f32[2,128,128]{2,1,0:T(8,128)S(1)}, f32[2,128,128]{2,1,0:T(8,128)S(1)}, u32[]{:S(2)}, u32[]{:S(2)}) collective-permute-start(f32[2,128,128]{2,1,0:T(8,128)S(1)} %get-tuple-element.51), channel_id=1, source_target_pairs={{0,128},{16,144},{32,160},{48,176},{64,192},{80,208},{96,224},{112... | collective-permute-start | bytes 393224 | tf_op jit(solution)/shard_map/ppermute | solution.py:545
  278.7 12.9 %collective-permute-start.5 = (f32[2,128,128]{2,1,0:T(8,128)S(1)}, f32[2,128,128]{2,1,0:T(8,128)S(1)}, u32[]{:S(2)}, u32[]{:S(2)}) collective-permute-start(f32[2,128,128]{2,1,0:T(8,128)S(1)} %get-tuple-element.52), channel_id=1, source_target_pairs={{0,160},{16,176},{32,128},{48,144},{64,224},{80,240},{96,192},{112... | collective-permute-start | bytes 393224 | tf_op jit(solution)/shard_map/ppermute | solution.py:545
  280.6 11.1 %collective-permute-start.6 = (f32[2,128,128]{2,1,0:T(8,128)S(1)}, f32[2,128,128]{2,1,0:T(8,128)S(1)}, u32[]{:S(2)}, u32[]{:S(2)}) collective-permute-start(f32[2,128,128]{2,1,0:T(8,128)S(1)} %get-tuple-element.53), channel_id=1, source_target_pairs={{0,192},{16,208},{32,224},{48,240},{64,128},{80,144},{96,160},{112... | collective-permute-start | bytes 393224 | tf_op jit(solution)/shard_map/ppermute | solution.py:545
  286.0 46.2 %copy-start.15 = (f32[2,128,128]{2,1,0:T(8,128)S(1)}, f32[2,128,128]{2,1,0:T(8,128)}, u32[]{:S(2)}) copy-start(f32[2,128,128]{2,1,0:T(8,128)} %refs_8_.3) | copy-start | bytes 393220
  286.0 22.6 %collective-permute-start.17 = (f32[2,256,128]{2,1,0:T(8,128)S(1)}, f32[2,256,128]{2,1,0:T(8,128)S(1)}, u32[]{:S(2)}, u32[]{:S(2)}) collective-permute-start(f32[2,256,128]{2,1,0:T(8,128)S(1)} %get-tuple-element.70), channel_id=1, source_target_pairs={{0,32},{16,48},{32,0},{48,16},{64,96},{80,112},{96,64},{112,80},{1... | collective-permute-start | bytes 786440 | tf_op jit(solution)/shard_map/ppermute | solution.py:545
  287.3 23.3 %collective-permute-start.18 = (f32[2,256,128]{2,1,0:T(8,128)S(1)}, f32[2,256,128]{2,1,0:T(8,128)S(1)}, u32[]{:S(2)}, u32[]{:S(2)}) collective-permute-start(f32[2,256,128]{2,1,0:T(8,128)S(1)} %get-tuple-element.71), channel_id=1, source_target_pairs={{0,64},{16,80},{32,96},{48,112},{64,0},{80,16},{96,32},{112,48},{1... | collective-permute-start | bytes 786440 | tf_op jit(solution)/shard_map/ppermute | solution.py:545
  287.8 7.3 %collective-permute-start.7 = (f32[2,128,128]{2,1,0:T(8,128)S(1)}, f32[2,128,128]{2,1,0:T(8,128)S(1)}, u32[]{:S(2)}, u32[]{:S(2)}) collective-permute-start(f32[2,128,128]{2,1,0:T(8,128)S(1)} %get-tuple-element.54), channel_id=1, source_target_pairs={{0,224},{16,240},{32,192},{48,208},{64,160},{80,176},{96,128},{112... | collective-permute-start | bytes 393224 | tf_op jit(solution)/shard_map/ppermute | solution.py:545
  291.6 12.5 %collective-permute-start.9 = (f32[2,128,128]{2,1,0:T(8,128)S(1)}, f32[2,128,128]{2,1,0:T(8,128)S(1)}, u32[]{:S(2)}, u32[]{:S(2)}) collective-permute-start(f32[2,128,128]{2,1,0:T(8,128)S(1)} %get-tuple-element.59), channel_id=1, source_target_pairs={{0,32},{16,48},{32,0},{48,16},{64,96},{80,112},{96,64},{112,80},{1... | collective-permute-start | bytes 393224 | tf_op jit(solution)/shard_map/ppermute | solution.py:545
  291.6 14.7 %collective-permute-start.10 = (f32[2,128,128]{2,1,0:T(8,128)S(1)}, f32[2,128,128]{2,1,0:T(8,128)S(1)}, u32[]{:S(2)}, u32[]{:S(2)}) collective-permute-start(f32[2,128,128]{2,1,0:T(8,128)S(1)} %get-tuple-element.60), channel_id=1, source_target_pairs={{0,64},{16,80},{32,96},{48,112},{64,0},{80,16},{96,32},{112,48},{1... | collective-permute-start | bytes 393224 | tf_op jit(solution)/shard_map/ppermute | solution.py:545
  295.1 17.5 %collective-permute-start.19 = (f32[2,256,128]{2,1,0:T(8,128)S(1)}, f32[2,256,128]{2,1,0:T(8,128)S(1)}, u32[]{:S(2)}, u32[]{:S(2)}) collective-permute-start(f32[2,256,128]{2,1,0:T(8,128)S(1)} %get-tuple-element.72), channel_id=1, source_target_pairs={{0,96},{16,112},{32,64},{48,80},{64,32},{80,48},{96,0},{112,16},{1... | collective-permute-start | bytes 786440 | tf_op jit(solution)/shard_map/ppermute | solution.py:545
  304.1 9.8 %collective-permute-start.20 = (f32[2,256,128]{2,1,0:T(8,128)S(1)}, f32[2,256,128]{2,1,0:T(8,128)S(1)}, u32[]{:S(2)}, u32[]{:S(2)}) collective-permute-start(f32[2,256,128]{2,1,0:T(8,128)S(1)} %get-tuple-element.73), channel_id=1, source_target_pairs={{0,128},{16,144},{32,160},{48,176},{64,192},{80,208},{96,224},{112... | collective-permute-start | bytes 786440 | tf_op jit(solution)/shard_map/ppermute | solution.py:545
  306.3 11.3 %collective-permute-start.21 = (f32[2,256,128]{2,1,0:T(8,128)S(1)}, f32[2,256,128]{2,1,0:T(8,128)S(1)}, u32[]{:S(2)}, u32[]{:S(2)}) collective-permute-start(f32[2,256,128]{2,1,0:T(8,128)S(1)} %get-tuple-element.74), channel_id=1, source_target_pairs={{0,160},{16,176},{32,128},{48,144},{64,224},{80,240},{96,192},{112... | collective-permute-start | bytes 786440 | tf_op jit(solution)/shard_map/ppermute | solution.py:545
  308.6 17.9 %collective-permute-start.22 = (f32[2,256,128]{2,1,0:T(8,128)S(1)}, f32[2,256,128]{2,1,0:T(8,128)S(1)}, u32[]{:S(2)}, u32[]{:S(2)}) collective-permute-start(f32[2,256,128]{2,1,0:T(8,128)S(1)} %get-tuple-element.75), channel_id=1, source_target_pairs={{0,192},{16,208},{32,224},{48,240},{64,128},{80,144},{96,160},{112... | collective-permute-start | bytes 786440 | tf_op jit(solution)/shard_map/ppermute | solution.py:545
  310.6 20.6 %collective-permute-start.23 = (f32[2,256,128]{2,1,0:T(8,128)S(1)}, f32[2,256,128]{2,1,0:T(8,128)S(1)}, u32[]{:S(2)}, u32[]{:S(2)}) collective-permute-start(f32[2,256,128]{2,1,0:T(8,128)S(1)} %get-tuple-element.76), channel_id=1, source_target_pairs={{0,224},{16,240},{32,192},{48,208},{64,160},{80,176},{96,128},{112... | collective-permute-start | bytes 786440 | tf_op jit(solution)/shard_map/ppermute | solution.py:545
  312.5 20.7 %collective-permute-start.11 = (f32[2,128,128]{2,1,0:T(8,128)S(1)}, f32[2,128,128]{2,1,0:T(8,128)S(1)}, u32[]{:S(2)}, u32[]{:S(2)}) collective-permute-start(f32[2,128,128]{2,1,0:T(8,128)S(1)} %get-tuple-element.61), channel_id=1, source_target_pairs={{0,96},{16,112},{32,64},{48,80},{64,32},{80,48},{96,0},{112,16},{1... | collective-permute-start | bytes 393224 | tf_op jit(solution)/shard_map/ppermute | solution.py:545
  314.0 19.3 %collective-permute-start.12 = (f32[2,128,128]{2,1,0:T(8,128)S(1)}, f32[2,128,128]{2,1,0:T(8,128)S(1)}, u32[]{:S(2)}, u32[]{:S(2)}) collective-permute-start(f32[2,128,128]{2,1,0:T(8,128)S(1)} %get-tuple-element.62), channel_id=1, source_target_pairs={{0,128},{16,144},{32,160},{48,176},{64,192},{80,208},{96,224},{112... | collective-permute-start | bytes 393224 | tf_op jit(solution)/shard_map/ppermute | solution.py:545
  317.6 17.3 %collective-permute-start.13 = (f32[2,128,128]{2,1,0:T(8,128)S(1)}, f32[2,128,128]{2,1,0:T(8,128)S(1)}, u32[]{:S(2)}, u32[]{:S(2)}) collective-permute-start(f32[2,128,128]{2,1,0:T(8,128)S(1)} %get-tuple-element.63), channel_id=1, source_target_pairs={{0,160},{16,176},{32,128},{48,144},{64,224},{80,240},{96,192},{112... | collective-permute-start | bytes 393224 | tf_op jit(solution)/shard_map/ppermute | solution.py:545
  326.5 13.1 %collective-permute-start.14 = (f32[2,128,128]{2,1,0:T(8,128)S(1)}, f32[2,128,128]{2,1,0:T(8,128)S(1)}, u32[]{:S(2)}, u32[]{:S(2)}) collective-permute-start(f32[2,128,128]{2,1,0:T(8,128)S(1)} %get-tuple-element.64), channel_id=1, source_target_pairs={{0,192},{16,208},{32,224},{48,240},{64,128},{80,144},{96,160},{112... | collective-permute-start | bytes 393224 | tf_op jit(solution)/shard_map/ppermute | solution.py:545
  331.1 10.2 %collective-permute-start.15 = (f32[2,128,128]{2,1,0:T(8,128)S(1)}, f32[2,128,128]{2,1,0:T(8,128)S(1)}, u32[]{:S(2)}, u32[]{:S(2)}) collective-permute-start(f32[2,128,128]{2,1,0:T(8,128)S(1)} %get-tuple-element.65), channel_id=1, source_target_pairs={{0,224},{16,240},{32,192},{48,208},{64,160},{80,176},{96,128},{112... | collective-permute-start | bytes 393224 | tf_op jit(solution)/shard_map/ppermute | solution.py:545
  (14 other events, 124.5 us)

commit v6 on v5

--- a/solution.py
+++ b/solution.py
@@ -156,25 +156,19 @@
     lax.fori_loop(0, SLABS // 8, window, 0)
 
 
-def second_windows(offset_ref, y_ref, za_ref, zb_ref):
+def second_windows(place_ref, offset_ref, y_ref, a_refs, zb_ref):
     lanes = lax.broadcasted_iota(jnp.int32, (2 * ROWS, INNER), 1)
     upper = pl.program_id(0) % 2
     mine = lanes // (INNER // 2) == upper
 
-    def window(step, carry):
-        for part in range(2):
-            dest = step * 2 + part
-            gates = window_at(offset_ref, y_ref, dest, 1, lanes)
-            other = pltpu.roll(gates, INNER // 2, 1)
-            for z_ref, value in (
-                (za_ref, jnp.where(upper == 0, gates, other)),
-                (zb_ref, jnp.where(upper == 0, other, gates)),
-            ):
-                held = z_ref[dest].reshape(2 * ROWS, INNER)
-                z_ref[dest] = jnp.where(mine, value, held).reshape(2, ROWS, INNER)
-        return carry
-
-    lax.fori_loop(0, SLABS // 4, window, 0)
+    for k, a_ref in enumerate(a_refs):
+        dest = jnp.bitwise_xor(place_ref[0], k)
+        gates = window_at(offset_ref, y_ref, dest, 1, lanes)
+        other = pltpu.roll(gates, INNER // 2, 1)
+        held = a_ref[...].reshape(2 * ROWS, INNER)
+        a_ref[...] = jnp.where(mine, jnp.where(upper == 0, gates, other), held).reshape(2, ROWS, INNER)
+        held = zb_ref[dest].reshape(2 * ROWS, INNER)
+        zb_ref[dest] = jnp.where(mine, jnp.where(upper == 0, other, gates), held).reshape(2, ROWS, INNER)
 
 
 def early_kernel(x_ref, fwd_ref, inv_ref, tw_ref, chirp_ref, y_ref, mid_ref):
@@ -185,8 +179,8 @@
     first_windows(offset_ref, y_ref.at[0], z0_ref)
 
 
-def second_kernel(offset_ref, y_ref, za_ref, zb_ref):
-    second_windows(offset_ref, y_ref.at[0], za_ref, zb_ref)
+def second_kernel(place_ref, offset_ref, y_ref, *refs):
+    second_windows(place_ref, offset_ref, y_ref.at[0], refs[:-1], refs[-1])
 
 
 def late_kernel(offset_ref, x_ref, fwd_ref, inv_ref, tw_ref, chirp_ref, other_ref, z0_ref, y_ref, mid_ref):
@@ -260,17 +254,23 @@
     )(offsets, echoes, *tables, compressed)
 
 
-def window_second(offsets, compressed):
-    part = jax.ShapeDtypeStruct((SLABS // 2, 2, INNER, BLOCK), jnp.float32)
-    spec = pl.BlockSpec((SLABS // 2, 2, ROWS, BLOCK), lambda i, *_: (0, 0, i // 2, 0))
+def window_second(place, offsets, compressed):
+    dests = SLABS // 2
+    piece = jax.ShapeDtypeStruct((2, INNER, BLOCK), jnp.float32)
+    part = jax.ShapeDtypeStruct((dests, 2, INNER, BLOCK), jnp.float32)
+    piece_spec = pl.BlockSpec((2, ROWS, BLOCK), lambda i, *_: (0, i // 2, 0))
+    part_spec = pl.BlockSpec((dests, 2, ROWS, BLOCK), lambda i, *_: (0, 0, i // 2, 0))
     return pl.pallas_call(
         second_kernel,
         grid_spec=pltpu.PrefetchScalarGridSpec(
-            num_scalar_prefetch=1, grid=(compressed.shape[0],), in_specs=[compressed_spec(0)], out_specs=[spec, spec]
+            num_scalar_prefetch=2,
+            grid=(compressed.shape[0],),
+            in_specs=[compressed_spec(0)],
+            out_specs=[piece_spec] * dests + [part_spec],
         ),
-        out_shape=[part, part],
+        out_shape=[piece] * dests + [part],
         name="window_second",
-    )(offsets, compressed)
+    )(place, offsets, compressed)
 
 
 def hand_out(place_ref, o_ref, keep_ref, give_ref, sem):
@@ -398,6 +398,19 @@
     hand_out(place_ref, o_ref, keep_ref, give_ref, sem)
 
 
+def pieces_kernel(place_ref, from_ref, *refs):
+    pieces = refs[: SLABS // 2]
+    *rest, x_ref, loads = refs[SLABS // 2 :]
+    copies = [
+        pltpu.make_async_copy(piece, x_ref.at[jnp.bitwise_xor(from_ref[0], k)], loads.at[k]) for k, piece in enumerate(pieces)
+    ]
+    for copy in copies:
+        copy.start()
+    for copy in copies:
+        copy.wait()
+    narrow_kernel(place_ref, x_ref, *rest)
+
+
 def widen_kernel(tw_ref, gain_ref, tw_wide_ref, gain_wide_ref):
     half = SLABS // 2
     high = lax.broadcasted_iota(jnp.int32, (8, INNER), 1) >= INNER // 2
@@ -449,6 +462,28 @@
 def narrow_filter(place, received, fwd, inv, wide):
     operands = (received, fwd, inv, *wide)
     return filter_call(narrow_kernel, place, operands, INNER, SLABS // 4, 0)
+
+
+def pieces_filter(place, source, pieces, fwd, inv, wide):
+    vmem, smem = pl.BlockSpec(memory_space=pltpu.VMEM), pl.BlockSpec(memory_space=pltpu.SMEM)
+    devices = len(pieces)
+    blocks = jax.ShapeDtypeStruct((devices // 2, 2, INNER, BLOCK), jnp.float32)
+    whole = pltpu.VMEM((devices, 2, INNER, BLOCK), jnp.float32)
+    return pl.pallas_call(
+        pieces_kernel,
+        in_specs=[smem, smem] + [pl.BlockSpec(memory_space=pl.ANY)] * devices + [vmem] * 4,
+        out_specs=[pl.BlockSpec(memory_space=pl.ANY)] * 2,
+        out_shape=[blocks, blocks],
+        scratch_shapes=[
+            pltpu.VMEM((SLABS // 4, 2 * INNER, 2 * INNER), jnp.float32),
+            whole,
+            pltpu.SemaphoreType.DMA((devices,)),
+            whole,
+            pltpu.SemaphoreType.DMA((devices,)),
+        ],
+        name="pieces_filter",
+        compiler_params=granted(18),
+    )(place, source, *pieces, fwd, inv, *wide)
 
 
 def pair_kernel(place_ref, keep_ref, other_ref, *out_refs):
@@ -540,9 +575,8 @@
     return lax.all_to_all(blocks, axis, split_axis=0, concat_axis=0, tiled=True)
 
 
-def swap(block, distance):
-    devices = range(lax.axis_size("chan"))
-    return lax.ppermute(block, "chan", [(i, i ^ distance) for i in devices])
+def swap(block, distance, axis="chan"):
+    return lax.ppermute(block, axis, [(i, i ^ distance) for i in range(lax.axis_size(axis))])
 
 
 def body(echoes, chirp_phase, rcmc_kernel, rcmc_offset, az_phase, weight_table, weight_index):
@@ -559,7 +593,8 @@
     compressed = range_early(EARLY, echoes, tables)
     early = window_first(EARLY, offsets, compressed)
     late, compressed = range_late(EARLY, offsets, echoes, tables, compressed)
-    part_a, part_b = window_second(offsets, compressed)
+    source = lax.axis_index("pulse").astype(jnp.int32).reshape(1)
+    *part_a, part_b = window_second(source, offsets, compressed)
 
     table_count = weight_table.shape[1]
     entry_ids = lax.broadcasted_iota(jnp.int32, (weight_index.shape[1], table_count), 1)
@@ -572,7 +607,7 @@
 
     early = turn(early, "pulse")
     late = turn(late, "pulse")
-    part_a = turn(part_a, "pulse")
+    part_a = [part_a[0]] + [swap(part_a[k], k, "pulse") for k in range(1, devices)]
     part_b = turn(part_b, "pulse")
     place = lax.axis_index("chan").astype(jnp.int32).reshape(1)
     channels = lax.axis_size("chan")
@@ -582,7 +617,7 @@
     first = pair_add(place, keep, swap(give, 1))
     first = [first[0]] + [swap(first[k], 2 * k) for k in range(1, channels // 2)]
     image = migrate(0, migrate_kernel, first, rcmc_kernel, rows)
-    keep, give = narrow_filter(place, part_a, fwd, inv, wide)
+    keep, give = pieces_filter(place, source, part_a, fwd, inv, wide)
     sum_a = pair_add(place, keep, swap(give, 1))
     sum_a = [sum_a[0]] + [swap(sum_a[k], 2 * k) for k in range(1, channels // 2)]
     sum_a = settle(sum_a)

time: 347 us -> 361 us (1.040)
  blocking collectives: 134 us -> 0 us
  waiting for transfers between devices: 40.3 us -> 129 us
  starting transfers between devices: 62.3 us -> 120 us
    all_to_all x2 -> x0, blocking collectives: 134 us -> none  [turn(): return lax.all_to_all(blocks, axis, split_axis=0, concat_axis=0, tiled=True)]
    all_to_all x3 -> x4, waiting for transfers between devices: 7.5 us -> 60.1 us  [turn(): return lax.all_to_all(blocks, axis, split_axis=0, concat_axis=0, tiled=True)]
    ppermute x24 -> x39, starting transfers between devices: 33.8 us -> 78.5 us  [swap(): lax.ppermute(block, axis, [(i, i ^ distance) for i in range(lax.axis_size...]
    ppermute x24 -> x39, waiting for transfers between devices: 32.8 us -> 69.3 us  [swap(): lax.ppermute(block, axis, [(i, i ^ distance) for i in range(lax.axis_size...]
    all_to_all x3 -> x4, starting transfers between devices: 28.5 us -> 41.3 us  [turn(): return lax.all_to_all(blocks, axis, split_axis=0, concat_axis=0, tiled=True)]
    pallas_call x0 -> x1, Pallas kernels: none -> 11.8 us  [pieces_filter(): pl.pallas_call(pieces_kernel, in_specs=[smem, smem] + [pl.BlockSpec(memor...]
    pallas_call x3 -> x2, Pallas kernels: 35.3 us -> 26.9 us  [filter_call(): pl.pallas_call(kernel, in_specs=[pl.BlockSpec(memory_space=pltpu.SMEM)] +...]
  transfers between devices with their start and end apart: 27 -> 43, of which waited for: 12 -> 20; matrix products, arithmetic and copies ran while one was open for 2% -> 2% of each run, Pallas kernels for 25% -> 25%
where the time goes in v6:
time: 361 us; the launch traced here: 359 us
  waiting for transfers between devices  129 us (36%)
  starting transfers between devices  120 us (33%)
  Pallas kernels  93.6 us (26%)
  local copies, waits for them, and re-layouts  13.2 us (4%)
    ppermute x39, starting transfers between devices, swap(): lax.ppermute(block, axis, [(i, i ^ distance) for i in range(lax.axis_size...  78.5 us
    ppermute x39, waiting for transfers between devices, swap(): lax.ppermute(block, axis, [(i, i ^ distance) for i in range(lax.axis_size...  69.3 us
    all_to_all x4, waiting for transfers between devices, turn(): return lax.all_to_all(blocks, axis, split_axis=0, concat_axis=0, tiled=True)  60.1 us
    all_to_all x4, starting transfers between devices, turn(): return lax.all_to_all(blocks, axis, split_axis=0, concat_axis=0, tiled=True)  41.3 us
    pallas_call x2, Pallas kernels, filter_call(): pl.pallas_call(kernel, in_specs=[pl.BlockSpec(memory_space=pltpu.SMEM)] +...  26.9 us
    pallas_call x1, Pallas kernels, range_late(): pl.pallas_call(late_kernel, grid_spec=pltpu.PrefetchScalarGridSpec(num_sc...  20.1 us
    pallas_call x1, Pallas kernels, window_second(): pl.pallas_call(second_kernel, grid_spec=pltpu.PrefetchScalarGridSpec(num_...  13.9 us
    pallas_call x1, Pallas kernels, pieces_filter(): pl.pallas_call(pieces_kernel, in_specs=[smem, smem] + [pl.BlockSpec(memor...  11.8 us
  transfers between devices with their start and end apart: 43, of which 20 were waited for; matrix products, arithmetic and copies ran while one was open for 2% of the time, Pallas kernels for 25%

profile of v6, /device:TPU:4, one launch (start us, length us, event | category | flops | bytes accessed | tf_op | source)
XLA Modules:
  0.0 358.9 jit_solution(2437325371261412253)
XLA Ops:
  1.3 11.4 %all-to-all-start = ((s32[16,1,2]{2,1,0:T(1,128)}), s32[16,1,2]{2,1,0:T(1,128)S(1)}, u32[]{:S(2)}, u32[]{:S(2)}) async-start(s32[16,1,2]{2,1,0:T(1,128)} %broadcast_in_dim.12), calls=%async_computation | async-start | bytes 16384 | tf_op jit(solution)/shard_map/all_to_all | solution.py:575
  14.5 6.8 %range_early.1.other_ref.y_ref = f32[8,33,64,128]{3,2,1,0:T(8,128)} custom-call(f32[1,2,256,4096]{3,2,1,0:T(8,128)} %x_ref.3, bf16[2,256,256]{2,1,0:T(8,128)(2,1)} %constant.18.clone.fwd_ref.refs_16_, bf16[2,256,256]{2,1,0:T(8,128)(2,1)} %constant.19.clone.inv_ref.refs_17_, f32[2,32,128]{2,1,0:T(8,128)} %constant.20.clone.tw_ref, ...), custom_call_target="tpu_custom_call" | custom-call | tf_op jit(solution)/shard_map/range_early/pallas_call | solution.py:210
  21.8 4.0 %window_first.1 = f32[16,2,2,32,128]{4,3,2,1,0:T(8,128)} custom-call(s32[16,1,2]{2,1,0:T(1,128)} %copy-done.16, f32[8,33,64,128]{3,2,1,0:T(8,128)} %range_early.1.other_ref.y_ref), custom_call_target="tpu_custom_call" | custom-call | tf_op jit(solution)/shard_map/window_first/pallas_call | solution.py:230
  25.8 9.6 %all-to-all-start.2 = ((f32[16,2,2,32,128]{4,3,2,1,0:T(8,128)}), f32[16,2,2,32,128]{4,3,2,1,0:T(8,128)S(1)}, u32[]{:S(2)}, u32[]{:S(2)}) async-start(f32[16,2,2,32,128]{4,3,2,1,0:T(8,128)} %window_first.1), calls=%async_computation.2 | async-start | bytes 2097152 | tf_op jit(solution)/shard_map/all_to_all | solution.py:575
  35.5 20.1 %range_late.1 = (f32[16,2,2,96,128]{4,3,2,1,0:T(8,128)}, f32[8,33,64,128]{3,2,1,0:T(8,128)}) custom-call(s32[16,1,2]{2,1,0:T(1,128)} %copy-done.16, f32[1,2,256,4096]{3,2,1,0:T(8,128)} %x_ref.3, bf16[2,256,256]{2,1,0:T(8,128)(2,1)} %constant.18.clone.fwd_ref.refs_16_, ...), custom_call_target="tpu_custom_call", output_to_operand_aliasing={{1}: (6, {})} | custom-call | tf_op jit(solution)/shard_map/range_late/pallas_call | solution.py:242
  55.6 4.6 %all-to-all-done.2.early_ref = f32[16,2,2,32,128]{4,3,2,1,0:T(8,128)S(1)} async-done(((f32[16,2,2,32,128]{4,3,2,1,0:T(8,128)}), f32[16,2,2,32,128]{4,3,2,1,0:T(8,128)S(1)}, u32[]{:S(2)}, u32[]{:S(2)}) %all-to-all-start.2) | async-done | bytes 1048608 | tf_op jit(solution)/shard_map/all_to_all | solution.py:575
  61.2 7.7 %all-to-all-start.3 = ((f32[16,2,2,96,128]{4,3,2,1,0:T(8,128)}), f32[16,2,2,96,128]{4,3,2,1,0:T(8,128)S(1)}, u32[]{:S(2)}, u32[]{:S(2)}) async-start(f32[16,2,2,96,128]{4,3,2,1,0:T(8,128)} %get-tuple-element.96), calls=%async_computation.3 | async-start | bytes 6291456 | tf_op jit(solution)/shard_map/all_to_all | solution.py:575
  68.9 13.9 %window_second.1 = (f32[2,128,128]{2,1,0:T(8,128)}, f32[2,128,128]{2,1,0:T(8,128)}, f32[2,128,128]{2,1,0:T(8,128)}, f32[2,128,128]{2,1,0:T(8,128)}, f32[2,128,12...) custom-call(s32[1]{0:T(128)} %bitcast.1.place_ref.from_ref, ...), custom_call_target="tpu_custom_call" | custom-call | tf_op jit(solution)/shard_map/window_second/pallas_call | solution.py:263
  82.7 55.5 %all-to-all-done.3.late_ref = f32[16,2,2,96,128]{4,3,2,1,0:T(8,128)S(1)} async-done(((f32[16,2,2,96,128]{4,3,2,1,0:T(8,128)}), f32[16,2,2,96,128]{4,3,2,1,0:T(8,128)S(1)}, u32[]{:S(2)}, u32[]{:S(2)}) %all-to-all-start.3) | async-done | bytes 3145760 | tf_op jit(solution)/shard_map/all_to_all | solution.py:575
  138.2 12.5 %all-to-all-start.1 = ((f32[16,2,128,128]{3,2,1,0:T(8,128)}), f32[16,2,128,128]{3,2,1,0:T(8,128)}, u32[]{:S(2)}, u32[]{:S(2)}) async-start(f32[16,2,128,128]{3,2,1,0:T(8,128)} %get-tuple-element.85), calls=%async_computation.1 | async-start | bytes 4194304 | tf_op jit(solution)/shard_map/all_to_all | solution.py:575
  159.3 16.1 %shard_map.119 = (f32[8,2,256,128]{3,2,1,0:T(8,128)S(1)}, f32[8,2,256,128]{3,2,1,0:T(8,128)}) custom-call(s32[1]{0:T(128)} %bitcast.place_ref, f32[16,2,2,32,128]{4,3,2,1,0:T(8,128)S(1)} %copy-done.8, f32[16,2,2,96,128]{4,3,2,1,0:T(8,128)S(1)} %all-to-all-done.3.late_ref, bf16[2,256,256]{2,1,0:T(8,128)(2,1)S(1)} %copy-done.3, ...), custom_call_target="tpu_custom_call" | custom-call | tf_op jit(solution)/shard_map/pallas_call | solution.py:446
  180.0 5.4 %collective-permute-start.3 = (f32[2,128,128]{2,1,0:T(8,128)S(1)}, f32[2,128,128]{2,1,0:T(8,128)S(1)}, u32[]{:S(2)}, u32[]{:S(2)}) collective-permute-start(f32[2,128,128]{2,1,0:T(8,128)S(1)} %copy-done.28), channel_id=1, source_target_pairs={{0,4},{1,5},{2,6},{3,7},{4,0},{5,1},{6,2},{7,3},{8,12},{9,13},{10,... | collective-permute-start | bytes 393224 | tf_op jit(solution)/shard_map/ppermute | solution.py:579
  185.3 19.0 %collective-permute-done.refs_1_ = f32[2,128,128]{2,1,0:T(8,128)S(1)} collective-permute-done((f32[2,128,128]{2,1,0:T(8,128)S(1)}, f32[2,128,128]{2,1,0:T(8,128)S(1)}, u32[]{:S(2)}, u32[]{:S(2)}) %collective-permute-start) | collective-permute-done | bytes 131104 | tf_op jit(solution)/shard_map/ppermute | solution.py:579
  206.1 4.0 %collective-permute-done.1.refs_2_ = f32[2,128,128]{2,1,0:T(8,128)S(1)} collective-permute-done((f32[2,128,128]{2,1,0:T(8,128)S(1)}, f32[2,128,128]{2,1,0:T(8,128)S(1)}, u32[]{:S(2)}, u32[]{:S(2)}) %collective-permute-start.1) | collective-permute-done | bytes 131104 | tf_op jit(solution)/shard_map/ppermute | solution.py:579
  210.0 4.4 %collective-permute-start.5 = (f32[2,128,128]{2,1,0:T(8,128)S(1)}, f32[2,128,128]{2,1,0:T(8,128)S(1)}, u32[]{:S(2)}, u32[]{:S(2)}) collective-permute-start(f32[2,128,128]{2,1,0:T(8,128)S(1)} %copy-done.26), channel_id=1, source_target_pairs={{0,6},{1,7},{2,4},{3,5},{4,2},{5,3},{6,0},{7,1},{8,14},{9,15},{10,... | collective-permute-start | bytes 393224 | tf_op jit(solution)/shard_map/ppermute | solution.py:579
  217.4 5.0 %collective-permute-done.4.refs_5_ = f32[2,128,128]{2,1,0:T(8,128)S(1)} collective-permute-done((f32[2,128,128]{2,1,0:T(8,128)S(1)}, f32[2,128,128]{2,1,0:T(8,128)S(1)}, u32[]{:S(2)}, u32[]{:S(2)}) %collective-permute-start.4) | collective-permute-done | bytes 131104 | tf_op jit(solution)/shard_map/ppermute | solution.py:579
  228.3 3.9 %collective-permute-start.10 = (f32[2,128,128]{2,1,0:T(8,128)S(1)}, f32[2,128,128]{2,1,0:T(8,128)S(1)}, u32[]{:S(2)}, u32[]{:S(2)}) collective-permute-start(f32[2,128,128]{2,1,0:T(8,128)S(1)} %copy-done.21), channel_id=1, source_target_pairs={{0,11},{1,10},{2,9},{3,8},{4,15},{5,14},{6,13},{7,12},{8,3},{9,2},... | collective-permute-start | bytes 393224 | tf_op jit(solution)/shard_map/ppermute | solution.py:579
  232.2 3.8 %collective-permute-start.11 = (f32[2,128,128]{2,1,0:T(8,128)S(1)}, f32[2,128,128]{2,1,0:T(8,128)S(1)}, u32[]{:S(2)}, u32[]{:S(2)}) collective-permute-start(f32[2,128,128]{2,1,0:T(8,128)S(1)} %copy-done.20), channel_id=1, source_target_pairs={{0,12},{1,13},{2,14},{3,15},{4,8},{5,9},{6,10},{7,11},{8,4},{9,5},... | collective-permute-start | bytes 393224 | tf_op jit(solution)/shard_map/ppermute | solution.py:579
  236.0 5.4 %collective-permute-start.12 = (f32[2,128,128]{2,1,0:T(8,128)S(1)}, f32[2,128,128]{2,1,0:T(8,128)S(1)}, u32[]{:S(2)}, u32[]{:S(2)}) collective-permute-start(f32[2,128,128]{2,1,0:T(8,128)S(1)} %copy-done.19), channel_id=1, source_target_pairs={{0,13},{1,12},{2,15},{3,14},{4,9},{5,8},{6,11},{7,10},{8,5},{9,4},... | collective-permute-start | bytes 393224 | tf_op jit(solution)/shard_map/ppermute | solution.py:579
  241.4 3.3 collective-permute-done.9.refs_10_
  244.8 4.1 %collective-permute-start.14 = (f32[2,128,128]{2,1,0:T(8,128)S(1)}, f32[2,128,128]{2,1,0:T(8,128)S(1)}, u32[]{:S(2)}, u32[]{:S(2)}) collective-permute-start(f32[2,128,128]{2,1,0:T(8,128)S(1)} %copy-done.17), channel_id=1, source_target_pairs={{0,15},{1,14},{2,13},{3,12},{4,11},{5,10},{6,9},{7,8},{8,7},{9,6},... | collective-permute-start | bytes 393224 | tf_op jit(solution)/shard_map/ppermute | solution.py:579
  248.9 4.6 %widen.1 = (f32[8,256,256]{2,1,0:T(8,128)S(1)}, f32[8,256,256]{2,1,0:T(8,128)S(1)}) custom-call(f32[2,128,32]{2,1,0:T(8,128)S(1)} %copy-done.13, f32[2,128,32]{2,1,0:T(8,128)S(1)} %get-tuple-element.108.gain_ref), custom_call_target="tpu_custom_call" | custom-call | tf_op jit(solution)/shard_map/widen/pallas_call | solution.py:438
  259.6 11.8 %pieces_filter.1 = (f32[8,2,128,128]{3,2,1,0:T(8,128)S(1)}, f32[8,2,128,128]{3,2,1,0:T(8,128)}) custom-call(s32[1]{0:T(128)} %bitcast.place_ref, s32[1]{0:T(128)} %bitcast.1.place_ref.from_ref, f32[2,128,128]{2,1,0:T(8,128)S(1)} %copy-done.15, f32[2,128,128]{2,1,0:T(8,128)S(1)} %collective-permute-done.refs_1_, ...), custom_call_target="tpu_custom_call" | custom-call | tf_op jit(solution)/shard_map/pieces_filter/pallas_call | solution.py:472
  274.1 10.8 %shard_map.118 = (f32[8,2,128,128]{3,2,1,0:T(8,128)S(1)}, f32[8,2,128,128]{3,2,1,0:T(8,128)S(1)}) custom-call(s32[1]{0:T(128)} %bitcast.place_ref, f32[16,2,128,128]{3,2,1,0:T(8,128)} %all-to-all-done.1.x_ref, bf16[2,256,256]{2,1,0:T(8,128)(2,1)S(1)} %copy-done.3, bf16[2,256,256]{2,1,0:T(8,128)(2,1)S(1)} %copy-done.6, ...), custom_call_target="tpu_custom_call" | custom-call | tf_op jit(solution)/shard_map/pallas_call | solution.py:446
  294.2 3.7 %collective-permute-done.17.refs_2_ = f32[2,128,128]{2,1,0:T(8,128)S(1)} collective-permute-done((f32[2,128,128]{2,1,0:T(8,128)S(1)}, f32[2,128,128]{2,1,0:T(8,128)S(1)}, u32[]{:S(2)}, u32[]{:S(2)}) %collective-permute-start.17) | collective-permute-done | bytes 131104 | tf_op jit(solution)/shard_map/ppermute | solution.py:579
  302.8 4.1 %collective-permute-start.33 = (f32[2,256,128]{2,1,0:T(8,128)S(1)}, f32[2,256,128]{2,1,0:T(8,128)S(1)}, u32[]{:S(2)}, u32[]{:S(2)}) collective-permute-start(f32[2,256,128]{2,1,0:T(8,128)S(1)} %get-tuple-element.101), channel_id=1, source_target_pairs={{0,64},{16,80},{32,96},{48,112},{64,0},{80,16},{96,32},{112,48},{1... | collective-permute-start | bytes 786440 | tf_op jit(solution)/shard_map/ppermute | solution.py:579
  307.9 4.5 %collective-permute-start.25 = (f32[2,128,128]{2,1,0:T(8,128)S(1)}, f32[2,128,128]{2,1,0:T(8,128)S(1)}, u32[]{:S(2)}, u32[]{:S(2)}) collective-permute-start(f32[2,128,128]{2,1,0:T(8,128)S(1)} %get-tuple-element.90), channel_id=1, source_target_pairs={{0,64},{16,80},{32,96},{48,112},{64,0},{80,16},{96,32},{112,48},{1... | collective-permute-start | bytes 393224 | tf_op jit(solution)/shard_map/ppermute | solution.py:579
  315.1 5.3 %collective-permute-done.24.refs_1_ = f32[2,128,128]{2,1,0:T(8,128)S(1)} collective-permute-done((f32[2,128,128]{2,1,0:T(8,128)S(1)}, f32[2,128,128]{2,1,0:T(8,128)S(1)}, u32[]{:S(2)}, u32[]{:S(2)}) %collective-permute-start.24) | collective-permute-done | bytes 131104 | tf_op jit(solution)/shard_map/ppermute | solution.py:579
  324.9 3.4 collective-permute-start.37
  337.3 4.2 %collective-permute-done.37.refs_6_ = f32[2,256,128]{2,1,0:T(8,128)S(1)} collective-permute-done((f32[2,256,128]{2,1,0:T(8,128)S(1)}, f32[2,256,128]{2,1,0:T(8,128)S(1)}, u32[]{:S(2)}, u32[]{:S(2)}) %collective-permute-start.37) | collective-permute-done | bytes 262176 | tf_op jit(solution)/shard_map/ppermute | solution.py:579
  341.5 3.6 %collective-permute-start.29 = (f32[2,128,128]{2,1,0:T(8,128)S(1)}, f32[2,128,128]{2,1,0:T(8,128)S(1)}, u32[]{:S(2)}, u32[]{:S(2)}) collective-permute-start(f32[2,128,128]{2,1,0:T(8,128)S(1)} %get-tuple-element.94), channel_id=1, source_target_pairs={{0,192},{16,208},{32,224},{48,240},{64,128},{80,144},{96,160},{112... | collective-permute-start | bytes 393224 | tf_op jit(solution)/shard_map/ppermute | solution.py:579
  352.9 3.7 %collective-permute-done.29.refs_6_ = f32[2,128,128]{2,1,0:T(8,128)S(1)} collective-permute-done((f32[2,128,128]{2,1,0:T(8,128)S(1)}, f32[2,128,128]{2,1,0:T(8,128)S(1)}, u32[]{:S(2)}, u32[]{:S(2)}) %collective-permute-start.29) | collective-permute-done | bytes 131104 | tf_op jit(solution)/shard_map/ppermute | solution.py:579
  (149 shorter events, 78.2 us)
Async XLA Ops:
  1.3 19.9 %all-to-all-start = ((s32[16,1,2]{2,1,0:T(1,128)}), s32[16,1,2]{2,1,0:T(1,128)S(1)}, u32[]{:S(2)}, u32[]{:S(2)}) async-start(s32[16,1,2]{2,1,0:T(1,128)} %broadcast_in_dim.12), calls=%async_computation | async-start | bytes 16384 | tf_op jit(solution)/shard_map/all_to_all | solution.py:575
  25.8 34.3 %all-to-all-start.2 = ((f32[16,2,2,32,128]{4,3,2,1,0:T(8,128)}), f32[16,2,2,32,128]{4,3,2,1,0:T(8,128)S(1)}, u32[]{:S(2)}, u32[]{:S(2)}) async-start(f32[16,2,2,32,128]{4,3,2,1,0:T(8,128)} %window_first.1), calls=%async_computation.2 | async-start | bytes 2097152 | tf_op jit(solution)/shard_map/all_to_all | solution.py:575
  61.2 77.0 %all-to-all-start.3 = ((f32[16,2,2,96,128]{4,3,2,1,0:T(8,128)}), f32[16,2,2,96,128]{4,3,2,1,0:T(8,128)S(1)}, u32[]{:S(2)}, u32[]{:S(2)}) async-start(f32[16,2,2,96,128]{4,3,2,1,0:T(8,128)} %get-tuple-element.96), calls=%async_computation.3 | async-start | bytes 6291456 | tf_op jit(solution)/shard_map/all_to_all | solution.py:575
  138.2 134.3 %all-to-all-start.1 = ((f32[16,2,128,128]{3,2,1,0:T(8,128)}), f32[16,2,128,128]{3,2,1,0:T(8,128)}, u32[]{:S(2)}, u32[]{:S(2)}) async-start(f32[16,2,128,128]{3,2,1,0:T(8,128)} %get-tuple-element.85), calls=%async_computation.1 | async-start | bytes 4194304 | tf_op jit(solution)/shard_map/all_to_all | solution.py:575
  175.4 123.3 %collective-permute-start.31 = (f32[8,2,256,128]{3,2,1,0:T(8,128)}, f32[8,2,256,128]{3,2,1,0:T(8,128)}, u32[]{:S(2)}, u32[]{:S(2)}) collective-permute-start(f32[8,2,256,128]{3,2,1,0:T(8,128)} %get-tuple-element.98), channel_id=1, source_target_pairs={{0,16},{16,0},{32,48},{48,32},{64,80},{80,64},{96,112},{112,96},{1... | collective-permute-start | bytes 6291464 | tf_op jit(solution)/shard_map/ppermute | solution.py:579
  175.5 28.8 %collective-permute-start = (f32[2,128,128]{2,1,0:T(8,128)S(1)}, f32[2,128,128]{2,1,0:T(8,128)S(1)}, u32[]{:S(2)}, u32[]{:S(2)}) collective-permute-start(f32[2,128,128]{2,1,0:T(8,128)S(1)} %copy-done.31), channel_id=1, source_target_pairs={{0,1},{1,0},{2,3},{3,2},{4,5},{5,4},{6,7},{7,6},{8,9},{9,8},{10,11... | collective-permute-start | bytes 393224 | tf_op jit(solution)/shard_map/ppermute | solution.py:579
  177.0 33.0 %collective-permute-start.1 = (f32[2,128,128]{2,1,0:T(8,128)S(1)}, f32[2,128,128]{2,1,0:T(8,128)S(1)}, u32[]{:S(2)}, u32[]{:S(2)}) collective-permute-start(f32[2,128,128]{2,1,0:T(8,128)S(1)} %copy-done.30), channel_id=1, source_target_pairs={{0,2},{1,3},{2,0},{3,1},{4,6},{5,7},{6,4},{7,5},{8,10},{9,11},{10,... | collective-permute-start | bytes 393224 | tf_op jit(solution)/shard_map/ppermute | solution.py:579
  179.4 35.5 %collective-permute-start.2 = (f32[2,128,128]{2,1,0:T(8,128)S(1)}, f32[2,128,128]{2,1,0:T(8,128)S(1)}, u32[]{:S(2)}, u32[]{:S(2)}) collective-permute-start(f32[2,128,128]{2,1,0:T(8,128)S(1)} %copy-done.29), channel_id=1, source_target_pairs={{0,3},{1,2},{2,1},{3,0},{4,7},{5,6},{6,5},{7,4},{8,11},{9,10},{10,... | collective-permute-start | bytes 393224 | tf_op jit(solution)/shard_map/ppermute | solution.py:579
  180.0 37.0 %collective-permute-start.3 = (f32[2,128,128]{2,1,0:T(8,128)S(1)}, f32[2,128,128]{2,1,0:T(8,128)S(1)}, u32[]{:S(2)}, u32[]{:S(2)}) collective-permute-start(f32[2,128,128]{2,1,0:T(8,128)S(1)} %copy-done.28), channel_id=1, source_target_pairs={{0,4},{1,5},{2,6},{3,7},{4,0},{5,1},{6,2},{7,3},{8,12},{9,13},{10,... | collective-permute-start | bytes 393224 | tf_op jit(solution)/shard_map/ppermute | solution.py:579
  204.3 18.1 %collective-permute-start.4 = (f32[2,128,128]{2,1,0:T(8,128)S(1)}, f32[2,128,128]{2,1,0:T(8,128)S(1)}, u32[]{:S(2)}, u32[]{:S(2)}) collective-permute-start(f32[2,128,128]{2,1,0:T(8,128)S(1)} %copy-done.27), channel_id=1, source_target_pairs={{0,5},{1,4},{2,7},{3,6},{4,1},{5,0},{6,3},{7,2},{8,13},{9,12},{10,... | collective-permute-start | bytes 393224 | tf_op jit(solution)/shard_map/ppermute | solution.py:579
  210.0 15.4 %collective-permute-start.5 = (f32[2,128,128]{2,1,0:T(8,128)S(1)}, f32[2,128,128]{2,1,0:T(8,128)S(1)}, u32[]{:S(2)}, u32[]{:S(2)}) collective-permute-start(f32[2,128,128]{2,1,0:T(8,128)S(1)} %copy-done.26), channel_id=1, source_target_pairs={{0,6},{1,7},{2,4},{3,5},{4,2},{5,3},{6,0},{7,1},{8,14},{9,15},{10,... | collective-permute-start | bytes 393224 | tf_op jit(solution)/shard_map/ppermute | solution.py:579
  214.8 13.5 %collective-permute-start.6 = (f32[2,128,128]{2,1,0:T(8,128)S(1)}, f32[2,128,128]{2,1,0:T(8,128)S(1)}, u32[]{:S(2)}, u32[]{:S(2)}) collective-permute-start(f32[2,128,128]{2,1,0:T(8,128)S(1)} %copy-done.25), channel_id=1, source_target_pairs={{0,7},{1,6},{2,5},{3,4},{4,3},{5,2},{6,1},{7,0},{8,15},{9,14},{10,... | collective-permute-start | bytes 393224 | tf_op jit(solution)/shard_map/ppermute | solution.py:579
  216.9 15.3 %collective-permute-start.7 = (f32[2,128,128]{2,1,0:T(8,128)S(1)}, f32[2,128,128]{2,1,0:T(8,128)S(1)}, u32[]{:S(2)}, u32[]{:S(2)}) collective-permute-start(f32[2,128,128]{2,1,0:T(8,128)S(1)} %copy-done.24), channel_id=1, source_target_pairs={{0,8},{1,9},{2,10},{3,11},{4,12},{5,13},{6,14},{7,15},{8,0},{9,1},... | collective-permute-start | bytes 393224 | tf_op jit(solution)/shard_map/ppermute | solution.py:579
  222.4 13.6 %collective-permute-start.8 = (f32[2,128,128]{2,1,0:T(8,128)S(1)}, f32[2,128,128]{2,1,0:T(8,128)S(1)}, u32[]{:S(2)}, u32[]{:S(2)}) collective-permute-start(f32[2,128,128]{2,1,0:T(8,128)S(1)} %copy-done.23), channel_id=1, source_target_pairs={{0,9},{1,8},{2,11},{3,10},{4,13},{5,12},{6,15},{7,14},{8,1},{9,0},... | collective-permute-start | bytes 393224 | tf_op jit(solution)/shard_map/ppermute | solution.py:579
  225.5 19.3 %collective-permute-start.9 = (f32[2,128,128]{2,1,0:T(8,128)S(1)}, f32[2,128,128]{2,1,0:T(8,128)S(1)}, u32[]{:S(2)}, u32[]{:S(2)}) collective-permute-start(f32[2,128,128]{2,1,0:T(8,128)S(1)} %copy-done.22), channel_id=1, source_target_pairs={{0,10},{1,11},{2,8},{3,9},{4,14},{5,15},{6,12},{7,13},{8,2},{9,3},... | collective-permute-start | bytes 393224 | tf_op jit(solution)/shard_map/ppermute | solution.py:579
  228.3 16.4 %collective-permute-start.10 = (f32[2,128,128]{2,1,0:T(8,128)S(1)}, f32[2,128,128]{2,1,0:T(8,128)S(1)}, u32[]{:S(2)}, u32[]{:S(2)}) collective-permute-start(f32[2,128,128]{2,1,0:T(8,128)S(1)} %copy-done.21), channel_id=1, source_target_pairs={{0,11},{1,10},{2,9},{3,8},{4,15},{5,14},{6,13},{7,12},{8,3},{9,2},... | collective-permute-start | bytes 393224 | tf_op jit(solution)/shard_map/ppermute | solution.py:579
  232.2 21.3 %collective-permute-start.11 = (f32[2,128,128]{2,1,0:T(8,128)S(1)}, f32[2,128,128]{2,1,0:T(8,128)S(1)}, u32[]{:S(2)}, u32[]{:S(2)}) collective-permute-start(f32[2,128,128]{2,1,0:T(8,128)S(1)} %copy-done.20), channel_id=1, source_target_pairs={{0,12},{1,13},{2,14},{3,15},{4,8},{5,9},{6,10},{7,11},{8,4},{9,5},... | collective-permute-start | bytes 393224 | tf_op jit(solution)/shard_map/ppermute | solution.py:579
  236.0 17.5 %collective-permute-start.12 = (f32[2,128,128]{2,1,0:T(8,128)S(1)}, f32[2,128,128]{2,1,0:T(8,128)S(1)}, u32[]{:S(2)}, u32[]{:S(2)}) collective-permute-start(f32[2,128,128]{2,1,0:T(8,128)S(1)} %copy-done.19), channel_id=1, source_target_pairs={{0,13},{1,12},{2,15},{3,14},{4,9},{5,8},{6,11},{7,10},{8,5},{9,4},... | collective-permute-start | bytes 393224 | tf_op jit(solution)/shard_map/ppermute | solution.py:579
  244.8 14.8 %collective-permute-start.14 = (f32[2,128,128]{2,1,0:T(8,128)S(1)}, f32[2,128,128]{2,1,0:T(8,128)S(1)}, u32[]{:S(2)}, u32[]{:S(2)}) collective-permute-start(f32[2,128,128]{2,1,0:T(8,128)S(1)} %copy-done.17), channel_id=1, source_target_pairs={{0,15},{1,14},{2,13},{3,12},{4,11},{5,10},{6,9},{7,8},{8,7},{9,6},... | collective-permute-start | bytes 393224 | tf_op jit(solution)/shard_map/ppermute | solution.py:579
  272.5 13.0 %collective-permute-start.15 = (f32[8,2,128,128]{3,2,1,0:T(8,128)}, f32[8,2,128,128]{3,2,1,0:T(8,128)}, u32[]{:S(2)}, u32[]{:S(2)}) collective-permute-start(f32[8,2,128,128]{3,2,1,0:T(8,128)} %get-tuple-element.76), channel_id=1, source_target_pairs={{0,16},{16,0},{32,48},{48,32},{64,80},{80,64},{96,112},{112,96},{1... | collective-permute-start | bytes 3145736 | tf_op jit(solution)/shard_map/ppermute | solution.py:579
  284.9 17.8 %collective-permute-start.23 = (f32[8,2,128,128]{3,2,1,0:T(8,128)S(1)}, f32[8,2,128,128]{3,2,1,0:T(8,128)S(1)}, u32[]{:S(2)}, u32[]{:S(2)}) collective-permute-start(f32[8,2,128,128]{3,2,1,0:T(8,128)S(1)} %get-tuple-element.87), channel_id=1, source_target_pairs={{0,16},{16,0},{32,48},{48,32},{64,80},{80,64},{96,112},{112,96},{1... | collective-permute-start | bytes 3145736 | tf_op jit(solution)/shard_map/ppermute | solution.py:579
  293.0 14.0 %collective-permute-start.19 = (f32[2,128,128]{2,1,0:T(8,128)S(1)}, f32[2,128,128]{2,1,0:T(8,128)S(1)}, u32[]{:S(2)}, u32[]{:S(2)}) collective-permute-start(f32[2,128,128]{2,1,0:T(8,128)S(1)} %get-tuple-element.81), channel_id=1, source_target_pairs={{0,128},{16,144},{32,160},{48,176},{64,192},{80,208},{96,224},{112... | collective-permute-start | bytes 393224 | tf_op jit(solution)/shard_map/ppermute | solution.py:579
  302.3 22.6 %collective-permute-start.32 = (f32[2,256,128]{2,1,0:T(8,128)S(1)}, f32[2,256,128]{2,1,0:T(8,128)S(1)}, u32[]{:S(2)}, u32[]{:S(2)}) collective-permute-start(f32[2,256,128]{2,1,0:T(8,128)S(1)} %get-tuple-element.100), channel_id=1, source_target_pairs={{0,32},{16,48},{32,0},{48,16},{64,96},{80,112},{96,64},{112,80},{1... | collective-permute-start | bytes 786440 | tf_op jit(solution)/shard_map/ppermute | solution.py:579
  302.8 25.5 %collective-permute-start.33 = (f32[2,256,128]{2,1,0:T(8,128)S(1)}, f32[2,256,128]{2,1,0:T(8,128)S(1)}, u32[]{:S(2)}, u32[]{:S(2)}) collective-permute-start(f32[2,256,128]{2,1,0:T(8,128)S(1)} %get-tuple-element.101), channel_id=1, source_target_pairs={{0,64},{16,80},{32,96},{48,112},{64,0},{80,16},{96,32},{112,48},{1... | collective-permute-start | bytes 786440 | tf_op jit(solution)/shard_map/ppermute | solution.py:579
  307.9 16.3 %collective-permute-start.25 = (f32[2,128,128]{2,1,0:T(8,128)S(1)}, f32[2,128,128]{2,1,0:T(8,128)S(1)}, u32[]{:S(2)}, u32[]{:S(2)}) collective-permute-start(f32[2,128,128]{2,1,0:T(8,128)S(1)} %get-tuple-element.90), channel_id=1, source_target_pairs={{0,64},{16,80},{32,96},{48,112},{64,0},{80,16},{96,32},{112,48},{1... | collective-permute-start | bytes 393224 | tf_op jit(solution)/shard_map/ppermute | solution.py:579
  315.1 15.3 %collective-permute-start.34 = (f32[2,256,128]{2,1,0:T(8,128)S(1)}, f32[2,256,128]{2,1,0:T(8,128)S(1)}, u32[]{:S(2)}, u32[]{:S(2)}) collective-permute-start(f32[2,256,128]{2,1,0:T(8,128)S(1)} %get-tuple-element.102), channel_id=1, source_target_pairs={{0,96},{16,112},{32,64},{48,80},{64,32},{80,48},{96,0},{112,16},{1... | collective-permute-start | bytes 786440 | tf_op jit(solution)/shard_map/ppermute | solution.py:579
  324.9 16.7 %collective-permute-start.37 = (f32[2,256,128]{2,1,0:T(8,128)S(1)}, f32[2,256,128]{2,1,0:T(8,128)S(1)}, u32[]{:S(2)}, u32[]{:S(2)}) collective-permute-start(f32[2,256,128]{2,1,0:T(8,128)S(1)} %get-tuple-element.105), channel_id=1, source_target_pairs={{0,192},{16,208},{32,224},{48,240},{64,128},{80,144},{96,160},{112... | collective-permute-start | bytes 786440 | tf_op jit(solution)/shard_map/ppermute | solution.py:579
  328.3 19.6 %collective-permute-start.38 = (f32[2,256,128]{2,1,0:T(8,128)S(1)}, f32[2,256,128]{2,1,0:T(8,128)S(1)}, u32[]{:S(2)}, u32[]{:S(2)}) collective-permute-start(f32[2,256,128]{2,1,0:T(8,128)S(1)} %get-tuple-element.106), channel_id=1, source_target_pairs={{0,224},{16,240},{32,192},{48,208},{64,160},{80,176},{96,128},{112... | collective-permute-start | bytes 786440 | tf_op jit(solution)/shard_map/ppermute | solution.py:579
  330.4 20.4 %collective-permute-start.26 = (f32[2,128,128]{2,1,0:T(8,128)S(1)}, f32[2,128,128]{2,1,0:T(8,128)S(1)}, u32[]{:S(2)}, u32[]{:S(2)}) collective-permute-start(f32[2,128,128]{2,1,0:T(8,128)S(1)} %get-tuple-element.91), channel_id=1, source_target_pairs={{0,96},{16,112},{32,64},{48,80},{64,32},{80,48},{96,0},{112,16},{1... | collective-permute-start | bytes 393224 | tf_op jit(solution)/shard_map/ppermute | solution.py:579
  332.1 18.8 %collective-permute-start.27 = (f32[2,128,128]{2,1,0:T(8,128)S(1)}, f32[2,128,128]{2,1,0:T(8,128)S(1)}, u32[]{:S(2)}, u32[]{:S(2)}) collective-permute-start(f32[2,128,128]{2,1,0:T(8,128)S(1)} %get-tuple-element.92), channel_id=1, source_target_pairs={{0,128},{16,144},{32,160},{48,176},{64,192},{80,208},{96,224},{112... | collective-permute-start | bytes 393224 | tf_op jit(solution)/shard_map/ppermute | solution.py:579
  335.1 17.8 %collective-permute-start.28 = (f32[2,128,128]{2,1,0:T(8,128)S(1)}, f32[2,128,128]{2,1,0:T(8,128)S(1)}, u32[]{:S(2)}, u32[]{:S(2)}) collective-permute-start(f32[2,128,128]{2,1,0:T(8,128)S(1)} %get-tuple-element.93), channel_id=1, source_target_pairs={{0,160},{16,176},{32,128},{48,144},{64,224},{80,240},{96,192},{112... | collective-permute-start | bytes 393224 | tf_op jit(solution)/shard_map/ppermute | solution.py:579
  341.5 15.1 %collective-permute-start.29 = (f32[2,128,128]{2,1,0:T(8,128)S(1)}, f32[2,128,128]{2,1,0:T(8,128)S(1)}, u32[]{:S(2)}, u32[]{:S(2)}) collective-permute-start(f32[2,128,128]{2,1,0:T(8,128)S(1)} %get-tuple-element.94), channel_id=1, source_target_pairs={{0,192},{16,208},{32,224},{48,240},{64,128},{80,144},{96,160},{112... | collective-permute-start | bytes 393224 | tf_op jit(solution)/shard_map/ppermute | solution.py:579
  (44 other events, 1524.1 us)
